TPU v7x, 32 devices: a whole 2x2x4 slice. The times are simulated.
32 devices in a mesh: grp: 4 (over x, core), wide: 8 (over z, y).
Axes of the slice: x: 2, y: 2, z: 4, core: 2. Of those that a mesh axis runs over, the one named last changes fastest.
Arguments:
- expression: float32 [1024, 4096], P(('grp', 'wide'))
- assignment: int32 [16], replicated, may hold values from 0 to 15, each once
- pairing: int32 [2, 16], replicated, may hold values from 0 to 15, as said below
Outputs:
- cross_scores: float32 [2, 16, 256, 256], P(None, 'wide', 'grp')
Inputs may be any that keep to these rules, and one draw needn't show every extreme that they name: Row r of pairing is round r of one round-robin plan over the 16 panels: every panel has a partner other than itself, and the partner's partner is the panel.
All inputs are finite; a program needn't handle non-finite values.
Results may differ from a plain program's by a relative error of at most 0.0043.
Values may be sent and summed in bfloat16 or wider, within the bound.
No kernel may reach another device: no remote copies, remote signals or barrier semaphores. Data moves between devices by JAX's collectives and lax.ppermute only.
A program may use at most 192 MiB of HBM per device.

v0:
```python
import functools

import jax
import jax.numpy as jnp
from jax import lax
from jax.experimental import pallas as pl
from jax.experimental.pallas import tpu as pltpu
from jax.sharding import Mesh
from jax.sharding import PartitionSpec as P


SLOTS = 2
ROUNDS = 2
EACH = 1 + ROUNDS
SIDE = 16
STATS = 8
F32 = jnp.float32
BF16 = jnp.bfloat16


def split_two(value):
    high = value.astype(BF16).astype(F32)
    return high, value - high


def prep_kernel(assignment, pairing, half, x_ref, out_ref, centred, high_rows, low_rows, side):
    cells, genes = x_ref.shape
    panels = assignment.shape[0]
    panel = genes // panels
    n_wide = out_ref.shape[0]

    def one_panel(p, carry):
        start = pl.multiple_of(p * panel, panel)
        block = x_ref[:, pl.ds(start, panel)]
        mean = jnp.sum(block, axis=0, keepdims=True) * (1.0 / cells)
        high, rest = split_two(mean)
        low = rest.astype(BF16).astype(F32)
        centred[p] = (block - (high + low)).astype(BF16)
        high_rows[pl.ds(p, 1), :] = high
        low_rows[pl.ds(p, 1), :] = low
        return carry

    lax.fori_loop(0, panels, one_panel, 0, unroll=panels <= 16)
    side[...] = jnp.zeros_like(side)

    def one_message(w, carry):
        nearer = (w // (n_wide // 2) + half[0]) % 2
        for place, s in ((0, 1 - nearer), (1, nearer)):
            owner = (w + s * (n_wide // 2)) % n_wide
            own = assignment[owner * SLOTS + s]
            for k in range(EACH):
                p = own if k == 0 else pairing[k - 1, own]
                out_ref[w, pl.ds((place * EACH + k) * cells, cells), :] = centred[p]
                side[pl.ds(place * 2 * EACH + k, 1), :] = high_rows[pl.ds(p, 1), :]
                side[pl.ds(place * 2 * EACH + EACH + k, 1), :] = low_rows[pl.ds(p, 1), :]
        out_ref[w, pl.ds(SLOTS * EACH * cells, SIDE), :] = side[...].astype(BF16)
        return carry

    lax.fori_loop(0, n_wide, one_message, 0, unroll=n_wide <= 8)


def gram_kernel(cells, which, place, here_ref, there_ref, same_ref, cross_ref, tile):
    n_wide, _, panel = here_ref.shape
    blocks = 2 * n_wide
    rows = blocks * cells
    quarter = panel // 4

    def part(start, size):
        halves = [r[:, pl.ds(start, size), :].reshape(n_wide * size, panel) for r in (here_ref, there_ref)]
        return jnp.concatenate(halves, axis=0)

    member = lax.broadcasted_iota(jnp.int32, (blocks, rows), 1) // cells
    member = (member == lax.broadcasted_iota(jnp.int32, (blocks, rows), 0)).astype(BF16)
    side = jnp.concatenate(
        [r[:, pl.ds(SLOTS * EACH * cells, SIDE), :].astype(F32) for r in (here_ref, there_ref)], axis=0
    )
    operands, means, squares = [], [], []
    for k in range(EACH):
        data = part((which * EACH + k) * cells, cells)
        sums = jnp.dot(member, data, preferred_element_type=F32)
        row = which * 2 * EACH + k
        block_mean = side[:, row, :] + side[:, row + EACH, :] + sums * (1.0 / cells)
        mean = jnp.sum(block_mean, axis=0, keepdims=True) * (1.0 / blocks)
        shift = block_mean - mean
        wide_data = data.astype(F32)
        square = jnp.sum(wide_data * wide_data, axis=0, keepdims=True) + jnp.sum(
            cells * (shift * shift) - sums * sums * (1.0 / cells), axis=0, keepdims=True
        )
        means.append(mean)
        squares.append(square)
        high, low = split_two(shift)
        scale = cells // 8
        if k == 0:
            extra = [8.0 * high, 8.0 * low, 8.0 * high, sums * 0.125]
        else:
            extra = [scale * high, scale * high, scale * low, sums * (-8.0 / cells)]
        operands.append(jnp.concatenate([data, jnp.concatenate(extra, axis=0).astype(BF16)], axis=0))
    stats = jnp.concatenate(means + squares + [jnp.zeros((STATS - 2 * EACH, panel), F32)], axis=0)
    high, rest = split_two(stats)
    middle, low = split_two(rest)
    packed = jnp.concatenate([high, middle, low, jnp.zeros_like(low)], axis=0).astype(BF16)
    for r in range(ROUNDS):
        tile[r] = lax.dot_general(
            operands[0], operands[1 + r], (((0,), (0,)), ((), ())), preferred_element_type=F32
        )
    mine = place[0]
    base = ROUNDS * quarter
    for ref, index in ((same_ref, mine), (cross_ref, (mine + 2) % 4)):
        start = pl.multiple_of(index * quarter, quarter)
        for r in range(ROUNDS):
            ref[pl.ds(r * quarter, quarter), :] = tile[r, pl.ds(start, quarter), :].astype(ref.dtype)
        if ref.dtype == F32:
            ref[pl.ds(base, STATS), :] = stats
        else:
            ref[pl.ds(base, 4 * STATS), :] = packed


def finish_kernel(total, place, nearer, keep_ref, x_ref, half_ref, both_ref, out_ref, columns):
    quarter, panel = out_ref.shape[2:]
    base = ROUNDS * quarter
    mine = pl.multiple_of(place[0] * quarter, quarter)
    near = nearer[0]
    sources = ((near, keep_ref, half_ref), (1 - near, x_ref, both_ref))
    for i, (slot, same_ref, other_ref) in enumerate(sources):
        same = same_ref[pl.ds(base, STATS), :]
        parts = other_ref[pl.ds(base, 4 * STATS), :].astype(F32)
        other = parts[2 * STATS : 3 * STATS] + parts[STATS : 2 * STATS] + parts[0:STATS]
        gap = (same - other)[0:EACH]
        square = (same + other)[EACH : 2 * EACH]
        var = square * (1.0 / total) + (gap * gap) * 0.25
        inv = lax.rsqrt(var + 1e-05)
        pair = jnp.concatenate([gap[0:1], inv[0:1], jnp.zeros((STATS - 2, panel), F32)], axis=0)
        columns[i] = pair.T
        side = columns[i, pl.ds(mine, quarter), :]
        gap_row = side[:, 0:1] * (total / 4)
        inv_row = side[:, 1:2] * total ** (-0.5)
        for r in range(ROUNDS):
            rows = pl.ds(r * quarter, quarter)
            tile = same_ref[rows, :] + other_ref[rows, :].astype(F32)
            tile = tile + gap_row * gap[1 + r : 2 + r]
            out_ref[r, slot] = tile * inv_row * inv[1 + r : 2 + r]


def on_chip(small):
    if not small:
        return jax.ShapeDtypeStruct, lambda value: value
    return pltpu.VMEM, lambda value: pltpu.with_memory_space_constraint(value, pltpu.VMEM)


def shards(expression, assignment, pairing):
    n_wide = lax.axis_size(("half", "rest"))
    n_grp = lax.axis_size(("x", "core"))
    cells, genes = expression.shape
    panels = assignment.shape[0]
    panel = genes // panels
    quarter = panel // n_grp
    total = cells * n_wide * n_grp
    x = lax.axis_index("x")
    place = (x * 2 + lax.axis_index("core")).reshape(1).astype(jnp.int32)
    nearer = (x ^ lax.axis_index("half")).reshape(1).astype(jnp.int32)
    smem = pl.BlockSpec(memory_space=pltpu.SMEM)
    vmem = pl.BlockSpec(memory_space=pltpu.VMEM)
    message = SLOTS * EACH * cells + SIDE
    received_bytes = 2 * n_wide * message * panel * 2
    array, in_vmem = on_chip(received_bytes <= 4 << 20)
    half = lax.axis_index("half")
    sent = pl.pallas_call(
        prep_kernel,
        out_shape=array((n_wide, message, panel), BF16),
        in_specs=[smem, smem, smem, vmem],
        out_specs=vmem,
        scratch_shapes=[
            pltpu.VMEM((panels, cells, panel), BF16),
            pltpu.VMEM((panels, panel), F32),
            pltpu.VMEM((panels, panel), F32),
            pltpu.VMEM((SIDE, panel), F32),
        ],
        name="prep",
    )(assignment, pairing, half.reshape(1).astype(jnp.int32), expression)
    here = lax.all_to_all(sent, ("x", "rest"), split_axis=0, concat_axis=0, tiled=True)
    there = lax.ppermute(here, "core", [(0, 1), (1, 0)])
    base = ROUNDS * quarter

    def gram(which, rows, dtype):
        return pl.pallas_call(
            functools.partial(gram_kernel, cells, which),
            out_shape=(array((rows, panel), dtype), array((rows, panel), dtype)),
            in_specs=[smem, vmem, vmem],
            out_specs=(vmem, vmem),
            scratch_shapes=[pltpu.VMEM((ROUNDS, panel, panel), F32)],
            compiler_params=pltpu.CompilerParams(
                vmem_limit_bytes=min(60 << 20, (8 << 20) + 6 * received_bytes)
            ),
            name="gram",
        )(place, in_vmem(here), in_vmem(there))

    to_half, to_both = gram(0, base + 4 * STATS, BF16)
    from_both = lax.ppermute(to_both, ("x", "half"), [(i, i ^ 3) for i in range(4)])
    from_half = lax.ppermute(to_half, "half", [(0, 1), (1, 0)])
    keep, to_x = gram(1, base + STATS, F32)
    from_x = lax.ppermute(to_x, "x", [(0, 1), (1, 0)])
    return pl.pallas_call(
        functools.partial(finish_kernel, total),
        out_shape=jax.ShapeDtypeStruct((ROUNDS, SLOTS, quarter, panel), F32),
        in_specs=[smem, smem, vmem, vmem, vmem, vmem],
        out_specs=vmem,
        scratch_shapes=[pltpu.VMEM((SLOTS, panel, STATS), F32)],
        name="finish",
    )(place, nearer, in_vmem(keep), in_vmem(from_x), in_vmem(from_half), in_vmem(from_both))


def solution(mesh):
    devices = mesh.devices
    n_wide = devices.shape[1]
    parted = Mesh(devices.reshape(2, 2, 2, n_wide // 2), ("x", "core", "half", "rest"))
    placed = (P(("x", "core", "half", "rest"), None), P(), P())
    return jax.shard_map(
        shards,
        mesh=parted,
        in_specs=placed,
        out_specs=P(None, ("half", "rest"), ("x", "core"), None),
        check_vma=False,
    )
```

profile of v0, /device:TPU:0, one launch (start us, length us, event | category | flops | bytes accessed | tf_op | source)
XLA Modules:
  0.0 37.0 jit_solution(2520655455486363220)
XLA Ops:
  0.0 1.4 %prep.1 = bf16[8,208,256]{2,1,0:T(8,128)(2,1)S(1)} custom-call(s32[16]{0:T(128)} %assignment.1, s32[2,16]{1,0:T(2,128)} %pairing.1, s32[1]{0:T(128)} %bitcast.2.half, f32[32,4096]{1,0:T(8,128)} %x_ref.1), custom_call_target="tpu_custom_call" | custom-call | tf_op jit(solution)/shard_map/prep/pallas_call | solution.py:167
  1.4 19.3 %all_to_all.5.here_ref = bf16[8,208,256]{2,1,0:T(8,128)(2,1)S(1)} all-to-all(bf16[8,208,256]{2,1,0:T(8,128)(2,1)S(1)} %prep.1), channel_id=1, replica_groups=mesh['x'=2,'core'=2,'half'=2,'rest'=4] {'x','rest'}, dimensions={0} | all-to-all | bytes 1703936 | tf_op jit(solution)/shard_map/all_to_all | solution.py:180
  20.6 0.0 collective-permute-start
  20.6 2.4 %collective-permute-done.there_ref = bf16[8,208,256]{2,1,0:T(8,128)(2,1)S(1)} collective-permute-done((bf16[8,208,256]{2,1,0:T(8,128)(2,1)S(1)}, bf16[8,208,256]{2,1,0:T(8,128)(2,1)S(1)}, u32[]{:S(2)}, u32[]{:S(2)}) %collective-permute-start) | collective-permute-done | bytes 852000 | tf_op jit(solution)/shard_map/ppermute | solution.py:181
  23.0 0.5 %gram.2 = (f32[136,256]{1,0:T(8,128)S(1)}, f32[136,256]{1,0:T(8,128)S(1)}) custom-call(s32[1]{0:T(128)} %bitcast.place, bf16[8,208,256]{2,1,0:T(8,128)(2,1)S(1)} %all_to_all.5.here_ref, bf16[8,208,256]{2,1,0:T(8,128)(2,1)S(1)} %collective-permute-done.there_ref), custom_call_target="tpu_custom_call" | custom-call | tf_op jit(solution)/shard_map/gram/pallas_call | solution.py:185
  23.5 0.6 %collective-permute-start.1 = (f32[136,256]{1,0:T(8,128)S(1)}, f32[136,256]{1,0:T(8,128)S(1)}, u32[]{:S(2)}, u32[]{:S(2)}) collective-permute-start(f32[136,256]{1,0:T(8,128)S(1)} %get-tuple-element.10), channel_id=1, source_target_pairs={{0,16},{16,0},{1,17},{17,1},{2,18},{18,2},{3,19},{19,3},{4,20},{20... | collective-permute-start | bytes 417800 | tf_op jit(solution)/shard_map/ppermute | solution.py:201
  24.2 0.5 %gram.3 = (bf16[160,256]{1,0:T(8,128)(2,1)S(1)}, bf16[160,256]{1,0:T(8,128)(2,1)S(1)}) custom-call(s32[1]{0:T(128)} %bitcast.place, bf16[8,208,256]{2,1,0:T(8,128)(2,1)S(1)} %all_to_all.5.here_ref, bf16[8,208,256]{2,1,0:T(8,128)(2,1)S(1)} %collective-permute-done.there_ref), custom_call_target="tpu_custom_call" | custom-call | tf_op jit(solution)/shard_map/gram/pallas_call | solution.py:185
  24.7 2.7 %collective-permute-start.2 = (bf16[160,256]{1,0:T(8,128)(2,1)S(1)}, bf16[160,256]{1,0:T(8,128)(2,1)S(1)}, u32[]{:S(2)}, u32[]{:S(2)}) collective-permute-start(bf16[160,256]{1,0:T(8,128)(2,1)S(1)} %get-tuple-element.11), channel_id=1, source_target_pairs={{0,4},{4,0},{1,5},{5,1},{2,6},{6,2},{3,7},{7,3},{8,12},{12,8},{9,1... | collective-permute-start | bytes 245768 | tf_op jit(solution)/shard_map/ppermute | solution.py:199
  27.3 1.2 %collective-permute-start.3 = (bf16[160,256]{1,0:T(8,128)(2,1)S(1)}, bf16[160,256]{1,0:T(8,128)(2,1)S(1)}, u32[]{:S(2)}, u32[]{:S(2)}) collective-permute-start(bf16[160,256]{1,0:T(8,128)(2,1)S(1)} %get-tuple-element.12), channel_id=1, source_target_pairs={{0,20},{4,16},{16,4},{20,0},{1,21},{5,17},{17,5},{21,1},{2,22},{6,... | collective-permute-start | bytes 245768 | tf_op jit(solution)/shard_map/ppermute | solution.py:198
  28.6 5.0 %collective-permute-done.2.half_ref = bf16[160,256]{1,0:T(8,128)(2,1)S(1)} collective-permute-done((bf16[160,256]{1,0:T(8,128)(2,1)S(1)}, bf16[160,256]{1,0:T(8,128)(2,1)S(1)}, u32[]{:S(2)}, u32[]{:S(2)}) %collective-permute-start.2) | collective-permute-done | bytes 81952 | tf_op jit(solution)/shard_map/ppermute | solution.py:199
  33.6 2.3 %collective-permute-done.3.both_ref = bf16[160,256]{1,0:T(8,128)(2,1)S(1)} collective-permute-done((bf16[160,256]{1,0:T(8,128)(2,1)S(1)}, bf16[160,256]{1,0:T(8,128)(2,1)S(1)}, u32[]{:S(2)}, u32[]{:S(2)}) %collective-permute-start.3) | collective-permute-done | bytes 81952 | tf_op jit(solution)/shard_map/ppermute | solution.py:198
  35.9 0.0 collective-permute-done.1.x_ref
  35.9 1.0 %finish.1 = f32[2,2,64,256]{3,2,1,0:T(8,128)} custom-call(s32[1]{0:T(128)} %bitcast.place, s32[1]{0:T(128)} %bitcast.1.nearer, f32[136,256]{1,0:T(8,128)S(1)} %get-tuple-element.9.keep_ref, f32[136,256]{1,0:T(8,128)S(1)} %collective-permute-done.1.x_ref, bf16[160,256]{1,0:T(8,128)(2,1)S(1)} %collective-permute-done.2.half_ref, ...), custom_call_target="tpu_custom_call" | custom-call | tf_op jit(solution)/shard_map/finish/pallas_call | solution.py:202
Async XLA Ops:
  20.6 2.4 %collective-permute-start = (bf16[8,208,256]{2,1,0:T(8,128)(2,1)S(1)}, bf16[8,208,256]{2,1,0:T(8,128)(2,1)S(1)}, u32[]{:S(2)}, u32[]{:S(2)}) collective-permute-start(bf16[8,208,256]{2,1,0:T(8,128)(2,1)S(1)} %all_to_all.5.here_ref), channel_id=1, source_target_pairs={{0,8},{8,0},{1,9},{9,1},{2,10},{10,2},{3,11},{11,3},{4,12},{12,4},... | collective-permute-start | bytes 2555912 | tf_op jit(solution)/shard_map/ppermute | solution.py:181
  23.5 12.4 %collective-permute-start.1 = (f32[136,256]{1,0:T(8,128)S(1)}, f32[136,256]{1,0:T(8,128)S(1)}, u32[]{:S(2)}, u32[]{:S(2)}) collective-permute-start(f32[136,256]{1,0:T(8,128)S(1)} %get-tuple-element.10), channel_id=1, source_target_pairs={{0,16},{16,0},{1,17},{17,1},{2,18},{18,2},{3,19},{19,3},{4,20},{20... | collective-permute-start | bytes 417800 | tf_op jit(solution)/shard_map/ppermute | solution.py:201
  24.7 8.9 %collective-permute-start.2 = (bf16[160,256]{1,0:T(8,128)(2,1)S(1)}, bf16[160,256]{1,0:T(8,128)(2,1)S(1)}, u32[]{:S(2)}, u32[]{:S(2)}) collective-permute-start(bf16[160,256]{1,0:T(8,128)(2,1)S(1)} %get-tuple-element.11), channel_id=1, source_target_pairs={{0,4},{4,0},{1,5},{5,1},{2,6},{6,2},{3,7},{7,3},{8,12},{12,8},{9,1... | collective-permute-start | bytes 245768 | tf_op jit(solution)/shard_map/ppermute | solution.py:199
  27.3 8.6 %collective-permute-start.3 = (bf16[160,256]{1,0:T(8,128)(2,1)S(1)}, bf16[160,256]{1,0:T(8,128)(2,1)S(1)}, u32[]{:S(2)}, u32[]{:S(2)}) collective-permute-start(bf16[160,256]{1,0:T(8,128)(2,1)S(1)} %get-tuple-element.12), channel_id=1, source_target_pairs={{0,20},{4,16},{16,4},{20,0},{1,21},{5,17},{17,5},{21,1},{2,22},{6,... | collective-permute-start | bytes 245768 | tf_op jit(solution)/shard_map/ppermute | solution.py:198
where the time goes:
time: 37.2 us; the launch traced here: 37 us
  blocking collectives  19.3 us (52%)
  waiting for transfers between devices  9.74 us (26%)
  starting transfers between devices  4.52 us (12%)
  Pallas kernels  3.41 us (9%)
    all_to_all x1, blocking collectives, shards(): lax.all_to_all(sent, ('x', 'rest'), split_axis=0, concat_axis=0, tiled=True)  19.3 us
    ppermute x1, waiting for transfers between devices, shards(): from_half = lax.ppermute(to_half, 'half', [(0, 1), (1, 0)])  5.02 us
    ppermute x1, starting transfers between devices, shards(): from_half = lax.ppermute(to_half, 'half', [(0, 1), (1, 0)])  2.65 us
    ppermute x1, waiting for transfers between devices, shards(): there = lax.ppermute(here, 'core', [(0, 1), (1, 0)])  2.38 us
    ppermute x1, waiting for transfers between devices, shards(): lax.ppermute(to_both, ('x', 'half'), [(i, i ^ 3) for i in range(4)])  2.34 us
    pallas_call x1, Pallas kernels, shards(): pl.pallas_call(prep_kernel, out_shape=array((n_wide, message, panel), BF1...  1.36 us
    ppermute x1, starting transfers between devices, shards(): lax.ppermute(to_both, ('x', 'half'), [(i, i ^ 3) for i in range(4)])  1.24 us
    pallas_call x1, Pallas kernels, shards(): pl.pallas_call(functools.partial(finish_kernel, total), out_shape=jax.Sha...  1.04 us
  transfers between devices with their start and end apart: 4, of which 3 were waited for; matrix products, arithmetic and copies ran while one was open for 0% of the time, Pallas kernels for 1%

commit v1 on v0

--- a/solution.py
+++ b/solution.py
@@ -13,6 +13,7 @@
 ROUNDS = 2
 EACH = 1 + ROUNDS
 SIDE = 16
+DIRECT = 8
 STATS = 8
 F32 = jnp.float32
 BF16 = jnp.bfloat16
@@ -23,11 +24,12 @@
     return high, value - high
 
 
-def prep_kernel(assignment, pairing, half, x_ref, out_ref, centred, high_rows, low_rows, side):
+def prep_kernel(apart, assignment, pairing, half, me, x_ref, *refs):
+    outs, (centred, high_rows, low_rows, side) = refs[:-4], refs[-4:]
     cells, genes = x_ref.shape
     panels = assignment.shape[0]
     panel = genes // panels
-    n_wide = out_ref.shape[0]
+    n_wide = len(outs) if apart else outs[0].shape[0]
 
     def one_panel(p, carry):
         start = pl.multiple_of(p * panel, panel)
@@ -43,36 +45,41 @@
     lax.fori_loop(0, panels, one_panel, 0, unroll=panels <= 16)
     side[...] = jnp.zeros_like(side)
 
-    def one_message(w, carry):
+    def one_message(w, out, at):
         nearer = (w // (n_wide // 2) + half[0]) % 2
         for place, s in ((0, 1 - nearer), (1, nearer)):
             owner = (w + s * (n_wide // 2)) % n_wide
             own = assignment[owner * SLOTS + s]
             for k in range(EACH):
                 p = own if k == 0 else pairing[k - 1, own]
-                out_ref[w, pl.ds((place * EACH + k) * cells, cells), :] = centred[p]
+                out[at, pl.ds((place * EACH + k) * cells, cells), :] = centred[p]
                 side[pl.ds(place * 2 * EACH + k, 1), :] = high_rows[pl.ds(p, 1), :]
                 side[pl.ds(place * 2 * EACH + EACH + k, 1), :] = low_rows[pl.ds(p, 1), :]
-        out_ref[w, pl.ds(SLOTS * EACH * cells, SIDE), :] = side[...].astype(BF16)
-        return carry
-
-    lax.fori_loop(0, n_wide, one_message, 0, unroll=n_wide <= 8)
-
-
-def gram_kernel(cells, which, place, here_ref, there_ref, same_ref, cross_ref, tile):
-    n_wide, _, panel = here_ref.shape
-    blocks = 2 * n_wide
+        out[at, pl.ds(SLOTS * EACH * cells, SIDE), :] = side[...].astype(BF16)
+
+    if apart:
+        for k, out in enumerate(outs):
+            one_message(me[0] ^ k, out, 0)
+    else:
+        lax.fori_loop(0, n_wide, lambda w, carry: one_message(w, outs[0], w) or carry, 0)
+
+
+def gram_kernel(cells, which, place, *refs):
+    received, (same_ref, cross_ref, tile) = refs[:-3], refs[-3:]
+    panel = same_ref.shape[1]
+    blocks = sum(r.shape[0] for r in received)
     rows = blocks * cells
     quarter = panel // 4
 
     def part(start, size):
-        halves = [r[:, pl.ds(start, size), :].reshape(n_wide * size, panel) for r in (here_ref, there_ref)]
-        return jnp.concatenate(halves, axis=0)
+        return jnp.concatenate(
+            [r[:, pl.ds(start, size), :].reshape(r.shape[0] * size, panel) for r in received], axis=0
+        )
 
     member = lax.broadcasted_iota(jnp.int32, (blocks, rows), 1) // cells
     member = (member == lax.broadcasted_iota(jnp.int32, (blocks, rows), 0)).astype(BF16)
     side = jnp.concatenate(
-        [r[:, pl.ds(SLOTS * EACH * cells, SIDE), :].astype(F32) for r in (here_ref, there_ref)], axis=0
+        [r[:, pl.ds(SLOTS * EACH * cells, SIDE), :].astype(F32) for r in received], axis=0
     )
     operands, means, squares = [], [], []
     for k in range(EACH):
@@ -98,7 +105,8 @@
     stats = jnp.concatenate(means + squares + [jnp.zeros((STATS - 2 * EACH, panel), F32)], axis=0)
     high, rest = split_two(stats)
     middle, low = split_two(rest)
-    packed = jnp.concatenate([high, middle, low, jnp.zeros_like(low)], axis=0).astype(BF16)
+    packed = [high[0 : 2 * EACH], middle[0 : 2 * EACH], low[0:EACH], jnp.zeros((SIDE - 5 * EACH, panel), F32)]
+    packed = jnp.concatenate(packed, axis=0).astype(BF16)
     for r in range(ROUNDS):
         tile[r] = lax.dot_general(
             operands[0], operands[1 + r], (((0,), (0,)), ((), ())), preferred_element_type=F32
@@ -112,7 +120,7 @@
         if ref.dtype == F32:
             ref[pl.ds(base, STATS), :] = stats
         else:
-            ref[pl.ds(base, 4 * STATS), :] = packed
+            ref[pl.ds(base, SIDE), :] = packed
 
 
 def finish_kernel(total, place, nearer, keep_ref, x_ref, half_ref, both_ref, out_ref, columns):
@@ -123,10 +131,10 @@
     sources = ((near, keep_ref, half_ref), (1 - near, x_ref, both_ref))
     for i, (slot, same_ref, other_ref) in enumerate(sources):
         same = same_ref[pl.ds(base, STATS), :]
-        parts = other_ref[pl.ds(base, 4 * STATS), :].astype(F32)
-        other = parts[2 * STATS : 3 * STATS] + parts[STATS : 2 * STATS] + parts[0:STATS]
-        gap = (same - other)[0:EACH]
-        square = (same + other)[EACH : 2 * EACH]
+        parts = other_ref[pl.ds(base, SIDE), :].astype(F32)
+        other = parts[4 * EACH : 5 * EACH] + parts[2 * EACH : 3 * EACH] + parts[0:EACH]
+        gap = same[0:EACH] - other
+        square = same[EACH : 2 * EACH] + (parts[3 * EACH : 4 * EACH] + parts[EACH : 2 * EACH])
         var = square * (1.0 / total) + (gap * gap) * 0.25
         inv = lax.rsqrt(var + 1e-05)
         pair = jnp.concatenate([gap[0:1], inv[0:1], jnp.zeros((STATS - 2, panel), F32)], axis=0)
@@ -145,6 +153,19 @@
     if not small:
         return jax.ShapeDtypeStruct, lambda value: value
     return pltpu.VMEM, lambda value: pltpu.with_memory_space_constraint(value, pltpu.VMEM)
+
+
+def gather(sent, n_wide):
+    if len(sent) == 1:
+        here = [lax.all_to_all(sent[0], ("x", "rest"), split_axis=0, concat_axis=0, tiled=True)]
+    else:
+        here = [sent[0]]
+        for k in range(1, n_wide):
+            here.append(lax.ppermute(sent[k], ("x", "rest"), [(i, i ^ k) for i in range(n_wide)]))
+    there = []
+    for value in here:
+        there.append(lax.ppermute(value, "core", [(0, 1), (1, 0)]))
+    return here + there
 
 
 def shards(expression, assignment, pairing):
@@ -163,12 +184,15 @@
     message = SLOTS * EACH * cells + SIDE
     received_bytes = 2 * n_wide * message * panel * 2
     array, in_vmem = on_chip(received_bytes <= 4 << 20)
-    half = lax.axis_index("half")
+    half = lax.axis_index("half").reshape(1).astype(jnp.int32)
+    me = lax.axis_index(("x", "rest")).reshape(1).astype(jnp.int32)
+    apart = n_wide <= DIRECT
+    shape = (1 if apart else n_wide, message, panel)
     sent = pl.pallas_call(
-        prep_kernel,
-        out_shape=array((n_wide, message, panel), BF16),
-        in_specs=[smem, smem, smem, vmem],
-        out_specs=vmem,
+        functools.partial(prep_kernel, apart),
+        out_shape=(array(shape, BF16),) * (n_wide if apart else 1),
+        in_specs=[smem, smem, smem, smem, vmem],
+        out_specs=(vmem,) * (n_wide if apart else 1),
         scratch_shapes=[
             pltpu.VMEM((panels, cells, panel), BF16),
             pltpu.VMEM((panels, panel), F32),
@@ -176,25 +200,24 @@
             pltpu.VMEM((SIDE, panel), F32),
         ],
         name="prep",
-    )(assignment, pairing, half.reshape(1).astype(jnp.int32), expression)
-    here = lax.all_to_all(sent, ("x", "rest"), split_axis=0, concat_axis=0, tiled=True)
-    there = lax.ppermute(here, "core", [(0, 1), (1, 0)])
+    )(assignment, pairing, half, me, expression)
+    received = gather(sent, n_wide)
     base = ROUNDS * quarter
 
     def gram(which, rows, dtype):
         return pl.pallas_call(
             functools.partial(gram_kernel, cells, which),
             out_shape=(array((rows, panel), dtype), array((rows, panel), dtype)),
-            in_specs=[smem, vmem, vmem],
+            in_specs=[smem] + [vmem] * len(received),
             out_specs=(vmem, vmem),
             scratch_shapes=[pltpu.VMEM((ROUNDS, panel, panel), F32)],
             compiler_params=pltpu.CompilerParams(
                 vmem_limit_bytes=min(60 << 20, (8 << 20) + 6 * received_bytes)
             ),
             name="gram",
-        )(place, in_vmem(here), in_vmem(there))
-
-    to_half, to_both = gram(0, base + 4 * STATS, BF16)
+        )(place, *map(in_vmem, received))
+
+    to_half, to_both = gram(0, base + SIDE, BF16)
     from_both = lax.ppermute(to_both, ("x", "half"), [(i, i ^ 3) for i in range(4)])
     from_half = lax.ppermute(to_half, "half", [(0, 1), (1, 0)])
     keep, to_x = gram(1, base + STATS, F32)

time: 37.2 us -> 34.7 us (0.933)
  blocking collectives: 19.3 us -> 0 us
  starting transfers between devices: 4.52 us -> 17.6 us
  waiting for transfers between devices: 9.74 us -> 13.4 us
    all_to_all x1 -> x0, blocking collectives: 19.3 us -> none  [shards(): lax.all_to_all(sent, ('x', 'rest'), split_axis=0, concat_axis=0, tiled=True)]
    ppermute x1 -> x15, starting transfers between devices: 0.01 us -> 13.1 us  [the longest x7 11.1 us: gather(): lax.ppermute(sent[k], ('x', 'rest'), [(i, i ^ k) for i in range(n_wide)])]
    ppermute x1 -> x15, waiting for transfers between devices: 2.38 us -> 5.89 us  [the longest x7 4.92 us: gather(): lax.ppermute(sent[k], ('x', 'rest'), [(i, i ^ k) for i in range(n_wide)])]
    ppermute x1, waiting for transfers between devices: 5.02 us -> 6.41 us  [shards(): from_half = lax.ppermute(to_half, 'half', [(0, 1), (1, 0)])]
    ppermute x1, waiting for transfers between devices: 2.34 us -> 1.06 us  [shards(): lax.ppermute(to_both, ('x', 'half'), [(i, i ^ 3) for i in range(4)])]
    ppermute x1, starting transfers between devices: 0.63 us -> 1.87 us  [shards(): from_x = lax.ppermute(to_x, 'x', [(0, 1), (1, 0)])]
    ppermute x1, starting transfers between devices: 1.24 us -> 0.01 us  [shards(): lax.ppermute(to_both, ('x', 'half'), [(i, i ^ 3) for i in range(4)])]
  transfers between devices with their start and end apart: 4 -> 18, of which waited for: 3 -> 8; matrix products, arithmetic and copies ran while one was open for 0% -> 0% of each run, Pallas kernels for 1% -> 2%
where the time goes in v1:
time: 34.7 us; the launch traced here: 34.5 us
  starting transfers between devices  17.6 us (51%)
  waiting for transfers between devices  13.4 us (39%)
  Pallas kernels  3.48 us (10%)
    ppermute x7, starting transfers between devices, gather(): lax.ppermute(sent[k], ('x', 'rest'), [(i, i ^ k) for i in range(n_wide)])  11.1 us
    ppermute x1, waiting for transfers between devices, shards(): from_half = lax.ppermute(to_half, 'half', [(0, 1), (1, 0)])  6.41 us
    ppermute x7, waiting for transfers between devices, gather(): lax.ppermute(sent[k], ('x', 'rest'), [(i, i ^ k) for i in range(n_wide)])  4.92 us
    ppermute x1, starting transfers between devices, shards(): from_half = lax.ppermute(to_half, 'half', [(0, 1), (1, 0)])  2.63 us
    ppermute x8, starting transfers between devices, gather(): there.append(lax.ppermute(value, 'core', [(0, 1), (1, 0)]))  2.04 us
    ppermute x1, starting transfers between devices, shards(): from_x = lax.ppermute(to_x, 'x', [(0, 1), (1, 0)])  1.87 us
    pallas_call x1, Pallas kernels, shards(): pl.pallas_call(functools.partial(prep_kernel, apart), out_shape=(array(sh...  1.4 us
    ppermute x1, waiting for transfers between devices, shards(): lax.ppermute(to_both, ('x', 'half'), [(i, i ^ 3) for i in range(4)])  1.06 us
  transfers between devices with their start and end apart: 18, of which 8 were waited for; matrix products, arithmetic and copies ran while one was open for 0% of the time, Pallas kernels for 2%

profile of v1, /device:TPU:0, one launch (start us, length us, event | category | flops | bytes accessed | tf_op | source)
XLA Modules:
  0.0 34.5 jit_solution(3547149888079795268)
XLA Ops:
  0.0 1.4 %prep.1 = (bf16[1,208,256]{2,1,0:T(8,128)(2,1)S(1)}, bf16[1,208,256]{2,1,0:T(8,128)(2,1)S(1)}, bf16[1,208,256]{2,1,0:T(8,128)(2,1)S(1)}, bf16[1,208,256]{2,1,0:T...) custom-call(s32[16]{0:T(128)} %assignment.1, ...), custom_call_target="tpu_custom_call" | custom-call | tf_op jit(solution)/shard_map/prep/pallas_call | solution.py:191
  1.4 3.1 %collective-permute-start = (bf16[1,208,256]{2,1,0:T(8,128)(2,1)S(1)}, bf16[1,208,256]{2,1,0:T(8,128)(2,1)S(1)}, u32[]{:S(2)}, u32[]{:S(2)}) collective-permute-start(bf16[1,208,256]{2,1,0:T(8,128)(2,1)S(1)} %get-tuple-element.18), channel_id=1, source_target_pairs={{0,1},{1,0},{2,3},{3,2},{16,17},{17,16},{18,19},{19,18},{4,5},{5,4... | collective-permute-start | bytes 319496 | tf_op jit(solution)/shard_map/ppermute | solution.py:164
  4.5 1.6 %collective-permute-start.1 = (bf16[1,208,256]{2,1,0:T(8,128)(2,1)S(1)}, bf16[1,208,256]{2,1,0:T(8,128)(2,1)S(1)}, u32[]{:S(2)}, u32[]{:S(2)}) collective-permute-start(bf16[1,208,256]{2,1,0:T(8,128)(2,1)S(1)} %get-tuple-element.19), channel_id=1, source_target_pairs={{0,2},{1,3},{2,0},{3,1},{16,18},{17,19},{18,16},{19,17},{4,6},{5,7... | collective-permute-start | bytes 319496 | tf_op jit(solution)/shard_map/ppermute | solution.py:164
  6.0 0.0 collective-permute-start.2
  6.0 1.9 %collective-permute-start.3 = (bf16[1,208,256]{2,1,0:T(8,128)(2,1)S(1)}, bf16[1,208,256]{2,1,0:T(8,128)(2,1)S(1)}, u32[]{:S(2)}, u32[]{:S(2)}) collective-permute-start(bf16[1,208,256]{2,1,0:T(8,128)(2,1)S(1)} %get-tuple-element.21), channel_id=1, source_target_pairs={{0,16},{1,17},{2,18},{3,19},{16,0},{17,1},{18,2},{19,3},{4,20},{5,... | collective-permute-start | bytes 319496 | tf_op jit(solution)/shard_map/ppermute | solution.py:164
  7.9 1.5 %collective-permute-start.4 = (bf16[1,208,256]{2,1,0:T(8,128)(2,1)S(1)}, bf16[1,208,256]{2,1,0:T(8,128)(2,1)S(1)}, u32[]{:S(2)}, u32[]{:S(2)}) collective-permute-start(bf16[1,208,256]{2,1,0:T(8,128)(2,1)S(1)} %get-tuple-element.22), channel_id=1, source_target_pairs={{0,17},{1,16},{2,19},{3,18},{16,1},{17,0},{18,3},{19,2},{4,21},{5,... | collective-permute-start | bytes 319496 | tf_op jit(solution)/shard_map/ppermute | solution.py:164
  9.4 0.0 collective-permute-done.refs_1_
  9.4 2.5 %collective-permute-start.5 = (bf16[1,208,256]{2,1,0:T(8,128)(2,1)S(1)}, bf16[1,208,256]{2,1,0:T(8,128)(2,1)S(1)}, u32[]{:S(2)}, u32[]{:S(2)}) collective-permute-start(bf16[1,208,256]{2,1,0:T(8,128)(2,1)S(1)} %get-tuple-element.23), channel_id=1, source_target_pairs={{0,18},{1,19},{2,16},{3,17},{16,2},{17,3},{18,0},{19,1},{4,22},{5,... | collective-permute-start | bytes 319496 | tf_op jit(solution)/shard_map/ppermute | solution.py:164
  11.9 0.0 collective-permute-done.1.refs_2_
  11.9 0.6 %collective-permute-start.6 = (bf16[1,208,256]{2,1,0:T(8,128)(2,1)S(1)}, bf16[1,208,256]{2,1,0:T(8,128)(2,1)S(1)}, u32[]{:S(2)}, u32[]{:S(2)}) collective-permute-start(bf16[1,208,256]{2,1,0:T(8,128)(2,1)S(1)} %get-tuple-element.24), channel_id=1, source_target_pairs={{0,19},{1,18},{2,17},{3,16},{16,3},{17,2},{18,1},{19,0},{4,23},{5,... | collective-permute-start | bytes 319496 | tf_op jit(solution)/shard_map/ppermute | solution.py:164
  12.5 0.0 collective-permute-done.2.refs_3_
  12.5 0.0 collective-permute-start.7
  12.5 0.0 collective-permute-done.3.refs_4_
  12.5 0.5 %collective-permute-start.8 = (bf16[1,208,256]{2,1,0:T(8,128)(2,1)S(1)}, bf16[1,208,256]{2,1,0:T(8,128)(2,1)S(1)}, u32[]{:S(2)}, u32[]{:S(2)}) collective-permute-start(bf16[1,208,256]{2,1,0:T(8,128)(2,1)S(1)} %collective-permute-done.refs_1_), channel_id=1, source_target_pairs={{0,8},{8,0},{1,9},{9,1},{2,10},{10,2},{3,11},{11,3},{4,12},{12,4},... | collective-permute-start | bytes 319496 | tf_op jit(solution)/shard_map/ppermute | solution.py:167
  13.0 4.0 %collective-permute-done.4.refs_5_ = bf16[1,208,256]{2,1,0:T(8,128)(2,1)S(1)} collective-permute-done((bf16[1,208,256]{2,1,0:T(8,128)(2,1)S(1)}, bf16[1,208,256]{2,1,0:T(8,128)(2,1)S(1)}, u32[]{:S(2)}, u32[]{:S(2)}) %collective-permute-start.4) | collective-permute-done | bytes 106528 | tf_op jit(solution)/shard_map/ppermute | solution.py:164
  17.0 0.5 %collective-permute-start.10 = (bf16[1,208,256]{2,1,0:T(8,128)(2,1)S(1)}, bf16[1,208,256]{2,1,0:T(8,128)(2,1)S(1)}, u32[]{:S(2)}, u32[]{:S(2)}) collective-permute-start(bf16[1,208,256]{2,1,0:T(8,128)(2,1)S(1)} %collective-permute-done.2.refs_3_), channel_id=1, source_target_pairs={{0,8},{8,0},{1,9},{9,1},{2,10},{10,2},{3,11},{11,3},{4,12},{12,4},... | collective-permute-start | bytes 319496 | tf_op jit(solution)/shard_map/ppermute | solution.py:167
  17.5 0.9 %collective-permute-done.6.refs_7_ = bf16[1,208,256]{2,1,0:T(8,128)(2,1)S(1)} collective-permute-done((bf16[1,208,256]{2,1,0:T(8,128)(2,1)S(1)}, bf16[1,208,256]{2,1,0:T(8,128)(2,1)S(1)}, u32[]{:S(2)}, u32[]{:S(2)}) %collective-permute-start.6) | collective-permute-done | bytes 106528 | tf_op jit(solution)/shard_map/ppermute | solution.py:164
  18.4 0.5 %collective-permute-start.12 = (bf16[1,208,256]{2,1,0:T(8,128)(2,1)S(1)}, bf16[1,208,256]{2,1,0:T(8,128)(2,1)S(1)}, u32[]{:S(2)}, u32[]{:S(2)}) collective-permute-start(bf16[1,208,256]{2,1,0:T(8,128)(2,1)S(1)} %collective-permute-done.4.refs_5_), channel_id=1, source_target_pairs={{0,8},{8,0},{1,9},{9,1},{2,10},{10,2},{3,11},{11,3},{4,12},{12,4},... | collective-permute-start | bytes 319496 | tf_op jit(solution)/shard_map/ppermute | solution.py:167
  18.9 0.1 collective-permute-start.13
  19.0 0.4 %collective-permute-start.14 = (bf16[1,208,256]{2,1,0:T(8,128)(2,1)S(1)}, bf16[1,208,256]{2,1,0:T(8,128)(2,1)S(1)}, u32[]{:S(2)}, u32[]{:S(2)}) collective-permute-start(bf16[1,208,256]{2,1,0:T(8,128)(2,1)S(1)} %collective-permute-done.6.refs_7_), channel_id=1, source_target_pairs={{0,8},{8,0},{1,9},{9,1},{2,10},{10,2},{3,11},{11,3},{4,12},{12,4},... | collective-permute-start | bytes 319496 | tf_op jit(solution)/shard_map/ppermute | solution.py:167
  19.5 0.3 collective-permute-done.11.refs_12_
  19.7 0.2 collective-permute-done.12.refs_13_
  19.9 0.4 %collective-permute-done.13.refs_14_ = bf16[1,208,256]{2,1,0:T(8,128)(2,1)S(1)} collective-permute-done((bf16[1,208,256]{2,1,0:T(8,128)(2,1)S(1)}, bf16[1,208,256]{2,1,0:T(8,128)(2,1)S(1)}, u32[]{:S(2)}, u32[]{:S(2)}) %collective-permute-start.13) | collective-permute-done | bytes 106528 | tf_op jit(solution)/shard_map/ppermute | solution.py:167
  20.3 0.2 collective-permute-done.14.refs_15_
  20.4 0.5 %gram.2 = (f32[136,256]{1,0:T(8,128)S(1)}, f32[136,256]{1,0:T(8,128)S(1)}) custom-call(s32[1]{0:T(128)} %bitcast.place, bf16[1,208,256]{2,1,0:T(8,128)(2,1)S(1)} %get-tuple-element.17.refs_0_, bf16[1,208,256]{2,1,0:T(8,128)(2,1)S(1)} %collective-permute-done.refs_1_, bf16[1,208,256]{2,1,0:T(8,128)(2,1)S(1)} %collective-permute-done.1.refs_2_, ...), custom_call_target="tpu_custom_call" | custom-call | tf_op jit(solution)/shard_map/gram/pallas_call | solution.py:208
  20.9 1.9 %collective-permute-start.15 = (f32[136,256]{1,0:T(8,128)S(1)}, f32[136,256]{1,0:T(8,128)S(1)}, u32[]{:S(2)}, u32[]{:S(2)}) collective-permute-start(f32[136,256]{1,0:T(8,128)S(1)} %get-tuple-element.26), channel_id=1, source_target_pairs={{0,16},{16,0},{1,17},{17,1},{2,18},{18,2},{3,19},{19,3},{4,20},{20... | collective-permute-start | bytes 417800 | tf_op jit(solution)/shard_map/ppermute | solution.py:224
  22.8 0.5 %gram.3 = (bf16[144,256]{1,0:T(8,128)(2,1)S(1)}, bf16[144,256]{1,0:T(8,128)(2,1)S(1)}) custom-call(s32[1]{0:T(128)} %bitcast.place, bf16[1,208,256]{2,1,0:T(8,128)(2,1)S(1)} %get-tuple-element.17.refs_0_, bf16[1,208,256]{2,1,0:T(8,128)(2,1)S(1)} %collective-permute-done.refs_1_, bf16[1,208,256]{2,1,0:T(8,128)(2,1)S(1)} %collective-permute-done.1.refs_2_, ...), custom_call_target="tpu_custom_call" | custom-call | tf_op jit(solution)/shard_map/gram/pallas_call | solution.py:208
  23.4 2.6 %collective-permute-start.16 = (bf16[144,256]{1,0:T(8,128)(2,1)S(1)}, bf16[144,256]{1,0:T(8,128)(2,1)S(1)}, u32[]{:S(2)}, u32[]{:S(2)}) collective-permute-start(bf16[144,256]{1,0:T(8,128)(2,1)S(1)} %get-tuple-element.27), channel_id=1, source_target_pairs={{0,4},{4,0},{1,5},{5,1},{2,6},{6,2},{3,7},{7,3},{8,12},{12,8},{9,1... | collective-permute-start | bytes 221192 | tf_op jit(solution)/shard_map/ppermute | solution.py:222
  26.0 0.0 collective-permute-start.17
  26.0 6.4 %collective-permute-done.16.half_ref = bf16[144,256]{1,0:T(8,128)(2,1)S(1)} collective-permute-done((bf16[144,256]{1,0:T(8,128)(2,1)S(1)}, bf16[144,256]{1,0:T(8,128)(2,1)S(1)}, u32[]{:S(2)}, u32[]{:S(2)}) %collective-permute-start.16) | collective-permute-done | bytes 73760 | tf_op jit(solution)/shard_map/ppermute | solution.py:222
  32.4 1.1 %collective-permute-done.17.both_ref = bf16[144,256]{1,0:T(8,128)(2,1)S(1)} collective-permute-done((bf16[144,256]{1,0:T(8,128)(2,1)S(1)}, bf16[144,256]{1,0:T(8,128)(2,1)S(1)}, u32[]{:S(2)}, u32[]{:S(2)}) %collective-permute-start.17) | collective-permute-done | bytes 73760 | tf_op jit(solution)/shard_map/ppermute | solution.py:221
  33.5 1.0 %finish.1 = f32[2,2,64,256]{3,2,1,0:T(8,128)} custom-call(s32[1]{0:T(128)} %bitcast.place, s32[1]{0:T(128)} %bitcast.1.nearer, f32[136,256]{1,0:T(8,128)S(1)} %get-tuple-element.25.keep_ref, f32[136,256]{1,0:T(8,128)S(1)} %collective-permute-done.15.x_ref, bf16[144,256]{1,0:T(8,128)(2,1)S(1)} %collective-permute-done.16.half_ref, ...), custom_call_target="tpu_custom_call" | custom-call | tf_op jit(solution)/shard_map/finish/pallas_call | solution.py:225
  (8 shorter events, 0.0 us)
Async XLA Ops:
  1.4 8.0 %collective-permute-start = (bf16[1,208,256]{2,1,0:T(8,128)(2,1)S(1)}, bf16[1,208,256]{2,1,0:T(8,128)(2,1)S(1)}, u32[]{:S(2)}, u32[]{:S(2)}) collective-permute-start(bf16[1,208,256]{2,1,0:T(8,128)(2,1)S(1)} %get-tuple-element.18), channel_id=1, source_target_pairs={{0,1},{1,0},{2,3},{3,2},{16,17},{17,16},{18,19},{19,18},{4,5},{5,4... | collective-permute-start | bytes 319496 | tf_op jit(solution)/shard_map/ppermute | solution.py:164
  4.5 7.5 %collective-permute-start.1 = (bf16[1,208,256]{2,1,0:T(8,128)(2,1)S(1)}, bf16[1,208,256]{2,1,0:T(8,128)(2,1)S(1)}, u32[]{:S(2)}, u32[]{:S(2)}) collective-permute-start(bf16[1,208,256]{2,1,0:T(8,128)(2,1)S(1)} %get-tuple-element.19), channel_id=1, source_target_pairs={{0,2},{1,3},{2,0},{3,1},{16,18},{17,19},{18,16},{19,17},{4,6},{5,7... | collective-permute-start | bytes 319496 | tf_op jit(solution)/shard_map/ppermute | solution.py:164
  6.0 6.4 %collective-permute-start.2 = (bf16[1,208,256]{2,1,0:T(8,128)(2,1)S(1)}, bf16[1,208,256]{2,1,0:T(8,128)(2,1)S(1)}, u32[]{:S(2)}, u32[]{:S(2)}) collective-permute-start(bf16[1,208,256]{2,1,0:T(8,128)(2,1)S(1)} %get-tuple-element.20), channel_id=1, source_target_pairs={{0,3},{1,2},{2,1},{3,0},{16,19},{17,18},{18,17},{19,16},{4,7},{5,6... | collective-permute-start | bytes 319496 | tf_op jit(solution)/shard_map/ppermute | solution.py:164
  6.0 6.5 %collective-permute-start.3 = (bf16[1,208,256]{2,1,0:T(8,128)(2,1)S(1)}, bf16[1,208,256]{2,1,0:T(8,128)(2,1)S(1)}, u32[]{:S(2)}, u32[]{:S(2)}) collective-permute-start(bf16[1,208,256]{2,1,0:T(8,128)(2,1)S(1)} %get-tuple-element.21), channel_id=1, source_target_pairs={{0,16},{1,17},{2,18},{3,19},{16,0},{17,1},{18,2},{19,3},{4,20},{5,... | collective-permute-start | bytes 319496 | tf_op jit(solution)/shard_map/ppermute | solution.py:164
  7.9 9.1 %collective-permute-start.4 = (bf16[1,208,256]{2,1,0:T(8,128)(2,1)S(1)}, bf16[1,208,256]{2,1,0:T(8,128)(2,1)S(1)}, u32[]{:S(2)}, u32[]{:S(2)}) collective-permute-start(bf16[1,208,256]{2,1,0:T(8,128)(2,1)S(1)} %get-tuple-element.22), channel_id=1, source_target_pairs={{0,17},{1,16},{2,19},{3,18},{16,1},{17,0},{18,3},{19,2},{4,21},{5,... | collective-permute-start | bytes 319496 | tf_op jit(solution)/shard_map/ppermute | solution.py:164
  9.4 7.6 %collective-permute-start.5 = (bf16[1,208,256]{2,1,0:T(8,128)(2,1)S(1)}, bf16[1,208,256]{2,1,0:T(8,128)(2,1)S(1)}, u32[]{:S(2)}, u32[]{:S(2)}) collective-permute-start(bf16[1,208,256]{2,1,0:T(8,128)(2,1)S(1)} %get-tuple-element.23), channel_id=1, source_target_pairs={{0,18},{1,19},{2,16},{3,17},{16,2},{17,3},{18,0},{19,1},{4,22},{5,... | collective-permute-start | bytes 319496 | tf_op jit(solution)/shard_map/ppermute | solution.py:164
  11.9 6.5 %collective-permute-start.6 = (bf16[1,208,256]{2,1,0:T(8,128)(2,1)S(1)}, bf16[1,208,256]{2,1,0:T(8,128)(2,1)S(1)}, u32[]{:S(2)}, u32[]{:S(2)}) collective-permute-start(bf16[1,208,256]{2,1,0:T(8,128)(2,1)S(1)} %get-tuple-element.24), channel_id=1, source_target_pairs={{0,19},{1,18},{2,17},{3,16},{16,3},{17,2},{18,1},{19,0},{4,23},{5,... | collective-permute-start | bytes 319496 | tf_op jit(solution)/shard_map/ppermute | solution.py:164
  12.5 5.9 %collective-permute-start.7 = (bf16[1,208,256]{2,1,0:T(8,128)(2,1)S(1)}, bf16[1,208,256]{2,1,0:T(8,128)(2,1)S(1)}, u32[]{:S(2)}, u32[]{:S(2)}) collective-permute-start(bf16[1,208,256]{2,1,0:T(8,128)(2,1)S(1)} %get-tuple-element.17.refs_0_), channel_id=1, source_target_pairs={{0,8},{8,0},{1,9},{9,1},{2,10},{10,2},{3,11},{11,3},{4,12},{12,4},... | collective-permute-start | bytes 319496 | tf_op jit(solution)/shard_map/ppermute | solution.py:167
  12.5 6.5 %collective-permute-start.8 = (bf16[1,208,256]{2,1,0:T(8,128)(2,1)S(1)}, bf16[1,208,256]{2,1,0:T(8,128)(2,1)S(1)}, u32[]{:S(2)}, u32[]{:S(2)}) collective-permute-start(bf16[1,208,256]{2,1,0:T(8,128)(2,1)S(1)} %collective-permute-done.refs_1_), channel_id=1, source_target_pairs={{0,8},{8,0},{1,9},{9,1},{2,10},{10,2},{3,11},{11,3},{4,12},{12,4},... | collective-permute-start | bytes 319496 | tf_op jit(solution)/shard_map/ppermute | solution.py:167
  17.0 2.0 %collective-permute-start.9 = (bf16[1,208,256]{2,1,0:T(8,128)(2,1)S(1)}, bf16[1,208,256]{2,1,0:T(8,128)(2,1)S(1)}, u32[]{:S(2)}, u32[]{:S(2)}) collective-permute-start(bf16[1,208,256]{2,1,0:T(8,128)(2,1)S(1)} %collective-permute-done.1.refs_2_), channel_id=1, source_target_pairs={{0,8},{8,0},{1,9},{9,1},{2,10},{10,2},{3,11},{11,3},{4,12},{12,4},... | collective-permute-start | bytes 319496 | tf_op jit(solution)/shard_map/ppermute | solution.py:167
  17.0 2.5 %collective-permute-start.10 = (bf16[1,208,256]{2,1,0:T(8,128)(2,1)S(1)}, bf16[1,208,256]{2,1,0:T(8,128)(2,1)S(1)}, u32[]{:S(2)}, u32[]{:S(2)}) collective-permute-start(bf16[1,208,256]{2,1,0:T(8,128)(2,1)S(1)} %collective-permute-done.2.refs_3_), channel_id=1, source_target_pairs={{0,8},{8,0},{1,9},{9,1},{2,10},{10,2},{3,11},{11,3},{4,12},{12,4},... | collective-permute-start | bytes 319496 | tf_op jit(solution)/shard_map/ppermute | solution.py:167
  18.4 1.3 %collective-permute-start.11 = (bf16[1,208,256]{2,1,0:T(8,128)(2,1)S(1)}, bf16[1,208,256]{2,1,0:T(8,128)(2,1)S(1)}, u32[]{:S(2)}, u32[]{:S(2)}) collective-permute-start(bf16[1,208,256]{2,1,0:T(8,128)(2,1)S(1)} %collective-permute-done.3.refs_4_), channel_id=1, source_target_pairs={{0,8},{8,0},{1,9},{9,1},{2,10},{10,2},{3,11},{11,3},{4,12},{12,4},... | collective-permute-start | bytes 319496 | tf_op jit(solution)/shard_map/ppermute | solution.py:167
  18.4 1.5 %collective-permute-start.12 = (bf16[1,208,256]{2,1,0:T(8,128)(2,1)S(1)}, bf16[1,208,256]{2,1,0:T(8,128)(2,1)S(1)}, u32[]{:S(2)}, u32[]{:S(2)}) collective-permute-start(bf16[1,208,256]{2,1,0:T(8,128)(2,1)S(1)} %collective-permute-done.4.refs_5_), channel_id=1, source_target_pairs={{0,8},{8,0},{1,9},{9,1},{2,10},{10,2},{3,11},{11,3},{4,12},{12,4},... | collective-permute-start | bytes 319496 | tf_op jit(solution)/shard_map/ppermute | solution.py:167
  18.9 1.3 %collective-permute-start.13 = (bf16[1,208,256]{2,1,0:T(8,128)(2,1)S(1)}, bf16[1,208,256]{2,1,0:T(8,128)(2,1)S(1)}, u32[]{:S(2)}, u32[]{:S(2)}) collective-permute-start(bf16[1,208,256]{2,1,0:T(8,128)(2,1)S(1)} %collective-permute-done.5.refs_6_), channel_id=1, source_target_pairs={{0,8},{8,0},{1,9},{9,1},{2,10},{10,2},{3,11},{11,3},{4,12},{12,4},... | collective-permute-start | bytes 319496 | tf_op jit(solution)/shard_map/ppermute | solution.py:167
  19.0 1.4 %collective-permute-start.14 = (bf16[1,208,256]{2,1,0:T(8,128)(2,1)S(1)}, bf16[1,208,256]{2,1,0:T(8,128)(2,1)S(1)}, u32[]{:S(2)}, u32[]{:S(2)}) collective-permute-start(bf16[1,208,256]{2,1,0:T(8,128)(2,1)S(1)} %collective-permute-done.6.refs_7_), channel_id=1, source_target_pairs={{0,8},{8,0},{1,9},{9,1},{2,10},{10,2},{3,11},{11,3},{4,12},{12,4},... | collective-permute-start | bytes 319496 | tf_op jit(solution)/shard_map/ppermute | solution.py:167
  20.9 12.5 %collective-permute-start.15 = (f32[136,256]{1,0:T(8,128)S(1)}, f32[136,256]{1,0:T(8,128)S(1)}, u32[]{:S(2)}, u32[]{:S(2)}) collective-permute-start(f32[136,256]{1,0:T(8,128)S(1)} %get-tuple-element.26), channel_id=1, source_target_pairs={{0,16},{16,0},{1,17},{17,1},{2,18},{18,2},{3,19},{19,3},{4,20},{20... | collective-permute-start | bytes 417800 | tf_op jit(solution)/shard_map/ppermute | solution.py:224
  23.4 9.1 %collective-permute-start.16 = (bf16[144,256]{1,0:T(8,128)(2,1)S(1)}, bf16[144,256]{1,0:T(8,128)(2,1)S(1)}, u32[]{:S(2)}, u32[]{:S(2)}) collective-permute-start(bf16[144,256]{1,0:T(8,128)(2,1)S(1)} %get-tuple-element.27), channel_id=1, source_target_pairs={{0,4},{4,0},{1,5},{5,1},{2,6},{6,2},{3,7},{7,3},{8,12},{12,8},{9,1... | collective-permute-start | bytes 221192 | tf_op jit(solution)/shard_map/ppermute | solution.py:222
  26.0 7.5 %collective-permute-start.17 = (bf16[144,256]{1,0:T(8,128)(2,1)S(1)}, bf16[144,256]{1,0:T(8,128)(2,1)S(1)}, u32[]{:S(2)}, u32[]{:S(2)}) collective-permute-start(bf16[144,256]{1,0:T(8,128)(2,1)S(1)} %get-tuple-element.28), channel_id=1, source_target_pairs={{0,20},{4,16},{16,4},{20,0},{1,21},{5,17},{17,5},{21,1},{2,22},{6,... | collective-permute-start | bytes 221192 | tf_op jit(solution)/shard_map/ppermute | solution.py:221

commit v2 on v1

--- a/solution.py
+++ b/solution.py
@@ -14,6 +14,7 @@
 EACH = 1 + ROUNDS
 SIDE = 16
 DIRECT = 8
+ORDER = (0, 7, 5, 6, 3, 4, 2, 1)
 STATS = 8
 F32 = jnp.float32
 BF16 = jnp.bfloat16
@@ -25,7 +26,7 @@
 
 
 def prep_kernel(apart, assignment, pairing, half, me, x_ref, *refs):
-    outs, (centred, high_rows, low_rows, side) = refs[:-4], refs[-4:]
+    outs, (centred, centres, side) = refs[:-3], refs[-3:]
     cells, genes = x_ref.shape
     panels = assignment.shape[0]
     panel = genes // panels
@@ -35,11 +36,9 @@
         start = pl.multiple_of(p * panel, panel)
         block = x_ref[:, pl.ds(start, panel)]
         mean = jnp.sum(block, axis=0, keepdims=True) * (1.0 / cells)
-        high, rest = split_two(mean)
-        low = rest.astype(BF16).astype(F32)
-        centred[p] = (block - (high + low)).astype(BF16)
-        high_rows[pl.ds(p, 1), :] = high
-        low_rows[pl.ds(p, 1), :] = low
+        centre = mean.astype(BF16).astype(F32)
+        centred[p] = (block - centre).astype(BF16)
+        centres[pl.ds(p, 1), :] = centre
         return carry
 
     lax.fori_loop(0, panels, one_panel, 0, unroll=panels <= 16)
@@ -53,12 +52,11 @@
             for k in range(EACH):
                 p = own if k == 0 else pairing[k - 1, own]
                 out[at, pl.ds((place * EACH + k) * cells, cells), :] = centred[p]
-                side[pl.ds(place * 2 * EACH + k, 1), :] = high_rows[pl.ds(p, 1), :]
-                side[pl.ds(place * 2 * EACH + EACH + k, 1), :] = low_rows[pl.ds(p, 1), :]
-        out[at, pl.ds(SLOTS * EACH * cells, SIDE), :] = side[...].astype(BF16)
+                side[pl.ds(place * EACH + k, 1), :] = centres[pl.ds(p, 1), :]
+        out[at, pl.ds(SLOTS * EACH * cells, STATS), :] = side[...].astype(BF16)
 
     if apart:
-        for k, out in enumerate(outs):
+        for k, out in zip(ORDER, outs):
             one_message(me[0] ^ k, out, 0)
     else:
         lax.fori_loop(0, n_wide, lambda w, carry: one_message(w, outs[0], w) or carry, 0)
@@ -79,14 +77,13 @@
     member = lax.broadcasted_iota(jnp.int32, (blocks, rows), 1) // cells
     member = (member == lax.broadcasted_iota(jnp.int32, (blocks, rows), 0)).astype(BF16)
     side = jnp.concatenate(
-        [r[:, pl.ds(SLOTS * EACH * cells, SIDE), :].astype(F32) for r in received], axis=0
+        [r[:, pl.ds(SLOTS * EACH * cells, STATS), :].astype(F32) for r in received], axis=0
     )
     operands, means, squares = [], [], []
     for k in range(EACH):
         data = part((which * EACH + k) * cells, cells)
         sums = jnp.dot(member, data, preferred_element_type=F32)
-        row = which * 2 * EACH + k
-        block_mean = side[:, row, :] + side[:, row + EACH, :] + sums * (1.0 / cells)
+        block_mean = side[:, which * EACH + k, :] + sums * (1.0 / cells)
         mean = jnp.sum(block_mean, axis=0, keepdims=True) * (1.0 / blocks)
         shift = block_mean - mean
         wide_data = data.astype(F32)
@@ -123,6 +120,15 @@
             ref[pl.ds(base, SIDE), :] = packed
 
 
+def unpacked(ref, base):
+    if ref.dtype == F32:
+        parts = ref[pl.ds(base, STATS), :]
+        return parts[0:EACH], parts[EACH : 2 * EACH]
+    parts = ref[pl.ds(base, SIDE), :].astype(F32)
+    mean = parts[4 * EACH : 5 * EACH] + parts[2 * EACH : 3 * EACH] + parts[0:EACH]
+    return mean, parts[3 * EACH : 4 * EACH] + parts[EACH : 2 * EACH]
+
+
 def finish_kernel(total, place, nearer, keep_ref, x_ref, half_ref, both_ref, out_ref, columns):
     quarter, panel = out_ref.shape[2:]
     base = ROUNDS * quarter
@@ -130,11 +136,10 @@
     near = nearer[0]
     sources = ((near, keep_ref, half_ref), (1 - near, x_ref, both_ref))
     for i, (slot, same_ref, other_ref) in enumerate(sources):
-        same = same_ref[pl.ds(base, STATS), :]
-        parts = other_ref[pl.ds(base, SIDE), :].astype(F32)
-        other = parts[4 * EACH : 5 * EACH] + parts[2 * EACH : 3 * EACH] + parts[0:EACH]
-        gap = same[0:EACH] - other
-        square = same[EACH : 2 * EACH] + (parts[3 * EACH : 4 * EACH] + parts[EACH : 2 * EACH])
+        same_mean, same_square = unpacked(same_ref, base)
+        other_mean, other_square = unpacked(other_ref, base)
+        gap = same_mean - other_mean
+        square = same_square + other_square
         var = square * (1.0 / total) + (gap * gap) * 0.25
         inv = lax.rsqrt(var + 1e-05)
         pair = jnp.concatenate([gap[0:1], inv[0:1], jnp.zeros((STATS - 2, panel), F32)], axis=0)
@@ -144,7 +149,7 @@
         inv_row = side[:, 1:2] * total ** (-0.5)
         for r in range(ROUNDS):
             rows = pl.ds(r * quarter, quarter)
-            tile = same_ref[rows, :] + other_ref[rows, :].astype(F32)
+            tile = same_ref[rows, :].astype(F32) + other_ref[rows, :].astype(F32)
             tile = tile + gap_row * gap[1 + r : 2 + r]
             out_ref[r, slot] = tile * inv_row * inv[1 + r : 2 + r]
 
@@ -160,8 +165,8 @@
         here = [lax.all_to_all(sent[0], ("x", "rest"), split_axis=0, concat_axis=0, tiled=True)]
     else:
         here = [sent[0]]
-        for k in range(1, n_wide):
-            here.append(lax.ppermute(sent[k], ("x", "rest"), [(i, i ^ k) for i in range(n_wide)]))
+        for k, value in zip(ORDER[1:], sent[1:]):
+            here.append(lax.ppermute(value, ("x", "rest"), [(i, i ^ k) for i in range(n_wide)]))
     there = []
     for value in here:
         there.append(lax.ppermute(value, "core", [(0, 1), (1, 0)]))
@@ -181,7 +186,7 @@
     nearer = (x ^ lax.axis_index("half")).reshape(1).astype(jnp.int32)
     smem = pl.BlockSpec(memory_space=pltpu.SMEM)
     vmem = pl.BlockSpec(memory_space=pltpu.VMEM)
-    message = SLOTS * EACH * cells + SIDE
+    message = SLOTS * EACH * cells + STATS
     received_bytes = 2 * n_wide * message * panel * 2
     array, in_vmem = on_chip(received_bytes <= 4 << 20)
     half = lax.axis_index("half").reshape(1).astype(jnp.int32)
@@ -196,18 +201,17 @@
         scratch_shapes=[
             pltpu.VMEM((panels, cells, panel), BF16),
             pltpu.VMEM((panels, panel), F32),
-            pltpu.VMEM((panels, panel), F32),
-            pltpu.VMEM((SIDE, panel), F32),
+            pltpu.VMEM((STATS, panel), F32),
         ],
         name="prep",
     )(assignment, pairing, half, me, expression)
     received = gather(sent, n_wide)
     base = ROUNDS * quarter
 
-    def gram(which, rows, dtype):
+    def gram(which, side):
         return pl.pallas_call(
             functools.partial(gram_kernel, cells, which),
-            out_shape=(array((rows, panel), dtype), array((rows, panel), dtype)),
+            out_shape=(array((base + side, panel), BF16 if side == SIDE else F32),) * 2,
             in_specs=[smem] + [vmem] * len(received),
             out_specs=(vmem, vmem),
             scratch_shapes=[pltpu.VMEM((ROUNDS, panel, panel), F32)],
@@ -217,10 +221,10 @@
             name="gram",
         )(place, *map(in_vmem, received))
 
-    to_half, to_both = gram(0, base + SIDE, BF16)
+    to_half, to_both = gram(0, SIDE)
     from_both = lax.ppermute(to_both, ("x", "half"), [(i, i ^ 3) for i in range(4)])
     from_half = lax.ppermute(to_half, "half", [(0, 1), (1, 0)])
-    keep, to_x = gram(1, base + STATS, F32)
+    keep, to_x = gram(1, STATS)
     from_x = lax.ppermute(to_x, "x", [(0, 1), (1, 0)])
     return pl.pallas_call(
         functools.partial(finish_kernel, total),

time: 34.7 us -> 35 us (level)
  waiting for transfers between devices: 13.4 us -> 14 us
    ppermute x1, waiting for transfers between devices: 6.41 us -> 4.57 us  [shards(): from_half = lax.ppermute(to_half, 'half', [(0, 1), (1, 0)])]
    ppermute x1, waiting for transfers between devices: 1.06 us -> 2.39 us  [shards(): lax.ppermute(to_both, ('x', 'half'), [(i, i ^ 3) for i in range(4)])]
    ppermute x7, waiting for transfers between devices: 4.92 us -> 6.05 us  [gather(): lax.ppermute(value, ('x', 'rest'), [(i, i ^ k) for i in range(n_wide)])]
    ppermute x1, starting transfers between devices: 1.87 us -> 1 us  [shards(): from_x = lax.ppermute(to_x, 'x', [(0, 1), (1, 0)])]
    ppermute x1, starting transfers between devices: 0.01 us -> 0.87 us  [shards(): lax.ppermute(to_both, ('x', 'half'), [(i, i ^ 3) for i in range(4)])]
    ppermute x8, starting transfers between devices: 2.04 us -> 1.6 us  [gather(): there.append(lax.ppermute(value, 'core', [(0, 1), (1, 0)]))]
  transfers between devices with their start and end apart: 18 -> 18, of which waited for: 8 -> 9; matrix products, arithmetic and copies ran while one was open for 0% -> 0% of each run, Pallas kernels for 2% -> 1%
where the time goes in v2:
time: 35 us; the launch traced here: 34.8 us
  starting transfers between devices  17.4 us (50%)
  waiting for transfers between devices  14 us (40%)
  Pallas kernels  3.42 us (10%)
    ppermute x7, starting transfers between devices, gather(): lax.ppermute(value, ('x', 'rest'), [(i, i ^ k) for i in range(n_wide)])  11.3 us
    ppermute x7, waiting for transfers between devices, gather(): lax.ppermute(value, ('x', 'rest'), [(i, i ^ k) for i in range(n_wide)])  6.05 us
    ppermute x1, waiting for transfers between devices, shards(): from_half = lax.ppermute(to_half, 'half', [(0, 1), (1, 0)])  4.57 us
    ppermute x1, starting transfers between devices, shards(): from_half = lax.ppermute(to_half, 'half', [(0, 1), (1, 0)])  2.66 us
    ppermute x1, waiting for transfers between devices, shards(): lax.ppermute(to_both, ('x', 'half'), [(i, i ^ 3) for i in range(4)])  2.39 us
    ppermute x8, starting transfers between devices, gather(): there.append(lax.ppermute(value, 'core', [(0, 1), (1, 0)]))  1.6 us
    pallas_call x1, Pallas kernels, shards(): pl.pallas_call(functools.partial(prep_kernel, apart), out_shape=(array(sh...  1.34 us
    pallas_call x1, Pallas kernels, shards(): pl.pallas_call(functools.partial(finish_kernel, total), out_shape=jax.Sha...  1.04 us
  transfers between devices with their start and end apart: 18, of which 9 were waited for; matrix products, arithmetic and copies ran while one was open for 0% of the time, Pallas kernels for 1%

profile of v2, /device:TPU:0, one launch (start us, length us, event | category | flops | bytes accessed | tf_op | source)
XLA Modules:
  0.0 34.8 jit_solution(12688403427886373726)
XLA Ops:
  0.0 1.3 %prep.1 = (bf16[1,200,256]{2,1,0:T(8,128)(2,1)S(1)}, bf16[1,200,256]{2,1,0:T(8,128)(2,1)S(1)}, bf16[1,200,256]{2,1,0:T(8,128)(2,1)S(1)}, bf16[1,200,256]{2,1,0:T...) custom-call(s32[16]{0:T(128)} %assignment.1, ...), custom_call_target="tpu_custom_call" | custom-call | tf_op jit(solution)/shard_map/prep/pallas_call | solution.py:196
  1.3 5.0 %collective-permute-start = (bf16[1,200,256]{2,1,0:T(8,128)(2,1)S(1)}, bf16[1,200,256]{2,1,0:T(8,128)(2,1)S(1)}, u32[]{:S(2)}, u32[]{:S(2)}) collective-permute-start(bf16[1,200,256]{2,1,0:T(8,128)(2,1)S(1)} %get-tuple-element.18), channel_id=1, source_target_pairs={{0,19},{1,18},{2,17},{3,16},{16,3},{17,2},{18,1},{19,0},{4,23},{5,... | collective-permute-start | bytes 307208 | tf_op jit(solution)/shard_map/ppermute | solution.py:169
  6.3 0.5 %collective-permute-start.1 = (bf16[1,200,256]{2,1,0:T(8,128)(2,1)S(1)}, bf16[1,200,256]{2,1,0:T(8,128)(2,1)S(1)}, u32[]{:S(2)}, u32[]{:S(2)}) collective-permute-start(bf16[1,200,256]{2,1,0:T(8,128)(2,1)S(1)} %get-tuple-element.19), channel_id=1, source_target_pairs={{0,17},{1,16},{2,19},{3,18},{16,1},{17,0},{18,3},{19,2},{4,21},{5,... | collective-permute-start | bytes 307208 | tf_op jit(solution)/shard_map/ppermute | solution.py:169
  6.8 1.4 %collective-permute-start.2 = (bf16[1,200,256]{2,1,0:T(8,128)(2,1)S(1)}, bf16[1,200,256]{2,1,0:T(8,128)(2,1)S(1)}, u32[]{:S(2)}, u32[]{:S(2)}) collective-permute-start(bf16[1,200,256]{2,1,0:T(8,128)(2,1)S(1)} %get-tuple-element.20), channel_id=1, source_target_pairs={{0,18},{1,19},{2,16},{3,17},{16,2},{17,3},{18,0},{19,1},{4,22},{5,... | collective-permute-start | bytes 307208 | tf_op jit(solution)/shard_map/ppermute | solution.py:169
  8.2 2.5 %collective-permute-start.3 = (bf16[1,200,256]{2,1,0:T(8,128)(2,1)S(1)}, bf16[1,200,256]{2,1,0:T(8,128)(2,1)S(1)}, u32[]{:S(2)}, u32[]{:S(2)}) collective-permute-start(bf16[1,200,256]{2,1,0:T(8,128)(2,1)S(1)} %get-tuple-element.21), channel_id=1, source_target_pairs={{0,3},{1,2},{2,1},{3,0},{16,19},{17,18},{18,17},{19,16},{4,7},{5,6... | collective-permute-start | bytes 307208 | tf_op jit(solution)/shard_map/ppermute | solution.py:169
  10.7 0.5 %collective-permute-start.4 = (bf16[1,200,256]{2,1,0:T(8,128)(2,1)S(1)}, bf16[1,200,256]{2,1,0:T(8,128)(2,1)S(1)}, u32[]{:S(2)}, u32[]{:S(2)}) collective-permute-start(bf16[1,200,256]{2,1,0:T(8,128)(2,1)S(1)} %get-tuple-element.22), channel_id=1, source_target_pairs={{0,16},{1,17},{2,18},{3,19},{16,0},{17,1},{18,2},{19,3},{4,20},{5,... | collective-permute-start | bytes 307208 | tf_op jit(solution)/shard_map/ppermute | solution.py:169
  11.3 0.0 collective-permute-done.refs_1_
  11.3 0.5 %collective-permute-start.5 = (bf16[1,200,256]{2,1,0:T(8,128)(2,1)S(1)}, bf16[1,200,256]{2,1,0:T(8,128)(2,1)S(1)}, u32[]{:S(2)}, u32[]{:S(2)}) collective-permute-start(bf16[1,200,256]{2,1,0:T(8,128)(2,1)S(1)} %get-tuple-element.23), channel_id=1, source_target_pairs={{0,2},{1,3},{2,0},{3,1},{16,18},{17,19},{18,16},{19,17},{4,6},{5,7... | collective-permute-start | bytes 307208 | tf_op jit(solution)/shard_map/ppermute | solution.py:169
  11.7 2.9 %collective-permute-done.1.refs_2_ = bf16[1,200,256]{2,1,0:T(8,128)(2,1)S(1)} collective-permute-done((bf16[1,200,256]{2,1,0:T(8,128)(2,1)S(1)}, bf16[1,200,256]{2,1,0:T(8,128)(2,1)S(1)}, u32[]{:S(2)}, u32[]{:S(2)}) %collective-permute-start.1) | collective-permute-done | bytes 102432 | tf_op jit(solution)/shard_map/ppermute | solution.py:169
  14.6 0.9 %collective-permute-start.6 = (bf16[1,200,256]{2,1,0:T(8,128)(2,1)S(1)}, bf16[1,200,256]{2,1,0:T(8,128)(2,1)S(1)}, u32[]{:S(2)}, u32[]{:S(2)}) collective-permute-start(bf16[1,200,256]{2,1,0:T(8,128)(2,1)S(1)} %get-tuple-element.24), channel_id=1, source_target_pairs={{0,1},{1,0},{2,3},{3,2},{16,17},{17,16},{18,19},{19,18},{4,5},{5,4... | collective-permute-start | bytes 307208 | tf_op jit(solution)/shard_map/ppermute | solution.py:169
  15.5 0.0 collective-permute-start.7
  15.5 0.6 %collective-permute-done.3.refs_4_ = bf16[1,200,256]{2,1,0:T(8,128)(2,1)S(1)} collective-permute-done((bf16[1,200,256]{2,1,0:T(8,128)(2,1)S(1)}, bf16[1,200,256]{2,1,0:T(8,128)(2,1)S(1)}, u32[]{:S(2)}, u32[]{:S(2)}) %collective-permute-start.3) | collective-permute-done | bytes 102432 | tf_op jit(solution)/shard_map/ppermute | solution.py:169
  16.1 0.0 collective-permute-start.8
  16.1 0.0 collective-permute-done.4.refs_5_
  16.1 0.5 %collective-permute-start.9 = (bf16[1,200,256]{2,1,0:T(8,128)(2,1)S(1)}, bf16[1,200,256]{2,1,0:T(8,128)(2,1)S(1)}, u32[]{:S(2)}, u32[]{:S(2)}) collective-permute-start(bf16[1,200,256]{2,1,0:T(8,128)(2,1)S(1)} %collective-permute-done.1.refs_2_), channel_id=1, source_target_pairs={{0,8},{8,0},{1,9},{9,1},{2,10},{10,2},{3,11},{11,3},{4,12},{12,4},... | collective-permute-start | bytes 307208 | tf_op jit(solution)/shard_map/ppermute | solution.py:172
  16.6 0.1 collective-permute-start.10
  16.7 2.5 %collective-permute-done.6.refs_7_ = bf16[1,200,256]{2,1,0:T(8,128)(2,1)S(1)} collective-permute-done((bf16[1,200,256]{2,1,0:T(8,128)(2,1)S(1)}, bf16[1,200,256]{2,1,0:T(8,128)(2,1)S(1)}, u32[]{:S(2)}, u32[]{:S(2)}) %collective-permute-start.6) | collective-permute-done | bytes 102432 | tf_op jit(solution)/shard_map/ppermute | solution.py:169
  19.3 0.5 %collective-permute-start.12 = (bf16[1,200,256]{2,1,0:T(8,128)(2,1)S(1)}, bf16[1,200,256]{2,1,0:T(8,128)(2,1)S(1)}, u32[]{:S(2)}, u32[]{:S(2)}) collective-permute-start(bf16[1,200,256]{2,1,0:T(8,128)(2,1)S(1)} %collective-permute-done.4.refs_5_), channel_id=1, source_target_pairs={{0,8},{8,0},{1,9},{9,1},{2,10},{10,2},{3,11},{11,3},{4,12},{12,4},... | collective-permute-start | bytes 307208 | tf_op jit(solution)/shard_map/ppermute | solution.py:172
  19.8 0.1 collective-permute-start.13
  19.8 0.4 %collective-permute-start.14 = (bf16[1,200,256]{2,1,0:T(8,128)(2,1)S(1)}, bf16[1,200,256]{2,1,0:T(8,128)(2,1)S(1)}, u32[]{:S(2)}, u32[]{:S(2)}) collective-permute-start(bf16[1,200,256]{2,1,0:T(8,128)(2,1)S(1)} %collective-permute-done.6.refs_7_), channel_id=1, source_target_pairs={{0,8},{8,0},{1,9},{9,1},{2,10},{10,2},{3,11},{11,3},{4,12},{12,4},... | collective-permute-start | bytes 307208 | tf_op jit(solution)/shard_map/ppermute | solution.py:172
  20.3 0.3 collective-permute-done.11.refs_12_
  20.6 0.2 collective-permute-done.12.refs_13_
  20.7 0.4 %collective-permute-done.13.refs_14_ = bf16[1,200,256]{2,1,0:T(8,128)(2,1)S(1)} collective-permute-done((bf16[1,200,256]{2,1,0:T(8,128)(2,1)S(1)}, bf16[1,200,256]{2,1,0:T(8,128)(2,1)S(1)}, u32[]{:S(2)}, u32[]{:S(2)}) %collective-permute-start.13) | collective-permute-done | bytes 102432 | tf_op jit(solution)/shard_map/ppermute | solution.py:172
  21.1 0.2 collective-permute-done.14.refs_15_
  21.2 0.5 %gram.2 = (f32[136,256]{1,0:T(8,128)S(1)}, f32[136,256]{1,0:T(8,128)S(1)}) custom-call(s32[1]{0:T(128)} %bitcast.place, bf16[1,200,256]{2,1,0:T(8,128)(2,1)S(1)} %get-tuple-element.17.refs_0_, bf16[1,200,256]{2,1,0:T(8,128)(2,1)S(1)} %collective-permute-done.refs_1_, bf16[1,200,256]{2,1,0:T(8,128)(2,1)S(1)} %collective-permute-done.1.refs_2_, ...), custom_call_target="tpu_custom_call" | custom-call | tf_op jit(solution)/shard_map/gram/pallas_call | solution.py:212
  21.8 1.0 %collective-permute-start.15 = (f32[136,256]{1,0:T(8,128)S(1)}, f32[136,256]{1,0:T(8,128)S(1)}, u32[]{:S(2)}, u32[]{:S(2)}) collective-permute-start(f32[136,256]{1,0:T(8,128)S(1)} %get-tuple-element.26), channel_id=1, source_target_pairs={{0,16},{16,0},{1,17},{17,1},{2,18},{18,2},{3,19},{19,3},{4,20},{20... | collective-permute-start | bytes 417800 | tf_op jit(solution)/shard_map/ppermute | solution.py:228
  22.8 0.5 %gram.3 = (bf16[144,256]{1,0:T(8,128)(2,1)S(1)}, bf16[144,256]{1,0:T(8,128)(2,1)S(1)}) custom-call(s32[1]{0:T(128)} %bitcast.place, bf16[1,200,256]{2,1,0:T(8,128)(2,1)S(1)} %get-tuple-element.17.refs_0_, bf16[1,200,256]{2,1,0:T(8,128)(2,1)S(1)} %collective-permute-done.refs_1_, bf16[1,200,256]{2,1,0:T(8,128)(2,1)S(1)} %collective-permute-done.1.refs_2_, ...), custom_call_target="tpu_custom_call" | custom-call | tf_op jit(solution)/shard_map/gram/pallas_call | solution.py:212
  23.3 2.7 %collective-permute-start.16 = (bf16[144,256]{1,0:T(8,128)(2,1)S(1)}, bf16[144,256]{1,0:T(8,128)(2,1)S(1)}, u32[]{:S(2)}, u32[]{:S(2)}) collective-permute-start(bf16[144,256]{1,0:T(8,128)(2,1)S(1)} %get-tuple-element.27), channel_id=1, source_target_pairs={{0,4},{4,0},{1,5},{5,1},{2,6},{6,2},{3,7},{7,3},{8,12},{12,8},{9,1... | collective-permute-start | bytes 221192 | tf_op jit(solution)/shard_map/ppermute | solution.py:226
  25.9 0.9 %collective-permute-start.17 = (bf16[144,256]{1,0:T(8,128)(2,1)S(1)}, bf16[144,256]{1,0:T(8,128)(2,1)S(1)}, u32[]{:S(2)}, u32[]{:S(2)}) collective-permute-start(bf16[144,256]{1,0:T(8,128)(2,1)S(1)} %get-tuple-element.28), channel_id=1, source_target_pairs={{0,20},{4,16},{16,4},{20,0},{1,21},{5,17},{17,5},{21,1},{2,22},{6,... | collective-permute-start | bytes 221192 | tf_op jit(solution)/shard_map/ppermute | solution.py:225
  26.8 4.6 %collective-permute-done.16.half_ref = bf16[144,256]{1,0:T(8,128)(2,1)S(1)} collective-permute-done((bf16[144,256]{1,0:T(8,128)(2,1)S(1)}, bf16[144,256]{1,0:T(8,128)(2,1)S(1)}, u32[]{:S(2)}, u32[]{:S(2)}) %collective-permute-start.16) | collective-permute-done | bytes 73760 | tf_op jit(solution)/shard_map/ppermute | solution.py:226
  31.4 2.4 %collective-permute-done.17.both_ref = bf16[144,256]{1,0:T(8,128)(2,1)S(1)} collective-permute-done((bf16[144,256]{1,0:T(8,128)(2,1)S(1)}, bf16[144,256]{1,0:T(8,128)(2,1)S(1)}, u32[]{:S(2)}, u32[]{:S(2)}) %collective-permute-start.17) | collective-permute-done | bytes 73760 | tf_op jit(solution)/shard_map/ppermute | solution.py:225
  33.8 1.0 %finish.1 = f32[2,2,64,256]{3,2,1,0:T(8,128)} custom-call(s32[1]{0:T(128)} %bitcast.place, s32[1]{0:T(128)} %bitcast.1.nearer, f32[136,256]{1,0:T(8,128)S(1)} %get-tuple-element.25.keep_ref, f32[136,256]{1,0:T(8,128)S(1)} %collective-permute-done.15.x_ref, bf16[144,256]{1,0:T(8,128)(2,1)S(1)} %collective-permute-done.16.half_ref, ...), custom_call_target="tpu_custom_call" | custom-call | tf_op jit(solution)/shard_map/finish/pallas_call | solution.py:229
  (8 shorter events, 0.0 us)
Async XLA Ops:
  1.3 9.9 %collective-permute-start = (bf16[1,200,256]{2,1,0:T(8,128)(2,1)S(1)}, bf16[1,200,256]{2,1,0:T(8,128)(2,1)S(1)}, u32[]{:S(2)}, u32[]{:S(2)}) collective-permute-start(bf16[1,200,256]{2,1,0:T(8,128)(2,1)S(1)} %get-tuple-element.18), channel_id=1, source_target_pairs={{0,19},{1,18},{2,17},{3,16},{16,3},{17,2},{18,1},{19,0},{4,23},{5,... | collective-permute-start | bytes 307208 | tf_op jit(solution)/shard_map/ppermute | solution.py:169
  6.3 8.2 %collective-permute-start.1 = (bf16[1,200,256]{2,1,0:T(8,128)(2,1)S(1)}, bf16[1,200,256]{2,1,0:T(8,128)(2,1)S(1)}, u32[]{:S(2)}, u32[]{:S(2)}) collective-permute-start(bf16[1,200,256]{2,1,0:T(8,128)(2,1)S(1)} %get-tuple-element.19), channel_id=1, source_target_pairs={{0,17},{1,16},{2,19},{3,18},{16,1},{17,0},{18,3},{19,2},{4,21},{5,... | collective-permute-start | bytes 307208 | tf_op jit(solution)/shard_map/ppermute | solution.py:169
  6.8 8.7 %collective-permute-start.2 = (bf16[1,200,256]{2,1,0:T(8,128)(2,1)S(1)}, bf16[1,200,256]{2,1,0:T(8,128)(2,1)S(1)}, u32[]{:S(2)}, u32[]{:S(2)}) collective-permute-start(bf16[1,200,256]{2,1,0:T(8,128)(2,1)S(1)} %get-tuple-element.20), channel_id=1, source_target_pairs={{0,18},{1,19},{2,16},{3,17},{16,2},{17,3},{18,0},{19,1},{4,22},{5,... | collective-permute-start | bytes 307208 | tf_op jit(solution)/shard_map/ppermute | solution.py:169
  8.2 7.9 %collective-permute-start.3 = (bf16[1,200,256]{2,1,0:T(8,128)(2,1)S(1)}, bf16[1,200,256]{2,1,0:T(8,128)(2,1)S(1)}, u32[]{:S(2)}, u32[]{:S(2)}) collective-permute-start(bf16[1,200,256]{2,1,0:T(8,128)(2,1)S(1)} %get-tuple-element.21), channel_id=1, source_target_pairs={{0,3},{1,2},{2,1},{3,0},{16,19},{17,18},{18,17},{19,16},{4,7},{5,6... | collective-permute-start | bytes 307208 | tf_op jit(solution)/shard_map/ppermute | solution.py:169
  10.7 5.4 %collective-permute-start.4 = (bf16[1,200,256]{2,1,0:T(8,128)(2,1)S(1)}, bf16[1,200,256]{2,1,0:T(8,128)(2,1)S(1)}, u32[]{:S(2)}, u32[]{:S(2)}) collective-permute-start(bf16[1,200,256]{2,1,0:T(8,128)(2,1)S(1)} %get-tuple-element.22), channel_id=1, source_target_pairs={{0,16},{1,17},{2,18},{3,19},{16,0},{17,1},{18,2},{19,3},{4,20},{5,... | collective-permute-start | bytes 307208 | tf_op jit(solution)/shard_map/ppermute | solution.py:169
  11.3 5.4 %collective-permute-start.5 = (bf16[1,200,256]{2,1,0:T(8,128)(2,1)S(1)}, bf16[1,200,256]{2,1,0:T(8,128)(2,1)S(1)}, u32[]{:S(2)}, u32[]{:S(2)}) collective-permute-start(bf16[1,200,256]{2,1,0:T(8,128)(2,1)S(1)} %get-tuple-element.23), channel_id=1, source_target_pairs={{0,2},{1,3},{2,0},{3,1},{16,18},{17,19},{18,16},{19,17},{4,6},{5,7... | collective-permute-start | bytes 307208 | tf_op jit(solution)/shard_map/ppermute | solution.py:169
  14.6 4.7 %collective-permute-start.6 = (bf16[1,200,256]{2,1,0:T(8,128)(2,1)S(1)}, bf16[1,200,256]{2,1,0:T(8,128)(2,1)S(1)}, u32[]{:S(2)}, u32[]{:S(2)}) collective-permute-start(bf16[1,200,256]{2,1,0:T(8,128)(2,1)S(1)} %get-tuple-element.24), channel_id=1, source_target_pairs={{0,1},{1,0},{2,3},{3,2},{16,17},{17,16},{18,19},{19,18},{4,5},{5,4... | collective-permute-start | bytes 307208 | tf_op jit(solution)/shard_map/ppermute | solution.py:169
  15.5 3.8 %collective-permute-start.7 = (bf16[1,200,256]{2,1,0:T(8,128)(2,1)S(1)}, bf16[1,200,256]{2,1,0:T(8,128)(2,1)S(1)}, u32[]{:S(2)}, u32[]{:S(2)}) collective-permute-start(bf16[1,200,256]{2,1,0:T(8,128)(2,1)S(1)} %get-tuple-element.17.refs_0_), channel_id=1, source_target_pairs={{0,8},{8,0},{1,9},{9,1},{2,10},{10,2},{3,11},{11,3},{4,12},{12,4},... | collective-permute-start | bytes 307208 | tf_op jit(solution)/shard_map/ppermute | solution.py:172
  16.1 3.7 %collective-permute-start.8 = (bf16[1,200,256]{2,1,0:T(8,128)(2,1)S(1)}, bf16[1,200,256]{2,1,0:T(8,128)(2,1)S(1)}, u32[]{:S(2)}, u32[]{:S(2)}) collective-permute-start(bf16[1,200,256]{2,1,0:T(8,128)(2,1)S(1)} %collective-permute-done.refs_1_), channel_id=1, source_target_pairs={{0,8},{8,0},{1,9},{9,1},{2,10},{10,2},{3,11},{11,3},{4,12},{12,4},... | collective-permute-start | bytes 307208 | tf_op jit(solution)/shard_map/ppermute | solution.py:172
  16.1 3.7 %collective-permute-start.9 = (bf16[1,200,256]{2,1,0:T(8,128)(2,1)S(1)}, bf16[1,200,256]{2,1,0:T(8,128)(2,1)S(1)}, u32[]{:S(2)}, u32[]{:S(2)}) collective-permute-start(bf16[1,200,256]{2,1,0:T(8,128)(2,1)S(1)} %collective-permute-done.1.refs_2_), channel_id=1, source_target_pairs={{0,8},{8,0},{1,9},{9,1},{2,10},{10,2},{3,11},{11,3},{4,12},{12,4},... | collective-permute-start | bytes 307208 | tf_op jit(solution)/shard_map/ppermute | solution.py:172
  16.6 3.7 %collective-permute-start.10 = (bf16[1,200,256]{2,1,0:T(8,128)(2,1)S(1)}, bf16[1,200,256]{2,1,0:T(8,128)(2,1)S(1)}, u32[]{:S(2)}, u32[]{:S(2)}) collective-permute-start(bf16[1,200,256]{2,1,0:T(8,128)(2,1)S(1)} %collective-permute-done.2.refs_3_), channel_id=1, source_target_pairs={{0,8},{8,0},{1,9},{9,1},{2,10},{10,2},{3,11},{11,3},{4,12},{12,4},... | collective-permute-start | bytes 307208 | tf_op jit(solution)/shard_map/ppermute | solution.py:172
  19.2 1.3 %collective-permute-start.11 = (bf16[1,200,256]{2,1,0:T(8,128)(2,1)S(1)}, bf16[1,200,256]{2,1,0:T(8,128)(2,1)S(1)}, u32[]{:S(2)}, u32[]{:S(2)}) collective-permute-start(bf16[1,200,256]{2,1,0:T(8,128)(2,1)S(1)} %collective-permute-done.3.refs_4_), channel_id=1, source_target_pairs={{0,8},{8,0},{1,9},{9,1},{2,10},{10,2},{3,11},{11,3},{4,12},{12,4},... | collective-permute-start | bytes 307208 | tf_op jit(solution)/shard_map/ppermute | solution.py:172
  19.3 1.5 %collective-permute-start.12 = (bf16[1,200,256]{2,1,0:T(8,128)(2,1)S(1)}, bf16[1,200,256]{2,1,0:T(8,128)(2,1)S(1)}, u32[]{:S(2)}, u32[]{:S(2)}) collective-permute-start(bf16[1,200,256]{2,1,0:T(8,128)(2,1)S(1)} %collective-permute-done.4.refs_5_), channel_id=1, source_target_pairs={{0,8},{8,0},{1,9},{9,1},{2,10},{10,2},{3,11},{11,3},{4,12},{12,4},... | collective-permute-start | bytes 307208 | tf_op jit(solution)/shard_map/ppermute | solution.py:172
  19.8 1.3 %collective-permute-start.13 = (bf16[1,200,256]{2,1,0:T(8,128)(2,1)S(1)}, bf16[1,200,256]{2,1,0:T(8,128)(2,1)S(1)}, u32[]{:S(2)}, u32[]{:S(2)}) collective-permute-start(bf16[1,200,256]{2,1,0:T(8,128)(2,1)S(1)} %collective-permute-done.5.refs_6_), channel_id=1, source_target_pairs={{0,8},{8,0},{1,9},{9,1},{2,10},{10,2},{3,11},{11,3},{4,12},{12,4},... | collective-permute-start | bytes 307208 | tf_op jit(solution)/shard_map/ppermute | solution.py:172
  19.8 1.4 %collective-permute-start.14 = (bf16[1,200,256]{2,1,0:T(8,128)(2,1)S(1)}, bf16[1,200,256]{2,1,0:T(8,128)(2,1)S(1)}, u32[]{:S(2)}, u32[]{:S(2)}) collective-permute-start(bf16[1,200,256]{2,1,0:T(8,128)(2,1)S(1)} %collective-permute-done.6.refs_7_), channel_id=1, source_target_pairs={{0,8},{8,0},{1,9},{9,1},{2,10},{10,2},{3,11},{11,3},{4,12},{12,4},... | collective-permute-start | bytes 307208 | tf_op jit(solution)/shard_map/ppermute | solution.py:172
  21.8 12.0 %collective-permute-start.15 = (f32[136,256]{1,0:T(8,128)S(1)}, f32[136,256]{1,0:T(8,128)S(1)}, u32[]{:S(2)}, u32[]{:S(2)}) collective-permute-start(f32[136,256]{1,0:T(8,128)S(1)} %get-tuple-element.26), channel_id=1, source_target_pairs={{0,16},{16,0},{1,17},{17,1},{2,18},{18,2},{3,19},{19,3},{4,20},{20... | collective-permute-start | bytes 417800 | tf_op jit(solution)/shard_map/ppermute | solution.py:228
  23.3 8.1 %collective-permute-start.16 = (bf16[144,256]{1,0:T(8,128)(2,1)S(1)}, bf16[144,256]{1,0:T(8,128)(2,1)S(1)}, u32[]{:S(2)}, u32[]{:S(2)}) collective-permute-start(bf16[144,256]{1,0:T(8,128)(2,1)S(1)} %get-tuple-element.27), channel_id=1, source_target_pairs={{0,4},{4,0},{1,5},{5,1},{2,6},{6,2},{3,7},{7,3},{8,12},{12,8},{9,1... | collective-permute-start | bytes 221192 | tf_op jit(solution)/shard_map/ppermute | solution.py:226
  25.9 7.8 %collective-permute-start.17 = (bf16[144,256]{1,0:T(8,128)(2,1)S(1)}, bf16[144,256]{1,0:T(8,128)(2,1)S(1)}, u32[]{:S(2)}, u32[]{:S(2)}) collective-permute-start(bf16[144,256]{1,0:T(8,128)(2,1)S(1)} %get-tuple-element.28), channel_id=1, source_target_pairs={{0,20},{4,16},{16,4},{20,0},{1,21},{5,17},{17,5},{21,1},{2,22},{6,... | collective-permute-start | bytes 221192 | tf_op jit(solution)/shard_map/ppermute | solution.py:225

commit v3 on v2

--- a/solution.py
+++ b/solution.py
@@ -12,7 +12,6 @@
 SLOTS = 2
 ROUNDS = 2
 EACH = 1 + ROUNDS
-SIDE = 16
 DIRECT = 8
 ORDER = (0, 7, 5, 6, 3, 4, 2, 1)
 STATS = 8
@@ -23,6 +22,11 @@
 def split_two(value):
     high = value.astype(BF16).astype(F32)
     return high, value - high
+
+
+def half_turn(row):
+    middle = row.shape[1] // 2
+    return jnp.concatenate([row[:, middle:], row[:, :middle]], axis=1)
 
 
 def prep_kernel(apart, assignment, pairing, half, me, x_ref, *refs):
@@ -100,10 +104,7 @@
             extra = [scale * high, scale * high, scale * low, sums * (-8.0 / cells)]
         operands.append(jnp.concatenate([data, jnp.concatenate(extra, axis=0).astype(BF16)], axis=0))
     stats = jnp.concatenate(means + squares + [jnp.zeros((STATS - 2 * EACH, panel), F32)], axis=0)
-    high, rest = split_two(stats)
-    middle, low = split_two(rest)
-    packed = [high[0 : 2 * EACH], middle[0 : 2 * EACH], low[0:EACH], jnp.zeros((SIDE - 5 * EACH, panel), F32)]
-    packed = jnp.concatenate(packed, axis=0).astype(BF16)
+    high, low = split_two(stats)
     for r in range(ROUNDS):
         tile[r] = lax.dot_general(
             operands[0], operands[1 + r], (((0,), (0,)), ((), ())), preferred_element_type=F32
@@ -117,16 +118,21 @@
         if ref.dtype == F32:
             ref[pl.ds(base, STATS), :] = stats
         else:
-            ref[pl.ds(base, SIDE), :] = packed
+            needed = lax.broadcasted_iota(jnp.int32, (1, panel), 1) // quarter == index
+            own = [jnp.where(needed, v[0:1], half_turn(v[EACH : EACH + 1])) for v in (high, low)]
+            partners = [high[1:EACH], low[1:EACH], high[EACH + 1 : 2 * EACH]]
+            ref[pl.ds(base, STATS), :] = jnp.concatenate(own + partners, axis=0).astype(BF16)
 
 
 def unpacked(ref, base):
     if ref.dtype == F32:
         parts = ref[pl.ds(base, STATS), :]
         return parts[0:EACH], parts[EACH : 2 * EACH]
-    parts = ref[pl.ds(base, SIDE), :].astype(F32)
-    mean = parts[4 * EACH : 5 * EACH] + parts[2 * EACH : 3 * EACH] + parts[0:EACH]
-    return mean, parts[3 * EACH : 4 * EACH] + parts[EACH : 2 * EACH]
+    parts = ref[pl.ds(base, STATS), :].astype(F32)
+    own = parts[0:1] + parts[1:2]
+    mean = parts[2 : 2 + ROUNDS] + parts[2 + ROUNDS : 2 + 2 * ROUNDS]
+    square = parts[2 + 2 * ROUNDS : 2 + 3 * ROUNDS]
+    return jnp.concatenate([own, mean], axis=0), jnp.concatenate([half_turn(own), square], axis=0)
 
 
 def finish_kernel(total, place, nearer, keep_ref, x_ref, half_ref, both_ref, out_ref, columns):
@@ -208,10 +214,10 @@
     received = gather(sent, n_wide)
     base = ROUNDS * quarter
 
-    def gram(which, side):
+    def gram(which, dtype):
         return pl.pallas_call(
             functools.partial(gram_kernel, cells, which),
-            out_shape=(array((base + side, panel), BF16 if side == SIDE else F32),) * 2,
+            out_shape=(array((base + STATS, panel), dtype),) * 2,
             in_specs=[smem] + [vmem] * len(received),
             out_specs=(vmem, vmem),
             scratch_shapes=[pltpu.VMEM((ROUNDS, panel, panel), F32)],
@@ -221,10 +227,10 @@
             name="gram",
         )(place, *map(in_vmem, received))
 
-    to_half, to_both = gram(0, SIDE)
+    to_half, to_both = gram(0, BF16)
     from_both = lax.ppermute(to_both, ("x", "half"), [(i, i ^ 3) for i in range(4)])
     from_half = lax.ppermute(to_half, "half", [(0, 1), (1, 0)])
-    keep, to_x = gram(1, STATS)
+    keep, to_x = gram(1, F32)
     from_x = lax.ppermute(to_x, "x", [(0, 1), (1, 0)])
     return pl.pallas_call(
         functools.partial(finish_kernel, total),

time: 35 us -> 34.6 us (0.989)
  waiting for transfers between devices: 14 us -> 13.6 us
    ppermute x1, waiting for transfers between devices: 4.57 us -> 3.55 us  [shards(): from_half = lax.ppermute(to_half, 'half', [(0, 1), (1, 0)])]
    ppermute x1, waiting for transfers between devices: 2.39 us -> 3.07 us  [shards(): lax.ppermute(to_both, ('x', 'half'), [(i, i ^ 3) for i in range(4)])]
where the time goes in v3:
time: 34.6 us; the launch traced here: 34.5 us
  starting transfers between devices  17.4 us (50%)
  waiting for transfers between devices  13.6 us (39%)
  Pallas kernels  3.41 us (10%)
    ppermute x7, starting transfers between devices, gather(): lax.ppermute(value, ('x', 'rest'), [(i, i ^ k) for i in range(n_wide)])  11.3 us
    ppermute x7, waiting for transfers between devices, gather(): lax.ppermute(value, ('x', 'rest'), [(i, i ^ k) for i in range(n_wide)])  6.05 us
    ppermute x1, waiting for transfers between devices, shards(): from_half = lax.ppermute(to_half, 'half', [(0, 1), (1, 0)])  3.55 us
    ppermute x1, waiting for transfers between devices, shards(): lax.ppermute(to_both, ('x', 'half'), [(i, i ^ 3) for i in range(4)])  3.07 us
    ppermute x1, starting transfers between devices, shards(): from_half = lax.ppermute(to_half, 'half', [(0, 1), (1, 0)])  2.65 us
    ppermute x8, starting transfers between devices, gather(): there.append(lax.ppermute(value, 'core', [(0, 1), (1, 0)]))  1.6 us
    pallas_call x1, Pallas kernels, shards(): pl.pallas_call(functools.partial(prep_kernel, apart), out_shape=(array(sh...  1.34 us
    pallas_call x1, Pallas kernels, shards(): pl.pallas_call(functools.partial(finish_kernel, total), out_shape=jax.Sha...  1.04 us
  transfers between devices with their start and end apart: 18, of which 9 were waited for; matrix products, arithmetic and copies ran while one was open for 0% of the time, Pallas kernels for 1%

profile of v3, /device:TPU:0, one launch (start us, length us, event | category | flops | bytes accessed | tf_op | source)
XLA Modules:
  0.0 34.5 jit_solution(13004850687098420280)
XLA Ops:
  0.0 1.3 %prep.1 = (bf16[1,200,256]{2,1,0:T(8,128)(2,1)S(1)}, bf16[1,200,256]{2,1,0:T(8,128)(2,1)S(1)}, bf16[1,200,256]{2,1,0:T(8,128)(2,1)S(1)}, bf16[1,200,256]{2,1,0:T...) custom-call(s32[16]{0:T(128)} %assignment.1, ...), custom_call_target="tpu_custom_call" | custom-call | tf_op jit(solution)/shard_map/prep/pallas_call | solution.py:202
  1.3 5.0 %collective-permute-start = (bf16[1,200,256]{2,1,0:T(8,128)(2,1)S(1)}, bf16[1,200,256]{2,1,0:T(8,128)(2,1)S(1)}, u32[]{:S(2)}, u32[]{:S(2)}) collective-permute-start(bf16[1,200,256]{2,1,0:T(8,128)(2,1)S(1)} %get-tuple-element.18), channel_id=1, source_target_pairs={{0,19},{1,18},{2,17},{3,16},{16,3},{17,2},{18,1},{19,0},{4,23},{5,... | collective-permute-start | bytes 307208 | tf_op jit(solution)/shard_map/ppermute | solution.py:175
  6.3 0.5 %collective-permute-start.1 = (bf16[1,200,256]{2,1,0:T(8,128)(2,1)S(1)}, bf16[1,200,256]{2,1,0:T(8,128)(2,1)S(1)}, u32[]{:S(2)}, u32[]{:S(2)}) collective-permute-start(bf16[1,200,256]{2,1,0:T(8,128)(2,1)S(1)} %get-tuple-element.19), channel_id=1, source_target_pairs={{0,17},{1,16},{2,19},{3,18},{16,1},{17,0},{18,3},{19,2},{4,21},{5,... | collective-permute-start | bytes 307208 | tf_op jit(solution)/shard_map/ppermute | solution.py:175
  6.8 1.4 %collective-permute-start.2 = (bf16[1,200,256]{2,1,0:T(8,128)(2,1)S(1)}, bf16[1,200,256]{2,1,0:T(8,128)(2,1)S(1)}, u32[]{:S(2)}, u32[]{:S(2)}) collective-permute-start(bf16[1,200,256]{2,1,0:T(8,128)(2,1)S(1)} %get-tuple-element.20), channel_id=1, source_target_pairs={{0,18},{1,19},{2,16},{3,17},{16,2},{17,3},{18,0},{19,1},{4,22},{5,... | collective-permute-start | bytes 307208 | tf_op jit(solution)/shard_map/ppermute | solution.py:175
  8.2 2.5 %collective-permute-start.3 = (bf16[1,200,256]{2,1,0:T(8,128)(2,1)S(1)}, bf16[1,200,256]{2,1,0:T(8,128)(2,1)S(1)}, u32[]{:S(2)}, u32[]{:S(2)}) collective-permute-start(bf16[1,200,256]{2,1,0:T(8,128)(2,1)S(1)} %get-tuple-element.21), channel_id=1, source_target_pairs={{0,3},{1,2},{2,1},{3,0},{16,19},{17,18},{18,17},{19,16},{4,7},{5,6... | collective-permute-start | bytes 307208 | tf_op jit(solution)/shard_map/ppermute | solution.py:175
  10.7 0.5 %collective-permute-start.4 = (bf16[1,200,256]{2,1,0:T(8,128)(2,1)S(1)}, bf16[1,200,256]{2,1,0:T(8,128)(2,1)S(1)}, u32[]{:S(2)}, u32[]{:S(2)}) collective-permute-start(bf16[1,200,256]{2,1,0:T(8,128)(2,1)S(1)} %get-tuple-element.22), channel_id=1, source_target_pairs={{0,16},{1,17},{2,18},{3,19},{16,0},{17,1},{18,2},{19,3},{4,20},{5,... | collective-permute-start | bytes 307208 | tf_op jit(solution)/shard_map/ppermute | solution.py:175
  11.3 0.0 collective-permute-done.refs_1_
  11.3 0.5 %collective-permute-start.5 = (bf16[1,200,256]{2,1,0:T(8,128)(2,1)S(1)}, bf16[1,200,256]{2,1,0:T(8,128)(2,1)S(1)}, u32[]{:S(2)}, u32[]{:S(2)}) collective-permute-start(bf16[1,200,256]{2,1,0:T(8,128)(2,1)S(1)} %get-tuple-element.23), channel_id=1, source_target_pairs={{0,2},{1,3},{2,0},{3,1},{16,18},{17,19},{18,16},{19,17},{4,6},{5,7... | collective-permute-start | bytes 307208 | tf_op jit(solution)/shard_map/ppermute | solution.py:175
  11.7 2.9 %collective-permute-done.1.refs_2_ = bf16[1,200,256]{2,1,0:T(8,128)(2,1)S(1)} collective-permute-done((bf16[1,200,256]{2,1,0:T(8,128)(2,1)S(1)}, bf16[1,200,256]{2,1,0:T(8,128)(2,1)S(1)}, u32[]{:S(2)}, u32[]{:S(2)}) %collective-permute-start.1) | collective-permute-done | bytes 102432 | tf_op jit(solution)/shard_map/ppermute | solution.py:175
  14.6 0.9 %collective-permute-start.6 = (bf16[1,200,256]{2,1,0:T(8,128)(2,1)S(1)}, bf16[1,200,256]{2,1,0:T(8,128)(2,1)S(1)}, u32[]{:S(2)}, u32[]{:S(2)}) collective-permute-start(bf16[1,200,256]{2,1,0:T(8,128)(2,1)S(1)} %get-tuple-element.24), channel_id=1, source_target_pairs={{0,1},{1,0},{2,3},{3,2},{16,17},{17,16},{18,19},{19,18},{4,5},{5,4... | collective-permute-start | bytes 307208 | tf_op jit(solution)/shard_map/ppermute | solution.py:175
  15.5 0.0 collective-permute-start.7
  15.5 0.6 %collective-permute-done.3.refs_4_ = bf16[1,200,256]{2,1,0:T(8,128)(2,1)S(1)} collective-permute-done((bf16[1,200,256]{2,1,0:T(8,128)(2,1)S(1)}, bf16[1,200,256]{2,1,0:T(8,128)(2,1)S(1)}, u32[]{:S(2)}, u32[]{:S(2)}) %collective-permute-start.3) | collective-permute-done | bytes 102432 | tf_op jit(solution)/shard_map/ppermute | solution.py:175
  16.1 0.0 collective-permute-start.8
  16.1 0.0 collective-permute-done.4.refs_5_
  16.1 0.5 %collective-permute-start.9 = (bf16[1,200,256]{2,1,0:T(8,128)(2,1)S(1)}, bf16[1,200,256]{2,1,0:T(8,128)(2,1)S(1)}, u32[]{:S(2)}, u32[]{:S(2)}) collective-permute-start(bf16[1,200,256]{2,1,0:T(8,128)(2,1)S(1)} %collective-permute-done.1.refs_2_), channel_id=1, source_target_pairs={{0,8},{8,0},{1,9},{9,1},{2,10},{10,2},{3,11},{11,3},{4,12},{12,4},... | collective-permute-start | bytes 307208 | tf_op jit(solution)/shard_map/ppermute | solution.py:178
  16.6 0.1 collective-permute-start.10
  16.7 2.5 %collective-permute-done.6.refs_7_ = bf16[1,200,256]{2,1,0:T(8,128)(2,1)S(1)} collective-permute-done((bf16[1,200,256]{2,1,0:T(8,128)(2,1)S(1)}, bf16[1,200,256]{2,1,0:T(8,128)(2,1)S(1)}, u32[]{:S(2)}, u32[]{:S(2)}) %collective-permute-start.6) | collective-permute-done | bytes 102432 | tf_op jit(solution)/shard_map/ppermute | solution.py:175
  19.3 0.5 %collective-permute-start.12 = (bf16[1,200,256]{2,1,0:T(8,128)(2,1)S(1)}, bf16[1,200,256]{2,1,0:T(8,128)(2,1)S(1)}, u32[]{:S(2)}, u32[]{:S(2)}) collective-permute-start(bf16[1,200,256]{2,1,0:T(8,128)(2,1)S(1)} %collective-permute-done.4.refs_5_), channel_id=1, source_target_pairs={{0,8},{8,0},{1,9},{9,1},{2,10},{10,2},{3,11},{11,3},{4,12},{12,4},... | collective-permute-start | bytes 307208 | tf_op jit(solution)/shard_map/ppermute | solution.py:178
  19.8 0.1 collective-permute-start.13
  19.8 0.4 %collective-permute-start.14 = (bf16[1,200,256]{2,1,0:T(8,128)(2,1)S(1)}, bf16[1,200,256]{2,1,0:T(8,128)(2,1)S(1)}, u32[]{:S(2)}, u32[]{:S(2)}) collective-permute-start(bf16[1,200,256]{2,1,0:T(8,128)(2,1)S(1)} %collective-permute-done.6.refs_7_), channel_id=1, source_target_pairs={{0,8},{8,0},{1,9},{9,1},{2,10},{10,2},{3,11},{11,3},{4,12},{12,4},... | collective-permute-start | bytes 307208 | tf_op jit(solution)/shard_map/ppermute | solution.py:178
  20.3 0.3 collective-permute-done.11.refs_12_
  20.6 0.2 collective-permute-done.12.refs_13_
  20.7 0.4 %collective-permute-done.13.refs_14_ = bf16[1,200,256]{2,1,0:T(8,128)(2,1)S(1)} collective-permute-done((bf16[1,200,256]{2,1,0:T(8,128)(2,1)S(1)}, bf16[1,200,256]{2,1,0:T(8,128)(2,1)S(1)}, u32[]{:S(2)}, u32[]{:S(2)}) %collective-permute-start.13) | collective-permute-done | bytes 102432 | tf_op jit(solution)/shard_map/ppermute | solution.py:178
  21.1 0.2 collective-permute-done.14.refs_15_
  21.2 0.5 %gram.2 = (f32[136,256]{1,0:T(8,128)S(1)}, f32[136,256]{1,0:T(8,128)S(1)}) custom-call(s32[1]{0:T(128)} %bitcast.place, bf16[1,200,256]{2,1,0:T(8,128)(2,1)S(1)} %get-tuple-element.17.refs_0_, bf16[1,200,256]{2,1,0:T(8,128)(2,1)S(1)} %collective-permute-done.refs_1_, bf16[1,200,256]{2,1,0:T(8,128)(2,1)S(1)} %collective-permute-done.1.refs_2_, ...), custom_call_target="tpu_custom_call" | custom-call | tf_op jit(solution)/shard_map/gram/pallas_call | solution.py:218
  21.8 1.0 %collective-permute-start.15 = (f32[136,256]{1,0:T(8,128)S(1)}, f32[136,256]{1,0:T(8,128)S(1)}, u32[]{:S(2)}, u32[]{:S(2)}) collective-permute-start(f32[136,256]{1,0:T(8,128)S(1)} %get-tuple-element.26), channel_id=1, source_target_pairs={{0,16},{16,0},{1,17},{17,1},{2,18},{18,2},{3,19},{19,3},{4,20},{20... | collective-permute-start | bytes 417800 | tf_op jit(solution)/shard_map/ppermute | solution.py:234
  22.8 0.5 %gram.3 = (bf16[136,256]{1,0:T(8,128)(2,1)S(1)}, bf16[136,256]{1,0:T(8,128)(2,1)S(1)}) custom-call(s32[1]{0:T(128)} %bitcast.place, bf16[1,200,256]{2,1,0:T(8,128)(2,1)S(1)} %get-tuple-element.17.refs_0_, bf16[1,200,256]{2,1,0:T(8,128)(2,1)S(1)} %collective-permute-done.refs_1_, bf16[1,200,256]{2,1,0:T(8,128)(2,1)S(1)} %collective-permute-done.1.refs_2_, ...), custom_call_target="tpu_custom_call" | custom-call | tf_op jit(solution)/shard_map/gram/pallas_call | solution.py:218
  23.3 2.7 %collective-permute-start.16 = (bf16[136,256]{1,0:T(8,128)(2,1)S(1)}, bf16[136,256]{1,0:T(8,128)(2,1)S(1)}, u32[]{:S(2)}, u32[]{:S(2)}) collective-permute-start(bf16[136,256]{1,0:T(8,128)(2,1)S(1)} %get-tuple-element.27), channel_id=1, source_target_pairs={{0,4},{4,0},{1,5},{5,1},{2,6},{6,2},{3,7},{7,3},{8,12},{12,8},{9,1... | collective-permute-start | bytes 208904 | tf_op jit(solution)/shard_map/ppermute | solution.py:232
  25.9 0.9 %collective-permute-start.17 = (bf16[136,256]{1,0:T(8,128)(2,1)S(1)}, bf16[136,256]{1,0:T(8,128)(2,1)S(1)}, u32[]{:S(2)}, u32[]{:S(2)}) collective-permute-start(bf16[136,256]{1,0:T(8,128)(2,1)S(1)} %get-tuple-element.28), channel_id=1, source_target_pairs={{0,20},{4,16},{16,4},{20,0},{1,21},{5,17},{17,5},{21,1},{2,22},{6,... | collective-permute-start | bytes 208904 | tf_op jit(solution)/shard_map/ppermute | solution.py:231
  26.8 3.6 %collective-permute-done.16.half_ref = bf16[136,256]{1,0:T(8,128)(2,1)S(1)} collective-permute-done((bf16[136,256]{1,0:T(8,128)(2,1)S(1)}, bf16[136,256]{1,0:T(8,128)(2,1)S(1)}, u32[]{:S(2)}, u32[]{:S(2)}) %collective-permute-start.16) | collective-permute-done | bytes 69664 | tf_op jit(solution)/shard_map/ppermute | solution.py:232
  30.4 3.1 %collective-permute-done.17.both_ref = bf16[136,256]{1,0:T(8,128)(2,1)S(1)} collective-permute-done((bf16[136,256]{1,0:T(8,128)(2,1)S(1)}, bf16[136,256]{1,0:T(8,128)(2,1)S(1)}, u32[]{:S(2)}, u32[]{:S(2)}) %collective-permute-start.17) | collective-permute-done | bytes 69664 | tf_op jit(solution)/shard_map/ppermute | solution.py:231
  33.4 1.0 %finish.1 = f32[2,2,64,256]{3,2,1,0:T(8,128)} custom-call(s32[1]{0:T(128)} %bitcast.place, s32[1]{0:T(128)} %bitcast.1.nearer, f32[136,256]{1,0:T(8,128)S(1)} %get-tuple-element.25.keep_ref, f32[136,256]{1,0:T(8,128)S(1)} %collective-permute-done.15.x_ref, bf16[136,256]{1,0:T(8,128)(2,1)S(1)} %collective-permute-done.16.half_ref, ...), custom_call_target="tpu_custom_call" | custom-call | tf_op jit(solution)/shard_map/finish/pallas_call | solution.py:235
  (8 shorter events, 0.0 us)
Async XLA Ops:
  1.3 9.9 %collective-permute-start = (bf16[1,200,256]{2,1,0:T(8,128)(2,1)S(1)}, bf16[1,200,256]{2,1,0:T(8,128)(2,1)S(1)}, u32[]{:S(2)}, u32[]{:S(2)}) collective-permute-start(bf16[1,200,256]{2,1,0:T(8,128)(2,1)S(1)} %get-tuple-element.18), channel_id=1, source_target_pairs={{0,19},{1,18},{2,17},{3,16},{16,3},{17,2},{18,1},{19,0},{4,23},{5,... | collective-permute-start | bytes 307208 | tf_op jit(solution)/shard_map/ppermute | solution.py:175
  6.3 8.2 %collective-permute-start.1 = (bf16[1,200,256]{2,1,0:T(8,128)(2,1)S(1)}, bf16[1,200,256]{2,1,0:T(8,128)(2,1)S(1)}, u32[]{:S(2)}, u32[]{:S(2)}) collective-permute-start(bf16[1,200,256]{2,1,0:T(8,128)(2,1)S(1)} %get-tuple-element.19), channel_id=1, source_target_pairs={{0,17},{1,16},{2,19},{3,18},{16,1},{17,0},{18,3},{19,2},{4,21},{5,... | collective-permute-start | bytes 307208 | tf_op jit(solution)/shard_map/ppermute | solution.py:175
  6.8 8.7 %collective-permute-start.2 = (bf16[1,200,256]{2,1,0:T(8,128)(2,1)S(1)}, bf16[1,200,256]{2,1,0:T(8,128)(2,1)S(1)}, u32[]{:S(2)}, u32[]{:S(2)}) collective-permute-start(bf16[1,200,256]{2,1,0:T(8,128)(2,1)S(1)} %get-tuple-element.20), channel_id=1, source_target_pairs={{0,18},{1,19},{2,16},{3,17},{16,2},{17,3},{18,0},{19,1},{4,22},{5,... | collective-permute-start | bytes 307208 | tf_op jit(solution)/shard_map/ppermute | solution.py:175
  8.2 7.9 %collective-permute-start.3 = (bf16[1,200,256]{2,1,0:T(8,128)(2,1)S(1)}, bf16[1,200,256]{2,1,0:T(8,128)(2,1)S(1)}, u32[]{:S(2)}, u32[]{:S(2)}) collective-permute-start(bf16[1,200,256]{2,1,0:T(8,128)(2,1)S(1)} %get-tuple-element.21), channel_id=1, source_target_pairs={{0,3},{1,2},{2,1},{3,0},{16,19},{17,18},{18,17},{19,16},{4,7},{5,6... | collective-permute-start | bytes 307208 | tf_op jit(solution)/shard_map/ppermute | solution.py:175
  10.7 5.4 %collective-permute-start.4 = (bf16[1,200,256]{2,1,0:T(8,128)(2,1)S(1)}, bf16[1,200,256]{2,1,0:T(8,128)(2,1)S(1)}, u32[]{:S(2)}, u32[]{:S(2)}) collective-permute-start(bf16[1,200,256]{2,1,0:T(8,128)(2,1)S(1)} %get-tuple-element.22), channel_id=1, source_target_pairs={{0,16},{1,17},{2,18},{3,19},{16,0},{17,1},{18,2},{19,3},{4,20},{5,... | collective-permute-start | bytes 307208 | tf_op jit(solution)/shard_map/ppermute | solution.py:175
  11.3 5.4 %collective-permute-start.5 = (bf16[1,200,256]{2,1,0:T(8,128)(2,1)S(1)}, bf16[1,200,256]{2,1,0:T(8,128)(2,1)S(1)}, u32[]{:S(2)}, u32[]{:S(2)}) collective-permute-start(bf16[1,200,256]{2,1,0:T(8,128)(2,1)S(1)} %get-tuple-element.23), channel_id=1, source_target_pairs={{0,2},{1,3},{2,0},{3,1},{16,18},{17,19},{18,16},{19,17},{4,6},{5,7... | collective-permute-start | bytes 307208 | tf_op jit(solution)/shard_map/ppermute | solution.py:175
  14.6 4.7 %collective-permute-start.6 = (bf16[1,200,256]{2,1,0:T(8,128)(2,1)S(1)}, bf16[1,200,256]{2,1,0:T(8,128)(2,1)S(1)}, u32[]{:S(2)}, u32[]{:S(2)}) collective-permute-start(bf16[1,200,256]{2,1,0:T(8,128)(2,1)S(1)} %get-tuple-element.24), channel_id=1, source_target_pairs={{0,1},{1,0},{2,3},{3,2},{16,17},{17,16},{18,19},{19,18},{4,5},{5,4... | collective-permute-start | bytes 307208 | tf_op jit(solution)/shard_map/ppermute | solution.py:175
  15.5 3.8 %collective-permute-start.7 = (bf16[1,200,256]{2,1,0:T(8,128)(2,1)S(1)}, bf16[1,200,256]{2,1,0:T(8,128)(2,1)S(1)}, u32[]{:S(2)}, u32[]{:S(2)}) collective-permute-start(bf16[1,200,256]{2,1,0:T(8,128)(2,1)S(1)} %get-tuple-element.17.refs_0_), channel_id=1, source_target_pairs={{0,8},{8,0},{1,9},{9,1},{2,10},{10,2},{3,11},{11,3},{4,12},{12,4},... | collective-permute-start | bytes 307208 | tf_op jit(solution)/shard_map/ppermute | solution.py:178
  16.1 3.7 %collective-permute-start.8 = (bf16[1,200,256]{2,1,0:T(8,128)(2,1)S(1)}, bf16[1,200,256]{2,1,0:T(8,128)(2,1)S(1)}, u32[]{:S(2)}, u32[]{:S(2)}) collective-permute-start(bf16[1,200,256]{2,1,0:T(8,128)(2,1)S(1)} %collective-permute-done.refs_1_), channel_id=1, source_target_pairs={{0,8},{8,0},{1,9},{9,1},{2,10},{10,2},{3,11},{11,3},{4,12},{12,4},... | collective-permute-start | bytes 307208 | tf_op jit(solution)/shard_map/ppermute | solution.py:178
  16.1 3.7 %collective-permute-start.9 = (bf16[1,200,256]{2,1,0:T(8,128)(2,1)S(1)}, bf16[1,200,256]{2,1,0:T(8,128)(2,1)S(1)}, u32[]{:S(2)}, u32[]{:S(2)}) collective-permute-start(bf16[1,200,256]{2,1,0:T(8,128)(2,1)S(1)} %collective-permute-done.1.refs_2_), channel_id=1, source_target_pairs={{0,8},{8,0},{1,9},{9,1},{2,10},{10,2},{3,11},{11,3},{4,12},{12,4},... | collective-permute-start | bytes 307208 | tf_op jit(solution)/shard_map/ppermute | solution.py:178
  16.6 3.7 %collective-permute-start.10 = (bf16[1,200,256]{2,1,0:T(8,128)(2,1)S(1)}, bf16[1,200,256]{2,1,0:T(8,128)(2,1)S(1)}, u32[]{:S(2)}, u32[]{:S(2)}) collective-permute-start(bf16[1,200,256]{2,1,0:T(8,128)(2,1)S(1)} %collective-permute-done.2.refs_3_), channel_id=1, source_target_pairs={{0,8},{8,0},{1,9},{9,1},{2,10},{10,2},{3,11},{11,3},{4,12},{12,4},... | collective-permute-start | bytes 307208 | tf_op jit(solution)/shard_map/ppermute | solution.py:178
  19.2 1.3 %collective-permute-start.11 = (bf16[1,200,256]{2,1,0:T(8,128)(2,1)S(1)}, bf16[1,200,256]{2,1,0:T(8,128)(2,1)S(1)}, u32[]{:S(2)}, u32[]{:S(2)}) collective-permute-start(bf16[1,200,256]{2,1,0:T(8,128)(2,1)S(1)} %collective-permute-done.3.refs_4_), channel_id=1, source_target_pairs={{0,8},{8,0},{1,9},{9,1},{2,10},{10,2},{3,11},{11,3},{4,12},{12,4},... | collective-permute-start | bytes 307208 | tf_op jit(solution)/shard_map/ppermute | solution.py:178
  19.3 1.5 %collective-permute-start.12 = (bf16[1,200,256]{2,1,0:T(8,128)(2,1)S(1)}, bf16[1,200,256]{2,1,0:T(8,128)(2,1)S(1)}, u32[]{:S(2)}, u32[]{:S(2)}) collective-permute-start(bf16[1,200,256]{2,1,0:T(8,128)(2,1)S(1)} %collective-permute-done.4.refs_5_), channel_id=1, source_target_pairs={{0,8},{8,0},{1,9},{9,1},{2,10},{10,2},{3,11},{11,3},{4,12},{12,4},... | collective-permute-start | bytes 307208 | tf_op jit(solution)/shard_map/ppermute | solution.py:178
  19.8 1.3 %collective-permute-start.13 = (bf16[1,200,256]{2,1,0:T(8,128)(2,1)S(1)}, bf16[1,200,256]{2,1,0:T(8,128)(2,1)S(1)}, u32[]{:S(2)}, u32[]{:S(2)}) collective-permute-start(bf16[1,200,256]{2,1,0:T(8,128)(2,1)S(1)} %collective-permute-done.5.refs_6_), channel_id=1, source_target_pairs={{0,8},{8,0},{1,9},{9,1},{2,10},{10,2},{3,11},{11,3},{4,12},{12,4},... | collective-permute-start | bytes 307208 | tf_op jit(solution)/shard_map/ppermute | solution.py:178
  19.8 1.4 %collective-permute-start.14 = (bf16[1,200,256]{2,1,0:T(8,128)(2,1)S(1)}, bf16[1,200,256]{2,1,0:T(8,128)(2,1)S(1)}, u32[]{:S(2)}, u32[]{:S(2)}) collective-permute-start(bf16[1,200,256]{2,1,0:T(8,128)(2,1)S(1)} %collective-permute-done.6.refs_7_), channel_id=1, source_target_pairs={{0,8},{8,0},{1,9},{9,1},{2,10},{10,2},{3,11},{11,3},{4,12},{12,4},... | collective-permute-start | bytes 307208 | tf_op jit(solution)/shard_map/ppermute | solution.py:178
  21.8 11.7 %collective-permute-start.15 = (f32[136,256]{1,0:T(8,128)S(1)}, f32[136,256]{1,0:T(8,128)S(1)}, u32[]{:S(2)}, u32[]{:S(2)}) collective-permute-start(f32[136,256]{1,0:T(8,128)S(1)} %get-tuple-element.26), channel_id=1, source_target_pairs={{0,16},{16,0},{1,17},{17,1},{2,18},{18,2},{3,19},{19,3},{4,20},{20... | collective-permute-start | bytes 417800 | tf_op jit(solution)/shard_map/ppermute | solution.py:234
  23.3 7.1 %collective-permute-start.16 = (bf16[136,256]{1,0:T(8,128)(2,1)S(1)}, bf16[136,256]{1,0:T(8,128)(2,1)S(1)}, u32[]{:S(2)}, u32[]{:S(2)}) collective-permute-start(bf16[136,256]{1,0:T(8,128)(2,1)S(1)} %get-tuple-element.27), channel_id=1, source_target_pairs={{0,4},{4,0},{1,5},{5,1},{2,6},{6,2},{3,7},{7,3},{8,12},{12,8},{9,1... | collective-permute-start | bytes 208904 | tf_op jit(solution)/shard_map/ppermute | solution.py:232
  25.9 7.5 %collective-permute-start.17 = (bf16[136,256]{1,0:T(8,128)(2,1)S(1)}, bf16[136,256]{1,0:T(8,128)(2,1)S(1)}, u32[]{:S(2)}, u32[]{:S(2)}) collective-permute-start(bf16[136,256]{1,0:T(8,128)(2,1)S(1)} %get-tuple-element.28), channel_id=1, source_target_pairs={{0,20},{4,16},{16,4},{20,0},{1,21},{5,17},{17,5},{21,1},{2,22},{6,... | collective-permute-start | bytes 208904 | tf_op jit(solution)/shard_map/ppermute | solution.py:231

commit v4 on v3

--- a/solution.py
+++ b/solution.py
@@ -97,11 +97,11 @@
         means.append(mean)
         squares.append(square)
         high, low = split_two(shift)
-        scale = cells // 8
+        sums_high, sums_low = split_two(sums)
         if k == 0:
-            extra = [8.0 * high, 8.0 * low, 8.0 * high, sums * 0.125]
+            extra = [high, low, high, sums_high, sums_low, sums_high]
         else:
-            extra = [scale * high, scale * high, scale * low, sums * (-8.0 / cells)]
+            extra = [cells * v for v in (high, high, low)] + [v * (-1.0 / cells) for v in (sums_high, sums_high, sums_low)]
         operands.append(jnp.concatenate([data, jnp.concatenate(extra, axis=0).astype(BF16)], axis=0))
     stats = jnp.concatenate(means + squares + [jnp.zeros((STATS - 2 * EACH, panel), F32)], axis=0)
     high, low = split_two(stats)

time: 34.6 us -> 34.6 us (level)
  transfers between devices with their start and end apart: 18 -> 18, of which waited for: 9 -> 9; matrix products, arithmetic and copies ran while one was open for 0% -> 0% of each run, Pallas kernels for 1% -> 2%
where the time goes in v4:
time: 34.6 us; the launch traced here: 34.5 us
  starting transfers between devices  17.4 us (50%)
  waiting for transfers between devices  13.6 us (39%)
  Pallas kernels  3.42 us (10%)
    ppermute x7, starting transfers between devices, gather(): lax.ppermute(value, ('x', 'rest'), [(i, i ^ k) for i in range(n_wide)])  11.3 us
    ppermute x7, waiting for transfers between devices, gather(): lax.ppermute(value, ('x', 'rest'), [(i, i ^ k) for i in range(n_wide)])  6.05 us
    ppermute x1, waiting for transfers between devices, shards(): from_half = lax.ppermute(to_half, 'half', [(0, 1), (1, 0)])  3.56 us
    ppermute x1, waiting for transfers between devices, shards(): lax.ppermute(to_both, ('x', 'half'), [(i, i ^ 3) for i in range(4)])  3.06 us
    ppermute x1, starting transfers between devices, shards(): from_half = lax.ppermute(to_half, 'half', [(0, 1), (1, 0)])  2.65 us
    ppermute x8, starting transfers between devices, gather(): there.append(lax.ppermute(value, 'core', [(0, 1), (1, 0)]))  1.6 us
    pallas_call x1, Pallas kernels, shards(): pl.pallas_call(functools.partial(prep_kernel, apart), out_shape=(array(sh...  1.34 us
    pallas_call x2, Pallas kernels, gram(): pl.pallas_call(functools.partial(gram_kernel, cells, which), out_shape=(a...  1.05 us
  transfers between devices with their start and end apart: 18, of which 9 were waited for; matrix products, arithmetic and copies ran while one was open for 0% of the time, Pallas kernels for 2%

profile of v4, /device:TPU:0, one launch (start us, length us, event | category | flops | bytes accessed | tf_op | source)
XLA Modules:
  0.0 34.5 jit_solution(3696824866884578503)
XLA Ops:
  0.0 1.3 %prep.1 = (bf16[1,200,256]{2,1,0:T(8,128)(2,1)S(1)}, bf16[1,200,256]{2,1,0:T(8,128)(2,1)S(1)}, bf16[1,200,256]{2,1,0:T(8,128)(2,1)S(1)}, bf16[1,200,256]{2,1,0:T...) custom-call(s32[16]{0:T(128)} %assignment.1, ...), custom_call_target="tpu_custom_call" | custom-call | tf_op jit(solution)/shard_map/prep/pallas_call | solution.py:202
  1.3 5.0 %collective-permute-start = (bf16[1,200,256]{2,1,0:T(8,128)(2,1)S(1)}, bf16[1,200,256]{2,1,0:T(8,128)(2,1)S(1)}, u32[]{:S(2)}, u32[]{:S(2)}) collective-permute-start(bf16[1,200,256]{2,1,0:T(8,128)(2,1)S(1)} %get-tuple-element.18), channel_id=1, source_target_pairs={{0,19},{1,18},{2,17},{3,16},{16,3},{17,2},{18,1},{19,0},{4,23},{5,... | collective-permute-start | bytes 307208 | tf_op jit(solution)/shard_map/ppermute | solution.py:175
  6.3 0.5 %collective-permute-start.1 = (bf16[1,200,256]{2,1,0:T(8,128)(2,1)S(1)}, bf16[1,200,256]{2,1,0:T(8,128)(2,1)S(1)}, u32[]{:S(2)}, u32[]{:S(2)}) collective-permute-start(bf16[1,200,256]{2,1,0:T(8,128)(2,1)S(1)} %get-tuple-element.19), channel_id=1, source_target_pairs={{0,17},{1,16},{2,19},{3,18},{16,1},{17,0},{18,3},{19,2},{4,21},{5,... | collective-permute-start | bytes 307208 | tf_op jit(solution)/shard_map/ppermute | solution.py:175
  6.8 1.4 %collective-permute-start.2 = (bf16[1,200,256]{2,1,0:T(8,128)(2,1)S(1)}, bf16[1,200,256]{2,1,0:T(8,128)(2,1)S(1)}, u32[]{:S(2)}, u32[]{:S(2)}) collective-permute-start(bf16[1,200,256]{2,1,0:T(8,128)(2,1)S(1)} %get-tuple-element.20), channel_id=1, source_target_pairs={{0,18},{1,19},{2,16},{3,17},{16,2},{17,3},{18,0},{19,1},{4,22},{5,... | collective-permute-start | bytes 307208 | tf_op jit(solution)/shard_map/ppermute | solution.py:175
  8.2 2.5 %collective-permute-start.3 = (bf16[1,200,256]{2,1,0:T(8,128)(2,1)S(1)}, bf16[1,200,256]{2,1,0:T(8,128)(2,1)S(1)}, u32[]{:S(2)}, u32[]{:S(2)}) collective-permute-start(bf16[1,200,256]{2,1,0:T(8,128)(2,1)S(1)} %get-tuple-element.21), channel_id=1, source_target_pairs={{0,3},{1,2},{2,1},{3,0},{16,19},{17,18},{18,17},{19,16},{4,7},{5,6... | collective-permute-start | bytes 307208 | tf_op jit(solution)/shard_map/ppermute | solution.py:175
  10.7 0.5 %collective-permute-start.4 = (bf16[1,200,256]{2,1,0:T(8,128)(2,1)S(1)}, bf16[1,200,256]{2,1,0:T(8,128)(2,1)S(1)}, u32[]{:S(2)}, u32[]{:S(2)}) collective-permute-start(bf16[1,200,256]{2,1,0:T(8,128)(2,1)S(1)} %get-tuple-element.22), channel_id=1, source_target_pairs={{0,16},{1,17},{2,18},{3,19},{16,0},{17,1},{18,2},{19,3},{4,20},{5,... | collective-permute-start | bytes 307208 | tf_op jit(solution)/shard_map/ppermute | solution.py:175
  11.3 0.0 collective-permute-done.refs_1_
  11.3 0.5 %collective-permute-start.5 = (bf16[1,200,256]{2,1,0:T(8,128)(2,1)S(1)}, bf16[1,200,256]{2,1,0:T(8,128)(2,1)S(1)}, u32[]{:S(2)}, u32[]{:S(2)}) collective-permute-start(bf16[1,200,256]{2,1,0:T(8,128)(2,1)S(1)} %get-tuple-element.23), channel_id=1, source_target_pairs={{0,2},{1,3},{2,0},{3,1},{16,18},{17,19},{18,16},{19,17},{4,6},{5,7... | collective-permute-start | bytes 307208 | tf_op jit(solution)/shard_map/ppermute | solution.py:175
  11.7 2.9 %collective-permute-done.1.refs_2_ = bf16[1,200,256]{2,1,0:T(8,128)(2,1)S(1)} collective-permute-done((bf16[1,200,256]{2,1,0:T(8,128)(2,1)S(1)}, bf16[1,200,256]{2,1,0:T(8,128)(2,1)S(1)}, u32[]{:S(2)}, u32[]{:S(2)}) %collective-permute-start.1) | collective-permute-done | bytes 102432 | tf_op jit(solution)/shard_map/ppermute | solution.py:175
  14.6 0.9 %collective-permute-start.6 = (bf16[1,200,256]{2,1,0:T(8,128)(2,1)S(1)}, bf16[1,200,256]{2,1,0:T(8,128)(2,1)S(1)}, u32[]{:S(2)}, u32[]{:S(2)}) collective-permute-start(bf16[1,200,256]{2,1,0:T(8,128)(2,1)S(1)} %get-tuple-element.24), channel_id=1, source_target_pairs={{0,1},{1,0},{2,3},{3,2},{16,17},{17,16},{18,19},{19,18},{4,5},{5,4... | collective-permute-start | bytes 307208 | tf_op jit(solution)/shard_map/ppermute | solution.py:175
  15.5 0.0 collective-permute-start.7
  15.5 0.6 %collective-permute-done.3.refs_4_ = bf16[1,200,256]{2,1,0:T(8,128)(2,1)S(1)} collective-permute-done((bf16[1,200,256]{2,1,0:T(8,128)(2,1)S(1)}, bf16[1,200,256]{2,1,0:T(8,128)(2,1)S(1)}, u32[]{:S(2)}, u32[]{:S(2)}) %collective-permute-start.3) | collective-permute-done | bytes 102432 | tf_op jit(solution)/shard_map/ppermute | solution.py:175
  16.1 0.0 collective-permute-start.8
  16.1 0.0 collective-permute-done.4.refs_5_
  16.1 0.5 %collective-permute-start.9 = (bf16[1,200,256]{2,1,0:T(8,128)(2,1)S(1)}, bf16[1,200,256]{2,1,0:T(8,128)(2,1)S(1)}, u32[]{:S(2)}, u32[]{:S(2)}) collective-permute-start(bf16[1,200,256]{2,1,0:T(8,128)(2,1)S(1)} %collective-permute-done.1.refs_2_), channel_id=1, source_target_pairs={{0,8},{8,0},{1,9},{9,1},{2,10},{10,2},{3,11},{11,3},{4,12},{12,4},... | collective-permute-start | bytes 307208 | tf_op jit(solution)/shard_map/ppermute | solution.py:178
  16.6 0.1 collective-permute-start.10
  16.7 2.5 %collective-permute-done.6.refs_7_ = bf16[1,200,256]{2,1,0:T(8,128)(2,1)S(1)} collective-permute-done((bf16[1,200,256]{2,1,0:T(8,128)(2,1)S(1)}, bf16[1,200,256]{2,1,0:T(8,128)(2,1)S(1)}, u32[]{:S(2)}, u32[]{:S(2)}) %collective-permute-start.6) | collective-permute-done | bytes 102432 | tf_op jit(solution)/shard_map/ppermute | solution.py:175
  19.3 0.5 %collective-permute-start.12 = (bf16[1,200,256]{2,1,0:T(8,128)(2,1)S(1)}, bf16[1,200,256]{2,1,0:T(8,128)(2,1)S(1)}, u32[]{:S(2)}, u32[]{:S(2)}) collective-permute-start(bf16[1,200,256]{2,1,0:T(8,128)(2,1)S(1)} %collective-permute-done.4.refs_5_), channel_id=1, source_target_pairs={{0,8},{8,0},{1,9},{9,1},{2,10},{10,2},{3,11},{11,3},{4,12},{12,4},... | collective-permute-start | bytes 307208 | tf_op jit(solution)/shard_map/ppermute | solution.py:178
  19.8 0.1 collective-permute-start.13
  19.8 0.4 %collective-permute-start.14 = (bf16[1,200,256]{2,1,0:T(8,128)(2,1)S(1)}, bf16[1,200,256]{2,1,0:T(8,128)(2,1)S(1)}, u32[]{:S(2)}, u32[]{:S(2)}) collective-permute-start(bf16[1,200,256]{2,1,0:T(8,128)(2,1)S(1)} %collective-permute-done.6.refs_7_), channel_id=1, source_target_pairs={{0,8},{8,0},{1,9},{9,1},{2,10},{10,2},{3,11},{11,3},{4,12},{12,4},... | collective-permute-start | bytes 307208 | tf_op jit(solution)/shard_map/ppermute | solution.py:178
  20.3 0.3 collective-permute-done.11.refs_12_
  20.6 0.2 collective-permute-done.12.refs_13_
  20.7 0.4 %collective-permute-done.13.refs_14_ = bf16[1,200,256]{2,1,0:T(8,128)(2,1)S(1)} collective-permute-done((bf16[1,200,256]{2,1,0:T(8,128)(2,1)S(1)}, bf16[1,200,256]{2,1,0:T(8,128)(2,1)S(1)}, u32[]{:S(2)}, u32[]{:S(2)}) %collective-permute-start.13) | collective-permute-done | bytes 102432 | tf_op jit(solution)/shard_map/ppermute | solution.py:178
  21.1 0.2 collective-permute-done.14.refs_15_
  21.2 0.5 %gram.2 = (f32[136,256]{1,0:T(8,128)S(1)}, f32[136,256]{1,0:T(8,128)S(1)}) custom-call(s32[1]{0:T(128)} %bitcast.place, bf16[1,200,256]{2,1,0:T(8,128)(2,1)S(1)} %get-tuple-element.17.refs_0_, bf16[1,200,256]{2,1,0:T(8,128)(2,1)S(1)} %collective-permute-done.refs_1_, bf16[1,200,256]{2,1,0:T(8,128)(2,1)S(1)} %collective-permute-done.1.refs_2_, ...), custom_call_target="tpu_custom_call" | custom-call | tf_op jit(solution)/shard_map/gram/pallas_call | solution.py:218
  21.8 1.0 %collective-permute-start.15 = (f32[136,256]{1,0:T(8,128)S(1)}, f32[136,256]{1,0:T(8,128)S(1)}, u32[]{:S(2)}, u32[]{:S(2)}) collective-permute-start(f32[136,256]{1,0:T(8,128)S(1)} %get-tuple-element.26), channel_id=1, source_target_pairs={{0,16},{16,0},{1,17},{17,1},{2,18},{18,2},{3,19},{19,3},{4,20},{20... | collective-permute-start | bytes 417800 | tf_op jit(solution)/shard_map/ppermute | solution.py:234
  22.8 0.5 %gram.3 = (bf16[136,256]{1,0:T(8,128)(2,1)S(1)}, bf16[136,256]{1,0:T(8,128)(2,1)S(1)}) custom-call(s32[1]{0:T(128)} %bitcast.place, bf16[1,200,256]{2,1,0:T(8,128)(2,1)S(1)} %get-tuple-element.17.refs_0_, bf16[1,200,256]{2,1,0:T(8,128)(2,1)S(1)} %collective-permute-done.refs_1_, bf16[1,200,256]{2,1,0:T(8,128)(2,1)S(1)} %collective-permute-done.1.refs_2_, ...), custom_call_target="tpu_custom_call" | custom-call | tf_op jit(solution)/shard_map/gram/pallas_call | solution.py:218
  23.3 2.6 %collective-permute-start.16 = (bf16[136,256]{1,0:T(8,128)(2,1)S(1)}, bf16[136,256]{1,0:T(8,128)(2,1)S(1)}, u32[]{:S(2)}, u32[]{:S(2)}) collective-permute-start(bf16[136,256]{1,0:T(8,128)(2,1)S(1)} %get-tuple-element.27), channel_id=1, source_target_pairs={{0,4},{4,0},{1,5},{5,1},{2,6},{6,2},{3,7},{7,3},{8,12},{12,8},{9,1... | collective-permute-start | bytes 208904 | tf_op jit(solution)/shard_map/ppermute | solution.py:232
  25.9 0.9 %collective-permute-start.17 = (bf16[136,256]{1,0:T(8,128)(2,1)S(1)}, bf16[136,256]{1,0:T(8,128)(2,1)S(1)}, u32[]{:S(2)}, u32[]{:S(2)}) collective-permute-start(bf16[136,256]{1,0:T(8,128)(2,1)S(1)} %get-tuple-element.28), channel_id=1, source_target_pairs={{0,20},{4,16},{16,4},{20,0},{1,21},{5,17},{17,5},{21,1},{2,22},{6,... | collective-permute-start | bytes 208904 | tf_op jit(solution)/shard_map/ppermute | solution.py:231
  26.8 3.6 %collective-permute-done.16.half_ref = bf16[136,256]{1,0:T(8,128)(2,1)S(1)} collective-permute-done((bf16[136,256]{1,0:T(8,128)(2,1)S(1)}, bf16[136,256]{1,0:T(8,128)(2,1)S(1)}, u32[]{:S(2)}, u32[]{:S(2)}) %collective-permute-start.16) | collective-permute-done | bytes 69664 | tf_op jit(solution)/shard_map/ppermute | solution.py:232
  30.4 3.1 %collective-permute-done.17.both_ref = bf16[136,256]{1,0:T(8,128)(2,1)S(1)} collective-permute-done((bf16[136,256]{1,0:T(8,128)(2,1)S(1)}, bf16[136,256]{1,0:T(8,128)(2,1)S(1)}, u32[]{:S(2)}, u32[]{:S(2)}) %collective-permute-start.17) | collective-permute-done | bytes 69664 | tf_op jit(solution)/shard_map/ppermute | solution.py:231
  33.4 1.0 %finish.1 = f32[2,2,64,256]{3,2,1,0:T(8,128)} custom-call(s32[1]{0:T(128)} %bitcast.place, s32[1]{0:T(128)} %bitcast.1.nearer, f32[136,256]{1,0:T(8,128)S(1)} %get-tuple-element.25.keep_ref, f32[136,256]{1,0:T(8,128)S(1)} %collective-permute-done.15.x_ref, bf16[136,256]{1,0:T(8,128)(2,1)S(1)} %collective-permute-done.16.half_ref, ...), custom_call_target="tpu_custom_call" | custom-call | tf_op jit(solution)/shard_map/finish/pallas_call | solution.py:235
  (8 shorter events, 0.0 us)
Async XLA Ops:
  1.3 9.9 %collective-permute-start = (bf16[1,200,256]{2,1,0:T(8,128)(2,1)S(1)}, bf16[1,200,256]{2,1,0:T(8,128)(2,1)S(1)}, u32[]{:S(2)}, u32[]{:S(2)}) collective-permute-start(bf16[1,200,256]{2,1,0:T(8,128)(2,1)S(1)} %get-tuple-element.18), channel_id=1, source_target_pairs={{0,19},{1,18},{2,17},{3,16},{16,3},{17,2},{18,1},{19,0},{4,23},{5,... | collective-permute-start | bytes 307208 | tf_op jit(solution)/shard_map/ppermute | solution.py:175
  6.3 8.2 %collective-permute-start.1 = (bf16[1,200,256]{2,1,0:T(8,128)(2,1)S(1)}, bf16[1,200,256]{2,1,0:T(8,128)(2,1)S(1)}, u32[]{:S(2)}, u32[]{:S(2)}) collective-permute-start(bf16[1,200,256]{2,1,0:T(8,128)(2,1)S(1)} %get-tuple-element.19), channel_id=1, source_target_pairs={{0,17},{1,16},{2,19},{3,18},{16,1},{17,0},{18,3},{19,2},{4,21},{5,... | collective-permute-start | bytes 307208 | tf_op jit(solution)/shard_map/ppermute | solution.py:175
  6.8 8.7 %collective-permute-start.2 = (bf16[1,200,256]{2,1,0:T(8,128)(2,1)S(1)}, bf16[1,200,256]{2,1,0:T(8,128)(2,1)S(1)}, u32[]{:S(2)}, u32[]{:S(2)}) collective-permute-start(bf16[1,200,256]{2,1,0:T(8,128)(2,1)S(1)} %get-tuple-element.20), channel_id=1, source_target_pairs={{0,18},{1,19},{2,16},{3,17},{16,2},{17,3},{18,0},{19,1},{4,22},{5,... | collective-permute-start | bytes 307208 | tf_op jit(solution)/shard_map/ppermute | solution.py:175
  8.2 7.9 %collective-permute-start.3 = (bf16[1,200,256]{2,1,0:T(8,128)(2,1)S(1)}, bf16[1,200,256]{2,1,0:T(8,128)(2,1)S(1)}, u32[]{:S(2)}, u32[]{:S(2)}) collective-permute-start(bf16[1,200,256]{2,1,0:T(8,128)(2,1)S(1)} %get-tuple-element.21), channel_id=1, source_target_pairs={{0,3},{1,2},{2,1},{3,0},{16,19},{17,18},{18,17},{19,16},{4,7},{5,6... | collective-permute-start | bytes 307208 | tf_op jit(solution)/shard_map/ppermute | solution.py:175
  10.7 5.4 %collective-permute-start.4 = (bf16[1,200,256]{2,1,0:T(8,128)(2,1)S(1)}, bf16[1,200,256]{2,1,0:T(8,128)(2,1)S(1)}, u32[]{:S(2)}, u32[]{:S(2)}) collective-permute-start(bf16[1,200,256]{2,1,0:T(8,128)(2,1)S(1)} %get-tuple-element.22), channel_id=1, source_target_pairs={{0,16},{1,17},{2,18},{3,19},{16,0},{17,1},{18,2},{19,3},{4,20},{5,... | collective-permute-start | bytes 307208 | tf_op jit(solution)/shard_map/ppermute | solution.py:175
  11.3 5.4 %collective-permute-start.5 = (bf16[1,200,256]{2,1,0:T(8,128)(2,1)S(1)}, bf16[1,200,256]{2,1,0:T(8,128)(2,1)S(1)}, u32[]{:S(2)}, u32[]{:S(2)}) collective-permute-start(bf16[1,200,256]{2,1,0:T(8,128)(2,1)S(1)} %get-tuple-element.23), channel_id=1, source_target_pairs={{0,2},{1,3},{2,0},{3,1},{16,18},{17,19},{18,16},{19,17},{4,6},{5,7... | collective-permute-start | bytes 307208 | tf_op jit(solution)/shard_map/ppermute | solution.py:175
  14.6 4.7 %collective-permute-start.6 = (bf16[1,200,256]{2,1,0:T(8,128)(2,1)S(1)}, bf16[1,200,256]{2,1,0:T(8,128)(2,1)S(1)}, u32[]{:S(2)}, u32[]{:S(2)}) collective-permute-start(bf16[1,200,256]{2,1,0:T(8,128)(2,1)S(1)} %get-tuple-element.24), channel_id=1, source_target_pairs={{0,1},{1,0},{2,3},{3,2},{16,17},{17,16},{18,19},{19,18},{4,5},{5,4... | collective-permute-start | bytes 307208 | tf_op jit(solution)/shard_map/ppermute | solution.py:175
  15.5 3.8 %collective-permute-start.7 = (bf16[1,200,256]{2,1,0:T(8,128)(2,1)S(1)}, bf16[1,200,256]{2,1,0:T(8,128)(2,1)S(1)}, u32[]{:S(2)}, u32[]{:S(2)}) collective-permute-start(bf16[1,200,256]{2,1,0:T(8,128)(2,1)S(1)} %get-tuple-element.17.refs_0_), channel_id=1, source_target_pairs={{0,8},{8,0},{1,9},{9,1},{2,10},{10,2},{3,11},{11,3},{4,12},{12,4},... | collective-permute-start | bytes 307208 | tf_op jit(solution)/shard_map/ppermute | solution.py:178
  16.1 3.7 %collective-permute-start.8 = (bf16[1,200,256]{2,1,0:T(8,128)(2,1)S(1)}, bf16[1,200,256]{2,1,0:T(8,128)(2,1)S(1)}, u32[]{:S(2)}, u32[]{:S(2)}) collective-permute-start(bf16[1,200,256]{2,1,0:T(8,128)(2,1)S(1)} %collective-permute-done.refs_1_), channel_id=1, source_target_pairs={{0,8},{8,0},{1,9},{9,1},{2,10},{10,2},{3,11},{11,3},{4,12},{12,4},... | collective-permute-start | bytes 307208 | tf_op jit(solution)/shard_map/ppermute | solution.py:178
  16.1 3.7 %collective-permute-start.9 = (bf16[1,200,256]{2,1,0:T(8,128)(2,1)S(1)}, bf16[1,200,256]{2,1,0:T(8,128)(2,1)S(1)}, u32[]{:S(2)}, u32[]{:S(2)}) collective-permute-start(bf16[1,200,256]{2,1,0:T(8,128)(2,1)S(1)} %collective-permute-done.1.refs_2_), channel_id=1, source_target_pairs={{0,8},{8,0},{1,9},{9,1},{2,10},{10,2},{3,11},{11,3},{4,12},{12,4},... | collective-permute-start | bytes 307208 | tf_op jit(solution)/shard_map/ppermute | solution.py:178
  16.6 3.7 %collective-permute-start.10 = (bf16[1,200,256]{2,1,0:T(8,128)(2,1)S(1)}, bf16[1,200,256]{2,1,0:T(8,128)(2,1)S(1)}, u32[]{:S(2)}, u32[]{:S(2)}) collective-permute-start(bf16[1,200,256]{2,1,0:T(8,128)(2,1)S(1)} %collective-permute-done.2.refs_3_), channel_id=1, source_target_pairs={{0,8},{8,0},{1,9},{9,1},{2,10},{10,2},{3,11},{11,3},{4,12},{12,4},... | collective-permute-start | bytes 307208 | tf_op jit(solution)/shard_map/ppermute | solution.py:178
  19.2 1.3 %collective-permute-start.11 = (bf16[1,200,256]{2,1,0:T(8,128)(2,1)S(1)}, bf16[1,200,256]{2,1,0:T(8,128)(2,1)S(1)}, u32[]{:S(2)}, u32[]{:S(2)}) collective-permute-start(bf16[1,200,256]{2,1,0:T(8,128)(2,1)S(1)} %collective-permute-done.3.refs_4_), channel_id=1, source_target_pairs={{0,8},{8,0},{1,9},{9,1},{2,10},{10,2},{3,11},{11,3},{4,12},{12,4},... | collective-permute-start | bytes 307208 | tf_op jit(solution)/shard_map/ppermute | solution.py:178
  19.3 1.5 %collective-permute-start.12 = (bf16[1,200,256]{2,1,0:T(8,128)(2,1)S(1)}, bf16[1,200,256]{2,1,0:T(8,128)(2,1)S(1)}, u32[]{:S(2)}, u32[]{:S(2)}) collective-permute-start(bf16[1,200,256]{2,1,0:T(8,128)(2,1)S(1)} %collective-permute-done.4.refs_5_), channel_id=1, source_target_pairs={{0,8},{8,0},{1,9},{9,1},{2,10},{10,2},{3,11},{11,3},{4,12},{12,4},... | collective-permute-start | bytes 307208 | tf_op jit(solution)/shard_map/ppermute | solution.py:178
  19.8 1.3 %collective-permute-start.13 = (bf16[1,200,256]{2,1,0:T(8,128)(2,1)S(1)}, bf16[1,200,256]{2,1,0:T(8,128)(2,1)S(1)}, u32[]{:S(2)}, u32[]{:S(2)}) collective-permute-start(bf16[1,200,256]{2,1,0:T(8,128)(2,1)S(1)} %collective-permute-done.5.refs_6_), channel_id=1, source_target_pairs={{0,8},{8,0},{1,9},{9,1},{2,10},{10,2},{3,11},{11,3},{4,12},{12,4},... | collective-permute-start | bytes 307208 | tf_op jit(solution)/shard_map/ppermute | solution.py:178
  19.8 1.4 %collective-permute-start.14 = (bf16[1,200,256]{2,1,0:T(8,128)(2,1)S(1)}, bf16[1,200,256]{2,1,0:T(8,128)(2,1)S(1)}, u32[]{:S(2)}, u32[]{:S(2)}) collective-permute-start(bf16[1,200,256]{2,1,0:T(8,128)(2,1)S(1)} %collective-permute-done.6.refs_7_), channel_id=1, source_target_pairs={{0,8},{8,0},{1,9},{9,1},{2,10},{10,2},{3,11},{11,3},{4,12},{12,4},... | collective-permute-start | bytes 307208 | tf_op jit(solution)/shard_map/ppermute | solution.py:178
  21.8 11.7 %collective-permute-start.15 = (f32[136,256]{1,0:T(8,128)S(1)}, f32[136,256]{1,0:T(8,128)S(1)}, u32[]{:S(2)}, u32[]{:S(2)}) collective-permute-start(f32[136,256]{1,0:T(8,128)S(1)} %get-tuple-element.26), channel_id=1, source_target_pairs={{0,16},{16,0},{1,17},{17,1},{2,18},{18,2},{3,19},{19,3},{4,20},{20... | collective-permute-start | bytes 417800 | tf_op jit(solution)/shard_map/ppermute | solution.py:234
  23.3 7.1 %collective-permute-start.16 = (bf16[136,256]{1,0:T(8,128)(2,1)S(1)}, bf16[136,256]{1,0:T(8,128)(2,1)S(1)}, u32[]{:S(2)}, u32[]{:S(2)}) collective-permute-start(bf16[136,256]{1,0:T(8,128)(2,1)S(1)} %get-tuple-element.27), channel_id=1, source_target_pairs={{0,4},{4,0},{1,5},{5,1},{2,6},{6,2},{3,7},{7,3},{8,12},{12,8},{9,1... | collective-permute-start | bytes 208904 | tf_op jit(solution)/shard_map/ppermute | solution.py:232
  25.9 7.5 %collective-permute-start.17 = (bf16[136,256]{1,0:T(8,128)(2,1)S(1)}, bf16[136,256]{1,0:T(8,128)(2,1)S(1)}, u32[]{:S(2)}, u32[]{:S(2)}) collective-permute-start(bf16[136,256]{1,0:T(8,128)(2,1)S(1)} %get-tuple-element.28), channel_id=1, source_target_pairs={{0,20},{4,16},{16,4},{20,0},{1,21},{5,17},{17,5},{21,1},{2,22},{6,... | collective-permute-start | bytes 208904 | tf_op jit(solution)/shard_map/ppermute | solution.py:231

commit v5 on v4

--- a/solution.py
+++ b/solution.py
@@ -29,8 +29,21 @@
     return jnp.concatenate([row[:, middle:], row[:, :middle]], axis=1)
 
 
+def by_core(block):
+    middle = block.shape[1] // 2
+    first, second = block[:, :middle], block[:, middle:]
+    left = lax.broadcasted_iota(jnp.int32, (1, middle), 1) < middle // 2
+    return jnp.concatenate(
+        [jnp.where(left, first, half_turn(second)), jnp.where(left, half_turn(first), second)], axis=1
+    )
+
+
+def spot(index):
+    return index % 2 * 2 + index // 2
+
+
 def prep_kernel(apart, assignment, pairing, half, me, x_ref, *refs):
-    outs, (centred, centres, side) = refs[:-3], refs[-3:]
+    outs, (centred, centres, owned, owned_centres, side) = refs[:-5], refs[-5:]
     cells, genes = x_ref.shape
     panels = assignment.shape[0]
     panel = genes // panels
@@ -41,8 +54,11 @@
         block = x_ref[:, pl.ds(start, panel)]
         mean = jnp.sum(block, axis=0, keepdims=True) * (1.0 / cells)
         centre = mean.astype(BF16).astype(F32)
-        centred[p] = (block - centre).astype(BF16)
+        block = block - centre
+        centred[p] = block.astype(BF16)
         centres[pl.ds(p, 1), :] = centre
+        owned[p] = by_core(block).astype(BF16)
+        owned_centres[pl.ds(p, 1), :] = by_core(centre)
         return carry
 
     lax.fori_loop(0, panels, one_panel, 0, unroll=panels <= 16)
@@ -55,8 +71,8 @@
             own = assignment[owner * SLOTS + s]
             for k in range(EACH):
                 p = own if k == 0 else pairing[k - 1, own]
-                out[at, pl.ds((place * EACH + k) * cells, cells), :] = centred[p]
-                side[pl.ds(place * EACH + k, 1), :] = centres[pl.ds(p, 1), :]
+                out[at, pl.ds((place * EACH + k) * cells, cells), :] = (owned if k == 0 else centred)[p]
+                side[pl.ds(place * EACH + k, 1), :] = (owned_centres if k == 0 else centres)[pl.ds(p, 1), :]
         out[at, pl.ds(SLOTS * EACH * cells, STATS), :] = side[...].astype(BF16)
 
     if apart:
@@ -105,20 +121,21 @@
         operands.append(jnp.concatenate([data, jnp.concatenate(extra, axis=0).astype(BF16)], axis=0))
     stats = jnp.concatenate(means + squares + [jnp.zeros((STATS - 2 * EACH, panel), F32)], axis=0)
     high, low = split_two(stats)
+    mine = place[0]
+    own = jnp.where(mine % 2 == 0, operands[0][:, : panel // 2], operands[0][:, panel // 2 :])
     for r in range(ROUNDS):
         tile[r] = lax.dot_general(
-            operands[0], operands[1 + r], (((0,), (0,)), ((), ())), preferred_element_type=F32
+            own, operands[1 + r], (((0,), (0,)), ((), ())), preferred_element_type=F32
         )
-    mine = place[0]
     base = ROUNDS * quarter
     for ref, index in ((same_ref, mine), (cross_ref, (mine + 2) % 4)):
-        start = pl.multiple_of(index * quarter, quarter)
+        start = pl.multiple_of(index // 2 * quarter, quarter)
         for r in range(ROUNDS):
             ref[pl.ds(r * quarter, quarter), :] = tile[r, pl.ds(start, quarter), :].astype(ref.dtype)
         if ref.dtype == F32:
             ref[pl.ds(base, STATS), :] = stats
         else:
-            needed = lax.broadcasted_iota(jnp.int32, (1, panel), 1) // quarter == index
+            needed = lax.broadcasted_iota(jnp.int32, (1, panel), 1) // quarter == spot(index)
             own = [jnp.where(needed, v[0:1], half_turn(v[EACH : EACH + 1])) for v in (high, low)]
             partners = [high[1:EACH], low[1:EACH], high[EACH + 1 : 2 * EACH]]
             ref[pl.ds(base, STATS), :] = jnp.concatenate(own + partners, axis=0).astype(BF16)
@@ -138,7 +155,7 @@
 def finish_kernel(total, place, nearer, keep_ref, x_ref, half_ref, both_ref, out_ref, columns):
     quarter, panel = out_ref.shape[2:]
     base = ROUNDS * quarter
-    mine = pl.multiple_of(place[0] * quarter, quarter)
+    mine = pl.multiple_of(spot(place[0]) * quarter, quarter)
     near = nearer[0]
     sources = ((near, keep_ref, half_ref), (1 - near, x_ref, both_ref))
     for i, (slot, same_ref, other_ref) in enumerate(sources):
@@ -207,6 +224,8 @@
         scratch_shapes=[
             pltpu.VMEM((panels, cells, panel), BF16),
             pltpu.VMEM((panels, panel), F32),
+            pltpu.VMEM((panels, cells, panel), BF16),
+            pltpu.VMEM((panels, panel), F32),
             pltpu.VMEM((STATS, panel), F32),
         ],
         name="prep",
@@ -220,7 +239,7 @@
             out_shape=(array((base + STATS, panel), dtype),) * 2,
             in_specs=[smem] + [vmem] * len(received),
             out_specs=(vmem, vmem),
-            scratch_shapes=[pltpu.VMEM((ROUNDS, panel, panel), F32)],
+            scratch_shapes=[pltpu.VMEM((ROUNDS, panel // 2, panel), F32)],
             compiler_params=pltpu.CompilerParams(
                 vmem_limit_bytes=min(60 << 20, (8 << 20) + 6 * received_bytes)
             ),

time: 34.6 us -> 34.6 us (level)
  transfers between devices with their start and end apart: 18 -> 18, of which waited for: 9 -> 9; matrix products, arithmetic and copies ran while one was open for 0% -> 0% of each run, Pallas kernels for 2% -> 1%
where the time goes in v5:
time: 34.6 us; the launch traced here: 34.4 us
  starting transfers between devices  17.4 us (50%)
  waiting for transfers between devices  13.6 us (39%)
  Pallas kernels  3.37 us (10%)
    ppermute x7, starting transfers between devices, gather(): lax.ppermute(value, ('x', 'rest'), [(i, i ^ k) for i in range(n_wide)])  11.3 us
    ppermute x7, waiting for transfers between devices, gather(): lax.ppermute(value, ('x', 'rest'), [(i, i ^ k) for i in range(n_wide)])  6.05 us
    ppermute x1, waiting for transfers between devices, shards(): from_half = lax.ppermute(to_half, 'half', [(0, 1), (1, 0)])  3.55 us
    ppermute x1, waiting for transfers between devices, shards(): lax.ppermute(to_both, ('x', 'half'), [(i, i ^ 3) for i in range(4)])  3.06 us
    ppermute x1, starting transfers between devices, shards(): from_half = lax.ppermute(to_half, 'half', [(0, 1), (1, 0)])  2.66 us
    ppermute x8, starting transfers between devices, gather(): there.append(lax.ppermute(value, 'core', [(0, 1), (1, 0)]))  1.6 us
    pallas_call x1, Pallas kernels, shards(): pl.pallas_call(functools.partial(prep_kernel, apart), out_shape=(array(sh...  1.38 us
    pallas_call x1, Pallas kernels, shards(): pl.pallas_call(functools.partial(finish_kernel, total), out_shape=jax.Sha...  1.04 us
  transfers between devices with their start and end apart: 18, of which 9 were waited for; matrix products, arithmetic and copies ran while one was open for 0% of the time, Pallas kernels for 1%

profile of v5, /device:TPU:0, one launch (start us, length us, event | category | flops | bytes accessed | tf_op | source)
XLA Modules:
  0.0 34.4 jit_solution(13524752622381794864)
XLA Ops:
  0.0 1.4 %prep.1 = (bf16[1,200,256]{2,1,0:T(8,128)(2,1)S(1)}, bf16[1,200,256]{2,1,0:T(8,128)(2,1)S(1)}, bf16[1,200,256]{2,1,0:T(8,128)(2,1)S(1)}, bf16[1,200,256]{2,1,0:T...) custom-call(s32[16]{0:T(128)} %assignment.1, ...), custom_call_target="tpu_custom_call" | custom-call | tf_op jit(solution)/shard_map/prep/pallas_call | solution.py:219
  1.4 5.0 %collective-permute-start = (bf16[1,200,256]{2,1,0:T(8,128)(2,1)S(1)}, bf16[1,200,256]{2,1,0:T(8,128)(2,1)S(1)}, u32[]{:S(2)}, u32[]{:S(2)}) collective-permute-start(bf16[1,200,256]{2,1,0:T(8,128)(2,1)S(1)} %get-tuple-element.18), channel_id=1, source_target_pairs={{0,19},{1,18},{2,17},{3,16},{16,3},{17,2},{18,1},{19,0},{4,23},{5,... | collective-permute-start | bytes 307208 | tf_op jit(solution)/shard_map/ppermute | solution.py:192
  6.4 0.5 %collective-permute-start.1 = (bf16[1,200,256]{2,1,0:T(8,128)(2,1)S(1)}, bf16[1,200,256]{2,1,0:T(8,128)(2,1)S(1)}, u32[]{:S(2)}, u32[]{:S(2)}) collective-permute-start(bf16[1,200,256]{2,1,0:T(8,128)(2,1)S(1)} %get-tuple-element.19), channel_id=1, source_target_pairs={{0,17},{1,16},{2,19},{3,18},{16,1},{17,0},{18,3},{19,2},{4,21},{5,... | collective-permute-start | bytes 307208 | tf_op jit(solution)/shard_map/ppermute | solution.py:192
  6.9 1.4 %collective-permute-start.2 = (bf16[1,200,256]{2,1,0:T(8,128)(2,1)S(1)}, bf16[1,200,256]{2,1,0:T(8,128)(2,1)S(1)}, u32[]{:S(2)}, u32[]{:S(2)}) collective-permute-start(bf16[1,200,256]{2,1,0:T(8,128)(2,1)S(1)} %get-tuple-element.20), channel_id=1, source_target_pairs={{0,18},{1,19},{2,16},{3,17},{16,2},{17,3},{18,0},{19,1},{4,22},{5,... | collective-permute-start | bytes 307208 | tf_op jit(solution)/shard_map/ppermute | solution.py:192
  8.2 2.5 %collective-permute-start.3 = (bf16[1,200,256]{2,1,0:T(8,128)(2,1)S(1)}, bf16[1,200,256]{2,1,0:T(8,128)(2,1)S(1)}, u32[]{:S(2)}, u32[]{:S(2)}) collective-permute-start(bf16[1,200,256]{2,1,0:T(8,128)(2,1)S(1)} %get-tuple-element.21), channel_id=1, source_target_pairs={{0,3},{1,2},{2,1},{3,0},{16,19},{17,18},{18,17},{19,16},{4,7},{5,6... | collective-permute-start | bytes 307208 | tf_op jit(solution)/shard_map/ppermute | solution.py:192
  10.8 0.5 %collective-permute-start.4 = (bf16[1,200,256]{2,1,0:T(8,128)(2,1)S(1)}, bf16[1,200,256]{2,1,0:T(8,128)(2,1)S(1)}, u32[]{:S(2)}, u32[]{:S(2)}) collective-permute-start(bf16[1,200,256]{2,1,0:T(8,128)(2,1)S(1)} %get-tuple-element.22), channel_id=1, source_target_pairs={{0,16},{1,17},{2,18},{3,19},{16,0},{17,1},{18,2},{19,3},{4,20},{5,... | collective-permute-start | bytes 307208 | tf_op jit(solution)/shard_map/ppermute | solution.py:192
  11.3 0.0 collective-permute-done.refs_1_
  11.3 0.5 %collective-permute-start.5 = (bf16[1,200,256]{2,1,0:T(8,128)(2,1)S(1)}, bf16[1,200,256]{2,1,0:T(8,128)(2,1)S(1)}, u32[]{:S(2)}, u32[]{:S(2)}) collective-permute-start(bf16[1,200,256]{2,1,0:T(8,128)(2,1)S(1)} %get-tuple-element.23), channel_id=1, source_target_pairs={{0,2},{1,3},{2,0},{3,1},{16,18},{17,19},{18,16},{19,17},{4,6},{5,7... | collective-permute-start | bytes 307208 | tf_op jit(solution)/shard_map/ppermute | solution.py:192
  11.8 2.9 %collective-permute-done.1.refs_2_ = bf16[1,200,256]{2,1,0:T(8,128)(2,1)S(1)} collective-permute-done((bf16[1,200,256]{2,1,0:T(8,128)(2,1)S(1)}, bf16[1,200,256]{2,1,0:T(8,128)(2,1)S(1)}, u32[]{:S(2)}, u32[]{:S(2)}) %collective-permute-start.1) | collective-permute-done | bytes 102432 | tf_op jit(solution)/shard_map/ppermute | solution.py:192
  14.6 0.9 %collective-permute-start.6 = (bf16[1,200,256]{2,1,0:T(8,128)(2,1)S(1)}, bf16[1,200,256]{2,1,0:T(8,128)(2,1)S(1)}, u32[]{:S(2)}, u32[]{:S(2)}) collective-permute-start(bf16[1,200,256]{2,1,0:T(8,128)(2,1)S(1)} %get-tuple-element.24), channel_id=1, source_target_pairs={{0,1},{1,0},{2,3},{3,2},{16,17},{17,16},{18,19},{19,18},{4,5},{5,4... | collective-permute-start | bytes 307208 | tf_op jit(solution)/shard_map/ppermute | solution.py:192
  15.5 0.0 collective-permute-done.2.refs_3_
  15.5 0.0 collective-permute-start.7
  15.5 0.6 %collective-permute-done.3.refs_4_ = bf16[1,200,256]{2,1,0:T(8,128)(2,1)S(1)} collective-permute-done((bf16[1,200,256]{2,1,0:T(8,128)(2,1)S(1)}, bf16[1,200,256]{2,1,0:T(8,128)(2,1)S(1)}, u32[]{:S(2)}, u32[]{:S(2)}) %collective-permute-start.3) | collective-permute-done | bytes 102432 | tf_op jit(solution)/shard_map/ppermute | solution.py:192
  16.1 0.0 collective-permute-start.8
  16.1 0.5 %collective-permute-start.9 = (bf16[1,200,256]{2,1,0:T(8,128)(2,1)S(1)}, bf16[1,200,256]{2,1,0:T(8,128)(2,1)S(1)}, u32[]{:S(2)}, u32[]{:S(2)}) collective-permute-start(bf16[1,200,256]{2,1,0:T(8,128)(2,1)S(1)} %collective-permute-done.1.refs_2_), channel_id=1, source_target_pairs={{0,8},{8,0},{1,9},{9,1},{2,10},{10,2},{3,11},{11,3},{4,12},{12,4},... | collective-permute-start | bytes 307208 | tf_op jit(solution)/shard_map/ppermute | solution.py:195
  16.7 0.1 collective-permute-start.10
  16.7 2.5 %collective-permute-done.6.refs_7_ = bf16[1,200,256]{2,1,0:T(8,128)(2,1)S(1)} collective-permute-done((bf16[1,200,256]{2,1,0:T(8,128)(2,1)S(1)}, bf16[1,200,256]{2,1,0:T(8,128)(2,1)S(1)}, u32[]{:S(2)}, u32[]{:S(2)}) %collective-permute-start.6) | collective-permute-done | bytes 102432 | tf_op jit(solution)/shard_map/ppermute | solution.py:192
  19.3 0.5 %collective-permute-start.12 = (bf16[1,200,256]{2,1,0:T(8,128)(2,1)S(1)}, bf16[1,200,256]{2,1,0:T(8,128)(2,1)S(1)}, u32[]{:S(2)}, u32[]{:S(2)}) collective-permute-start(bf16[1,200,256]{2,1,0:T(8,128)(2,1)S(1)} %collective-permute-done.4.refs_5_), channel_id=1, source_target_pairs={{0,8},{8,0},{1,9},{9,1},{2,10},{10,2},{3,11},{11,3},{4,12},{12,4},... | collective-permute-start | bytes 307208 | tf_op jit(solution)/shard_map/ppermute | solution.py:195
  19.8 0.1 collective-permute-start.13
  19.9 0.4 %collective-permute-start.14 = (bf16[1,200,256]{2,1,0:T(8,128)(2,1)S(1)}, bf16[1,200,256]{2,1,0:T(8,128)(2,1)S(1)}, u32[]{:S(2)}, u32[]{:S(2)}) collective-permute-start(bf16[1,200,256]{2,1,0:T(8,128)(2,1)S(1)} %collective-permute-done.6.refs_7_), channel_id=1, source_target_pairs={{0,8},{8,0},{1,9},{9,1},{2,10},{10,2},{3,11},{11,3},{4,12},{12,4},... | collective-permute-start | bytes 307208 | tf_op jit(solution)/shard_map/ppermute | solution.py:195
  20.3 0.3 collective-permute-done.11.refs_12_
  20.6 0.2 collective-permute-done.12.refs_13_
  20.7 0.4 %collective-permute-done.13.refs_14_ = bf16[1,200,256]{2,1,0:T(8,128)(2,1)S(1)} collective-permute-done((bf16[1,200,256]{2,1,0:T(8,128)(2,1)S(1)}, bf16[1,200,256]{2,1,0:T(8,128)(2,1)S(1)}, u32[]{:S(2)}, u32[]{:S(2)}) %collective-permute-start.13) | collective-permute-done | bytes 102432 | tf_op jit(solution)/shard_map/ppermute | solution.py:195
  21.1 0.2 collective-permute-done.14.refs_15_
  21.3 0.5 %gram.2 = (f32[136,256]{1,0:T(8,128)S(1)}, f32[136,256]{1,0:T(8,128)S(1)}) custom-call(s32[1]{0:T(128)} %bitcast.place, bf16[1,200,256]{2,1,0:T(8,128)(2,1)S(1)} %get-tuple-element.17.refs_0_, bf16[1,200,256]{2,1,0:T(8,128)(2,1)S(1)} %collective-permute-done.refs_1_, bf16[1,200,256]{2,1,0:T(8,128)(2,1)S(1)} %collective-permute-done.1.refs_2_, ...), custom_call_target="tpu_custom_call" | custom-call | tf_op jit(solution)/shard_map/gram/pallas_call | solution.py:237
  21.8 1.0 %collective-permute-start.15 = (f32[136,256]{1,0:T(8,128)S(1)}, f32[136,256]{1,0:T(8,128)S(1)}, u32[]{:S(2)}, u32[]{:S(2)}) collective-permute-start(f32[136,256]{1,0:T(8,128)S(1)} %get-tuple-element.26), channel_id=1, source_target_pairs={{0,16},{16,0},{1,17},{17,1},{2,18},{18,2},{3,19},{19,3},{4,20},{20... | collective-permute-start | bytes 417800 | tf_op jit(solution)/shard_map/ppermute | solution.py:253
  22.8 0.5 %gram.3 = (bf16[136,256]{1,0:T(8,128)(2,1)S(1)}, bf16[136,256]{1,0:T(8,128)(2,1)S(1)}) custom-call(s32[1]{0:T(128)} %bitcast.place, bf16[1,200,256]{2,1,0:T(8,128)(2,1)S(1)} %get-tuple-element.17.refs_0_, bf16[1,200,256]{2,1,0:T(8,128)(2,1)S(1)} %collective-permute-done.refs_1_, bf16[1,200,256]{2,1,0:T(8,128)(2,1)S(1)} %collective-permute-done.1.refs_2_, ...), custom_call_target="tpu_custom_call" | custom-call | tf_op jit(solution)/shard_map/gram/pallas_call | solution.py:237
  23.2 2.7 %collective-permute-start.16 = (bf16[136,256]{1,0:T(8,128)(2,1)S(1)}, bf16[136,256]{1,0:T(8,128)(2,1)S(1)}, u32[]{:S(2)}, u32[]{:S(2)}) collective-permute-start(bf16[136,256]{1,0:T(8,128)(2,1)S(1)} %get-tuple-element.27), channel_id=1, source_target_pairs={{0,4},{4,0},{1,5},{5,1},{2,6},{6,2},{3,7},{7,3},{8,12},{12,8},{9,1... | collective-permute-start | bytes 208904 | tf_op jit(solution)/shard_map/ppermute | solution.py:251
  25.9 0.9 %collective-permute-start.17 = (bf16[136,256]{1,0:T(8,128)(2,1)S(1)}, bf16[136,256]{1,0:T(8,128)(2,1)S(1)}, u32[]{:S(2)}, u32[]{:S(2)}) collective-permute-start(bf16[136,256]{1,0:T(8,128)(2,1)S(1)} %get-tuple-element.28), channel_id=1, source_target_pairs={{0,20},{4,16},{16,4},{20,0},{1,21},{5,17},{17,5},{21,1},{2,22},{6,... | collective-permute-start | bytes 208904 | tf_op jit(solution)/shard_map/ppermute | solution.py:250
  26.8 3.5 %collective-permute-done.16.half_ref = bf16[136,256]{1,0:T(8,128)(2,1)S(1)} collective-permute-done((bf16[136,256]{1,0:T(8,128)(2,1)S(1)}, bf16[136,256]{1,0:T(8,128)(2,1)S(1)}, u32[]{:S(2)}, u32[]{:S(2)}) %collective-permute-start.16) | collective-permute-done | bytes 69664 | tf_op jit(solution)/shard_map/ppermute | solution.py:251
  30.3 3.1 %collective-permute-done.17.both_ref = bf16[136,256]{1,0:T(8,128)(2,1)S(1)} collective-permute-done((bf16[136,256]{1,0:T(8,128)(2,1)S(1)}, bf16[136,256]{1,0:T(8,128)(2,1)S(1)}, u32[]{:S(2)}, u32[]{:S(2)}) %collective-permute-start.17) | collective-permute-done | bytes 69664 | tf_op jit(solution)/shard_map/ppermute | solution.py:250
  33.4 1.0 %finish.1 = f32[2,2,64,256]{3,2,1,0:T(8,128)} custom-call(s32[1]{0:T(128)} %bitcast.place, s32[1]{0:T(128)} %bitcast.1.nearer, f32[136,256]{1,0:T(8,128)S(1)} %get-tuple-element.25.keep_ref, f32[136,256]{1,0:T(8,128)S(1)} %collective-permute-done.15.x_ref, bf16[136,256]{1,0:T(8,128)(2,1)S(1)} %collective-permute-done.16.half_ref, ...), custom_call_target="tpu_custom_call" | custom-call | tf_op jit(solution)/shard_map/finish/pallas_call | solution.py:254
  (8 shorter events, 0.0 us)
Async XLA Ops:
  1.4 9.9 %collective-permute-start = (bf16[1,200,256]{2,1,0:T(8,128)(2,1)S(1)}, bf16[1,200,256]{2,1,0:T(8,128)(2,1)S(1)}, u32[]{:S(2)}, u32[]{:S(2)}) collective-permute-start(bf16[1,200,256]{2,1,0:T(8,128)(2,1)S(1)} %get-tuple-element.18), channel_id=1, source_target_pairs={{0,19},{1,18},{2,17},{3,16},{16,3},{17,2},{18,1},{19,0},{4,23},{5,... | collective-permute-start | bytes 307208 | tf_op jit(solution)/shard_map/ppermute | solution.py:192
  6.4 8.2 %collective-permute-start.1 = (bf16[1,200,256]{2,1,0:T(8,128)(2,1)S(1)}, bf16[1,200,256]{2,1,0:T(8,128)(2,1)S(1)}, u32[]{:S(2)}, u32[]{:S(2)}) collective-permute-start(bf16[1,200,256]{2,1,0:T(8,128)(2,1)S(1)} %get-tuple-element.19), channel_id=1, source_target_pairs={{0,17},{1,16},{2,19},{3,18},{16,1},{17,0},{18,3},{19,2},{4,21},{5,... | collective-permute-start | bytes 307208 | tf_op jit(solution)/shard_map/ppermute | solution.py:192
  6.9 8.7 %collective-permute-start.2 = (bf16[1,200,256]{2,1,0:T(8,128)(2,1)S(1)}, bf16[1,200,256]{2,1,0:T(8,128)(2,1)S(1)}, u32[]{:S(2)}, u32[]{:S(2)}) collective-permute-start(bf16[1,200,256]{2,1,0:T(8,128)(2,1)S(1)} %get-tuple-element.20), channel_id=1, source_target_pairs={{0,18},{1,19},{2,16},{3,17},{16,2},{17,3},{18,0},{19,1},{4,22},{5,... | collective-permute-start | bytes 307208 | tf_op jit(solution)/shard_map/ppermute | solution.py:192
  8.2 7.9 %collective-permute-start.3 = (bf16[1,200,256]{2,1,0:T(8,128)(2,1)S(1)}, bf16[1,200,256]{2,1,0:T(8,128)(2,1)S(1)}, u32[]{:S(2)}, u32[]{:S(2)}) collective-permute-start(bf16[1,200,256]{2,1,0:T(8,128)(2,1)S(1)} %get-tuple-element.21), channel_id=1, source_target_pairs={{0,3},{1,2},{2,1},{3,0},{16,19},{17,18},{18,17},{19,16},{4,7},{5,6... | collective-permute-start | bytes 307208 | tf_op jit(solution)/shard_map/ppermute | solution.py:192
  10.8 5.4 %collective-permute-start.4 = (bf16[1,200,256]{2,1,0:T(8,128)(2,1)S(1)}, bf16[1,200,256]{2,1,0:T(8,128)(2,1)S(1)}, u32[]{:S(2)}, u32[]{:S(2)}) collective-permute-start(bf16[1,200,256]{2,1,0:T(8,128)(2,1)S(1)} %get-tuple-element.22), channel_id=1, source_target_pairs={{0,16},{1,17},{2,18},{3,19},{16,0},{17,1},{18,2},{19,3},{4,20},{5,... | collective-permute-start | bytes 307208 | tf_op jit(solution)/shard_map/ppermute | solution.py:192
  11.3 5.4 %collective-permute-start.5 = (bf16[1,200,256]{2,1,0:T(8,128)(2,1)S(1)}, bf16[1,200,256]{2,1,0:T(8,128)(2,1)S(1)}, u32[]{:S(2)}, u32[]{:S(2)}) collective-permute-start(bf16[1,200,256]{2,1,0:T(8,128)(2,1)S(1)} %get-tuple-element.23), channel_id=1, source_target_pairs={{0,2},{1,3},{2,0},{3,1},{16,18},{17,19},{18,16},{19,17},{4,6},{5,7... | collective-permute-start | bytes 307208 | tf_op jit(solution)/shard_map/ppermute | solution.py:192
  14.6 4.7 %collective-permute-start.6 = (bf16[1,200,256]{2,1,0:T(8,128)(2,1)S(1)}, bf16[1,200,256]{2,1,0:T(8,128)(2,1)S(1)}, u32[]{:S(2)}, u32[]{:S(2)}) collective-permute-start(bf16[1,200,256]{2,1,0:T(8,128)(2,1)S(1)} %get-tuple-element.24), channel_id=1, source_target_pairs={{0,1},{1,0},{2,3},{3,2},{16,17},{17,16},{18,19},{19,18},{4,5},{5,4... | collective-permute-start | bytes 307208 | tf_op jit(solution)/shard_map/ppermute | solution.py:192
  15.5 3.8 %collective-permute-start.7 = (bf16[1,200,256]{2,1,0:T(8,128)(2,1)S(1)}, bf16[1,200,256]{2,1,0:T(8,128)(2,1)S(1)}, u32[]{:S(2)}, u32[]{:S(2)}) collective-permute-start(bf16[1,200,256]{2,1,0:T(8,128)(2,1)S(1)} %get-tuple-element.17.refs_0_), channel_id=1, source_target_pairs={{0,8},{8,0},{1,9},{9,1},{2,10},{10,2},{3,11},{11,3},{4,12},{12,4},... | collective-permute-start | bytes 307208 | tf_op jit(solution)/shard_map/ppermute | solution.py:195
  16.1 3.7 %collective-permute-start.8 = (bf16[1,200,256]{2,1,0:T(8,128)(2,1)S(1)}, bf16[1,200,256]{2,1,0:T(8,128)(2,1)S(1)}, u32[]{:S(2)}, u32[]{:S(2)}) collective-permute-start(bf16[1,200,256]{2,1,0:T(8,128)(2,1)S(1)} %collective-permute-done.refs_1_), channel_id=1, source_target_pairs={{0,8},{8,0},{1,9},{9,1},{2,10},{10,2},{3,11},{11,3},{4,12},{12,4},... | collective-permute-start | bytes 307208 | tf_op jit(solution)/shard_map/ppermute | solution.py:195
  16.1 3.7 %collective-permute-start.9 = (bf16[1,200,256]{2,1,0:T(8,128)(2,1)S(1)}, bf16[1,200,256]{2,1,0:T(8,128)(2,1)S(1)}, u32[]{:S(2)}, u32[]{:S(2)}) collective-permute-start(bf16[1,200,256]{2,1,0:T(8,128)(2,1)S(1)} %collective-permute-done.1.refs_2_), channel_id=1, source_target_pairs={{0,8},{8,0},{1,9},{9,1},{2,10},{10,2},{3,11},{11,3},{4,12},{12,4},... | collective-permute-start | bytes 307208 | tf_op jit(solution)/shard_map/ppermute | solution.py:195
  16.7 3.7 %collective-permute-start.10 = (bf16[1,200,256]{2,1,0:T(8,128)(2,1)S(1)}, bf16[1,200,256]{2,1,0:T(8,128)(2,1)S(1)}, u32[]{:S(2)}, u32[]{:S(2)}) collective-permute-start(bf16[1,200,256]{2,1,0:T(8,128)(2,1)S(1)} %collective-permute-done.2.refs_3_), channel_id=1, source_target_pairs={{0,8},{8,0},{1,9},{9,1},{2,10},{10,2},{3,11},{11,3},{4,12},{12,4},... | collective-permute-start | bytes 307208 | tf_op jit(solution)/shard_map/ppermute | solution.py:195
  19.3 1.3 %collective-permute-start.11 = (bf16[1,200,256]{2,1,0:T(8,128)(2,1)S(1)}, bf16[1,200,256]{2,1,0:T(8,128)(2,1)S(1)}, u32[]{:S(2)}, u32[]{:S(2)}) collective-permute-start(bf16[1,200,256]{2,1,0:T(8,128)(2,1)S(1)} %collective-permute-done.3.refs_4_), channel_id=1, source_target_pairs={{0,8},{8,0},{1,9},{9,1},{2,10},{10,2},{3,11},{11,3},{4,12},{12,4},... | collective-permute-start | bytes 307208 | tf_op jit(solution)/shard_map/ppermute | solution.py:195
  19.3 1.5 %collective-permute-start.12 = (bf16[1,200,256]{2,1,0:T(8,128)(2,1)S(1)}, bf16[1,200,256]{2,1,0:T(8,128)(2,1)S(1)}, u32[]{:S(2)}, u32[]{:S(2)}) collective-permute-start(bf16[1,200,256]{2,1,0:T(8,128)(2,1)S(1)} %collective-permute-done.4.refs_5_), channel_id=1, source_target_pairs={{0,8},{8,0},{1,9},{9,1},{2,10},{10,2},{3,11},{11,3},{4,12},{12,4},... | collective-permute-start | bytes 307208 | tf_op jit(solution)/shard_map/ppermute | solution.py:195
  19.8 1.3 %collective-permute-start.13 = (bf16[1,200,256]{2,1,0:T(8,128)(2,1)S(1)}, bf16[1,200,256]{2,1,0:T(8,128)(2,1)S(1)}, u32[]{:S(2)}, u32[]{:S(2)}) collective-permute-start(bf16[1,200,256]{2,1,0:T(8,128)(2,1)S(1)} %collective-permute-done.5.refs_6_), channel_id=1, source_target_pairs={{0,8},{8,0},{1,9},{9,1},{2,10},{10,2},{3,11},{11,3},{4,12},{12,4},... | collective-permute-start | bytes 307208 | tf_op jit(solution)/shard_map/ppermute | solution.py:195
  19.9 1.4 %collective-permute-start.14 = (bf16[1,200,256]{2,1,0:T(8,128)(2,1)S(1)}, bf16[1,200,256]{2,1,0:T(8,128)(2,1)S(1)}, u32[]{:S(2)}, u32[]{:S(2)}) collective-permute-start(bf16[1,200,256]{2,1,0:T(8,128)(2,1)S(1)} %collective-permute-done.6.refs_7_), channel_id=1, source_target_pairs={{0,8},{8,0},{1,9},{9,1},{2,10},{10,2},{3,11},{11,3},{4,12},{12,4},... | collective-permute-start | bytes 307208 | tf_op jit(solution)/shard_map/ppermute | solution.py:195
  21.8 11.6 %collective-permute-start.15 = (f32[136,256]{1,0:T(8,128)S(1)}, f32[136,256]{1,0:T(8,128)S(1)}, u32[]{:S(2)}, u32[]{:S(2)}) collective-permute-start(f32[136,256]{1,0:T(8,128)S(1)} %get-tuple-element.26), channel_id=1, source_target_pairs={{0,16},{16,0},{1,17},{17,1},{2,18},{18,2},{3,19},{19,3},{4,20},{20... | collective-permute-start | bytes 417800 | tf_op jit(solution)/shard_map/ppermute | solution.py:253
  23.2 7.1 %collective-permute-start.16 = (bf16[136,256]{1,0:T(8,128)(2,1)S(1)}, bf16[136,256]{1,0:T(8,128)(2,1)S(1)}, u32[]{:S(2)}, u32[]{:S(2)}) collective-permute-start(bf16[136,256]{1,0:T(8,128)(2,1)S(1)} %get-tuple-element.27), channel_id=1, source_target_pairs={{0,4},{4,0},{1,5},{5,1},{2,6},{6,2},{3,7},{7,3},{8,12},{12,8},{9,1... | collective-permute-start | bytes 208904 | tf_op jit(solution)/shard_map/ppermute | solution.py:251
  25.9 7.5 %collective-permute-start.17 = (bf16[136,256]{1,0:T(8,128)(2,1)S(1)}, bf16[136,256]{1,0:T(8,128)(2,1)S(1)}, u32[]{:S(2)}, u32[]{:S(2)}) collective-permute-start(bf16[136,256]{1,0:T(8,128)(2,1)S(1)} %get-tuple-element.28), channel_id=1, source_target_pairs={{0,20},{4,16},{16,4},{20,0},{1,21},{5,17},{17,5},{21,1},{2,22},{6,... | collective-permute-start | bytes 208904 | tf_op jit(solution)/shard_map/ppermute | solution.py:250

commit v6 on v4

--- a/solution.py
+++ b/solution.py
@@ -13,7 +13,7 @@
 ROUNDS = 2
 EACH = 1 + ROUNDS
 DIRECT = 8
-ORDER = (0, 7, 5, 6, 3, 4, 2, 1)
+ORDERS = ((0, 7, 5, 6, 3, 4, 1, 2), (0, 7, 3, 4, 5, 2, 6, 1))
 STATS = 8
 F32 = jnp.float32
 BF16 = jnp.bfloat16
@@ -29,7 +29,7 @@
     return jnp.concatenate([row[:, middle:], row[:, :middle]], axis=1)
 
 
-def prep_kernel(apart, assignment, pairing, half, me, x_ref, *refs):
+def prep_kernel(apart, assignment, pairing, half, me, place, x_ref, *refs):
     outs, (centred, centres, side) = refs[:-3], refs[-3:]
     cells, genes = x_ref.shape
     panels = assignment.shape[0]
@@ -60,8 +60,9 @@
         out[at, pl.ds(SLOTS * EACH * cells, STATS), :] = side[...].astype(BF16)
 
     if apart:
-        for k, out in zip(ORDER, outs):
-            one_message(me[0] ^ k, out, 0)
+        core = half[0]
+        for first, second, out in zip(*ORDERS, outs):
+            one_message(me[0] ^ (first + core * (second - first)), out, 0)
     else:
         lax.fori_loop(0, n_wide, lambda w, carry: one_message(w, outs[0], w) or carry, 0)
 
@@ -171,8 +172,14 @@
         here = [lax.all_to_all(sent[0], ("x", "rest"), split_axis=0, concat_axis=0, tiled=True)]
     else:
         here = [sent[0]]
-        for k, value in zip(ORDER[1:], sent[1:]):
-            here.append(lax.ppermute(value, ("x", "rest"), [(i, i ^ k) for i in range(n_wide)]))
+        apart = n_wide // 2
+        for step in range(1, n_wide):
+            pairs = []
+            for i in range(2 * n_wide):
+                x, core, rest = i // n_wide, i // apart % 2, i % apart
+                to = (x * apart + rest) ^ ORDERS[core][step]
+                pairs.append((i, (to // apart * 2 + core) * apart + to % apart))
+            here.append(lax.ppermute(sent[step], ("x", "half", "rest"), pairs))
     there = []
     for value in here:
         there.append(lax.ppermute(value, "core", [(0, 1), (1, 0)]))
@@ -202,7 +209,7 @@
     sent = pl.pallas_call(
         functools.partial(prep_kernel, apart),
         out_shape=(array(shape, BF16),) * (n_wide if apart else 1),
-        in_specs=[smem, smem, smem, smem, vmem],
+        in_specs=[smem, smem, smem, smem, smem, vmem],
         out_specs=(vmem,) * (n_wide if apart else 1),
         scratch_shapes=[
             pltpu.VMEM((panels, cells, panel), BF16),
@@ -210,7 +217,7 @@
             pltpu.VMEM((STATS, panel), F32),
         ],
         name="prep",
-    )(assignment, pairing, half, me, expression)
+    )(assignment, pairing, half, me, place, expression)
     received = gather(sent, n_wide)
     base = ROUNDS * quarter
 

time: 34.6 us -> 34.9 us (level)
  starting transfers between devices: 17.4 us -> 18.2 us
  waiting for transfers between devices: 13.6 us -> 13.1 us
    ppermute x1, starting transfers between devices: 0.86 us -> 3.04 us  [shards(): lax.ppermute(to_both, ('x', 'half'), [(i, i ^ 3) for i in range(4)])]
    ppermute x1, starting transfers between devices: 2.65 us -> 0.55 us  [shards(): from_half = lax.ppermute(to_half, 'half', [(0, 1), (1, 0)])]
    ppermute x1, waiting for transfers between devices: 3.56 us -> 5.21 us  [shards(): from_half = lax.ppermute(to_half, 'half', [(0, 1), (1, 0)])]
    ppermute x1, waiting for transfers between devices: 3.06 us -> 1.41 us  [shards(): lax.ppermute(to_both, ('x', 'half'), [(i, i ^ 3) for i in range(4)])]
    ppermute x7, starting transfers between devices: 11.3 us -> 11.9 us  [gather(): here.append(lax.ppermute(sent[step], ('x', 'half', 'rest'), pairs))]
    ppermute x7, waiting for transfers between devices: 6.05 us -> 5.53 us  [gather(): here.append(lax.ppermute(sent[step], ('x', 'half', 'rest'), pairs))]
  transfers between devices with their start and end apart: 18 -> 18, of which waited for: 9 -> 9; matrix products, arithmetic and copies ran while one was open for 0% -> 0% of each run, Pallas kernels for 2% -> 1%
where the time goes in v6:
time: 34.9 us; the launch traced here: 34.8 us
  starting transfers between devices  18.2 us (52%)
  waiting for transfers between devices  13.1 us (38%)
  Pallas kernels  3.42 us (10%)
    ppermute x7, starting transfers between devices, gather(): here.append(lax.ppermute(sent[step], ('x', 'half', 'rest'), pairs))  11.9 us
    ppermute x7, waiting for transfers between devices, gather(): here.append(lax.ppermute(sent[step], ('x', 'half', 'rest'), pairs))  5.53 us
    ppermute x1, waiting for transfers between devices, shards(): from_half = lax.ppermute(to_half, 'half', [(0, 1), (1, 0)])  5.21 us
    ppermute x1, starting transfers between devices, shards(): lax.ppermute(to_both, ('x', 'half'), [(i, i ^ 3) for i in range(4)])  3.04 us
    ppermute x8, starting transfers between devices, gather(): there.append(lax.ppermute(value, 'core', [(0, 1), (1, 0)]))  1.86 us
    ppermute x1, waiting for transfers between devices, shards(): lax.ppermute(to_both, ('x', 'half'), [(i, i ^ 3) for i in range(4)])  1.41 us
    pallas_call x1, Pallas kernels, shards(): pl.pallas_call(functools.partial(prep_kernel, apart), out_shape=(array(sh...  1.33 us
    pallas_call x2, Pallas kernels, gram(): pl.pallas_call(functools.partial(gram_kernel, cells, which), out_shape=(a...  1.05 us
  transfers between devices with their start and end apart: 18, of which 9 were waited for; matrix products, arithmetic and copies ran while one was open for 0% of the time, Pallas kernels for 1%

profile of v6, /device:TPU:0, one launch (start us, length us, event | category | flops | bytes accessed | tf_op | source)
XLA Modules:
  0.0 34.8 jit_solution(9323152132269004076)
XLA Ops:
  0.0 1.3 %prep.1 = (bf16[1,200,256]{2,1,0:T(8,128)(2,1)S(1)}, bf16[1,200,256]{2,1,0:T(8,128)(2,1)S(1)}, bf16[1,200,256]{2,1,0:T(8,128)(2,1)S(1)}, bf16[1,200,256]{2,1,0:T...) custom-call(s32[16]{0:T(128)} %assignment.1, ...), custom_call_target="tpu_custom_call" | custom-call | tf_op jit(solution)/shard_map/prep/pallas_call | solution.py:209
  1.3 5.0 %collective-permute-start = (bf16[1,200,256]{2,1,0:T(8,128)(2,1)S(1)}, bf16[1,200,256]{2,1,0:T(8,128)(2,1)S(1)}, u32[]{:S(2)}, u32[]{:S(2)}) collective-permute-start(bf16[1,200,256]{2,1,0:T(8,128)(2,1)S(1)} %get-tuple-element.18), channel_id=1, source_target_pairs={{0,19},{1,18},{2,17},{3,16},{4,23},{5,22},{6,21},{7,20},{16,3},{17... | collective-permute-start | bytes 307208 | tf_op jit(solution)/shard_map/ppermute | solution.py:182
  6.3 0.5 %collective-permute-start.1 = (bf16[1,200,256]{2,1,0:T(8,128)(2,1)S(1)}, bf16[1,200,256]{2,1,0:T(8,128)(2,1)S(1)}, u32[]{:S(2)}, u32[]{:S(2)}) collective-permute-start(bf16[1,200,256]{2,1,0:T(8,128)(2,1)S(1)} %get-tuple-element.19), channel_id=1, source_target_pairs={{0,17},{1,16},{2,19},{3,18},{4,7},{5,6},{6,5},{7,4},{16,1},{17,0},... | collective-permute-start | bytes 307208 | tf_op jit(solution)/shard_map/ppermute | solution.py:182
  6.8 1.4 %collective-permute-start.2 = (bf16[1,200,256]{2,1,0:T(8,128)(2,1)S(1)}, bf16[1,200,256]{2,1,0:T(8,128)(2,1)S(1)}, u32[]{:S(2)}, u32[]{:S(2)}) collective-permute-start(bf16[1,200,256]{2,1,0:T(8,128)(2,1)S(1)} %get-tuple-element.20), channel_id=1, source_target_pairs={{0,18},{1,19},{2,16},{3,17},{4,20},{5,21},{6,22},{7,23},{16,2},{17... | collective-permute-start | bytes 307208 | tf_op jit(solution)/shard_map/ppermute | solution.py:182
  8.2 2.5 %collective-permute-start.3 = (bf16[1,200,256]{2,1,0:T(8,128)(2,1)S(1)}, bf16[1,200,256]{2,1,0:T(8,128)(2,1)S(1)}, u32[]{:S(2)}, u32[]{:S(2)}) collective-permute-start(bf16[1,200,256]{2,1,0:T(8,128)(2,1)S(1)} %get-tuple-element.21), channel_id=1, source_target_pairs={{0,3},{1,2},{2,1},{3,0},{4,21},{5,20},{6,23},{7,22},{16,19},{17,18... | collective-permute-start | bytes 307208 | tf_op jit(solution)/shard_map/ppermute | solution.py:182
  10.7 0.5 %collective-permute-start.4 = (bf16[1,200,256]{2,1,0:T(8,128)(2,1)S(1)}, bf16[1,200,256]{2,1,0:T(8,128)(2,1)S(1)}, u32[]{:S(2)}, u32[]{:S(2)}) collective-permute-start(bf16[1,200,256]{2,1,0:T(8,128)(2,1)S(1)} %get-tuple-element.22), channel_id=1, source_target_pairs={{0,16},{1,17},{2,18},{3,19},{4,6},{5,7},{6,4},{7,5},{16,0},{17,1},... | collective-permute-start | bytes 307208 | tf_op jit(solution)/shard_map/ppermute | solution.py:182
  11.3 0.5 %collective-permute-start.5 = (bf16[1,200,256]{2,1,0:T(8,128)(2,1)S(1)}, bf16[1,200,256]{2,1,0:T(8,128)(2,1)S(1)}, u32[]{:S(2)}, u32[]{:S(2)}) collective-permute-start(bf16[1,200,256]{2,1,0:T(8,128)(2,1)S(1)} %get-tuple-element.23), channel_id=1, source_target_pairs={{0,1},{1,0},{2,3},{3,2},{4,22},{5,23},{6,20},{7,21},{16,17},{17,16... | collective-permute-start | bytes 307208 | tf_op jit(solution)/shard_map/ppermute | solution.py:182
  11.8 3.1 %collective-permute-done.1.refs_2_ = bf16[1,200,256]{2,1,0:T(8,128)(2,1)S(1)} collective-permute-done((bf16[1,200,256]{2,1,0:T(8,128)(2,1)S(1)}, bf16[1,200,256]{2,1,0:T(8,128)(2,1)S(1)}, u32[]{:S(2)}, u32[]{:S(2)}) %collective-permute-start.1) | collective-permute-done | bytes 102432 | tf_op jit(solution)/shard_map/ppermute | solution.py:182
  14.9 1.4 %collective-permute-start.6 = (bf16[1,200,256]{2,1,0:T(8,128)(2,1)S(1)}, bf16[1,200,256]{2,1,0:T(8,128)(2,1)S(1)}, u32[]{:S(2)}, u32[]{:S(2)}) collective-permute-start(bf16[1,200,256]{2,1,0:T(8,128)(2,1)S(1)} %get-tuple-element.24), channel_id=1, source_target_pairs={{0,2},{1,3},{2,0},{3,1},{4,5},{5,4},{6,7},{7,6},{16,18},{17,19},{1... | collective-permute-start | bytes 307208 | tf_op jit(solution)/shard_map/ppermute | solution.py:182
  16.3 0.0 collective-permute-done.2.refs_3_
  16.3 0.0 collective-permute-start.7
  16.3 0.0 collective-permute-done.3.refs_4_
  16.3 0.5 %collective-permute-start.8 = (bf16[1,200,256]{2,1,0:T(8,128)(2,1)S(1)}, bf16[1,200,256]{2,1,0:T(8,128)(2,1)S(1)}, u32[]{:S(2)}, u32[]{:S(2)}) collective-permute-start(bf16[1,200,256]{2,1,0:T(8,128)(2,1)S(1)} %collective-permute-done.refs_1_), channel_id=1, source_target_pairs={{0,8},{8,0},{1,9},{9,1},{2,10},{10,2},{3,11},{11,3},{4,12},{12,4},... | collective-permute-start | bytes 307208 | tf_op jit(solution)/shard_map/ppermute | solution.py:185
  16.9 0.1 collective-permute-start.9
  16.9 0.2 collective-permute-done.5.refs_6_
  17.1 0.3 collective-permute-start.10
  17.4 2.2 %collective-permute-done.6.refs_7_ = bf16[1,200,256]{2,1,0:T(8,128)(2,1)S(1)} collective-permute-done((bf16[1,200,256]{2,1,0:T(8,128)(2,1)S(1)}, bf16[1,200,256]{2,1,0:T(8,128)(2,1)S(1)}, u32[]{:S(2)}, u32[]{:S(2)}) %collective-permute-start.6) | collective-permute-done | bytes 102432 | tf_op jit(solution)/shard_map/ppermute | solution.py:182
  19.6 0.5 %collective-permute-start.12 = (bf16[1,200,256]{2,1,0:T(8,128)(2,1)S(1)}, bf16[1,200,256]{2,1,0:T(8,128)(2,1)S(1)}, u32[]{:S(2)}, u32[]{:S(2)}) collective-permute-start(bf16[1,200,256]{2,1,0:T(8,128)(2,1)S(1)} %collective-permute-done.4.refs_5_), channel_id=1, source_target_pairs={{0,8},{8,0},{1,9},{9,1},{2,10},{10,2},{3,11},{11,3},{4,12},{12,4},... | collective-permute-start | bytes 307208 | tf_op jit(solution)/shard_map/ppermute | solution.py:185
  20.1 0.1 collective-permute-start.13
  20.2 0.4 %collective-permute-start.14 = (bf16[1,200,256]{2,1,0:T(8,128)(2,1)S(1)}, bf16[1,200,256]{2,1,0:T(8,128)(2,1)S(1)}, u32[]{:S(2)}, u32[]{:S(2)}) collective-permute-start(bf16[1,200,256]{2,1,0:T(8,128)(2,1)S(1)} %collective-permute-done.6.refs_7_), channel_id=1, source_target_pairs={{0,8},{8,0},{1,9},{9,1},{2,10},{10,2},{3,11},{11,3},{4,12},{12,4},... | collective-permute-start | bytes 307208 | tf_op jit(solution)/shard_map/ppermute | solution.py:185
  20.6 0.3 collective-permute-done.11.refs_12_
  20.9 0.2 collective-permute-done.12.refs_13_
  21.0 0.4 %collective-permute-done.13.refs_14_ = bf16[1,200,256]{2,1,0:T(8,128)(2,1)S(1)} collective-permute-done((bf16[1,200,256]{2,1,0:T(8,128)(2,1)S(1)}, bf16[1,200,256]{2,1,0:T(8,128)(2,1)S(1)}, u32[]{:S(2)}, u32[]{:S(2)}) %collective-permute-start.13) | collective-permute-done | bytes 102432 | tf_op jit(solution)/shard_map/ppermute | solution.py:185
  21.4 0.2 collective-permute-done.14.refs_15_
  21.6 0.5 %gram.2 = (f32[136,256]{1,0:T(8,128)S(1)}, f32[136,256]{1,0:T(8,128)S(1)}) custom-call(s32[1]{0:T(128)} %bitcast.place, bf16[1,200,256]{2,1,0:T(8,128)(2,1)S(1)} %get-tuple-element.17.refs_0_, bf16[1,200,256]{2,1,0:T(8,128)(2,1)S(1)} %collective-permute-done.refs_1_, bf16[1,200,256]{2,1,0:T(8,128)(2,1)S(1)} %collective-permute-done.1.refs_2_, ...), custom_call_target="tpu_custom_call" | custom-call | tf_op jit(solution)/shard_map/gram/pallas_call | solution.py:225
  22.1 0.9 %collective-permute-start.15 = (f32[136,256]{1,0:T(8,128)S(1)}, f32[136,256]{1,0:T(8,128)S(1)}, u32[]{:S(2)}, u32[]{:S(2)}) collective-permute-start(f32[136,256]{1,0:T(8,128)S(1)} %get-tuple-element.26), channel_id=1, source_target_pairs={{0,16},{16,0},{1,17},{17,1},{2,18},{18,2},{3,19},{19,3},{4,20},{20... | collective-permute-start | bytes 417800 | tf_op jit(solution)/shard_map/ppermute | solution.py:241
  23.0 0.5 %gram.3 = (bf16[136,256]{1,0:T(8,128)(2,1)S(1)}, bf16[136,256]{1,0:T(8,128)(2,1)S(1)}) custom-call(s32[1]{0:T(128)} %bitcast.place, bf16[1,200,256]{2,1,0:T(8,128)(2,1)S(1)} %get-tuple-element.17.refs_0_, bf16[1,200,256]{2,1,0:T(8,128)(2,1)S(1)} %collective-permute-done.refs_1_, bf16[1,200,256]{2,1,0:T(8,128)(2,1)S(1)} %collective-permute-done.1.refs_2_, ...), custom_call_target="tpu_custom_call" | custom-call | tf_op jit(solution)/shard_map/gram/pallas_call | solution.py:225
  23.5 0.5 %collective-permute-start.16 = (bf16[136,256]{1,0:T(8,128)(2,1)S(1)}, bf16[136,256]{1,0:T(8,128)(2,1)S(1)}, u32[]{:S(2)}, u32[]{:S(2)}) collective-permute-start(bf16[136,256]{1,0:T(8,128)(2,1)S(1)} %get-tuple-element.27), channel_id=1, source_target_pairs={{0,4},{4,0},{1,5},{5,1},{2,6},{6,2},{3,7},{7,3},{8,12},{12,8},{9,1... | collective-permute-start | bytes 208904 | tf_op jit(solution)/shard_map/ppermute | solution.py:239
  24.1 3.0 %collective-permute-start.17 = (bf16[136,256]{1,0:T(8,128)(2,1)S(1)}, bf16[136,256]{1,0:T(8,128)(2,1)S(1)}, u32[]{:S(2)}, u32[]{:S(2)}) collective-permute-start(bf16[136,256]{1,0:T(8,128)(2,1)S(1)} %get-tuple-element.28), channel_id=1, source_target_pairs={{0,20},{4,16},{16,4},{20,0},{1,21},{5,17},{17,5},{21,1},{2,22},{6,... | collective-permute-start | bytes 208904 | tf_op jit(solution)/shard_map/ppermute | solution.py:238
  27.1 5.2 %collective-permute-done.16.half_ref = bf16[136,256]{1,0:T(8,128)(2,1)S(1)} collective-permute-done((bf16[136,256]{1,0:T(8,128)(2,1)S(1)}, bf16[136,256]{1,0:T(8,128)(2,1)S(1)}, u32[]{:S(2)}, u32[]{:S(2)}) %collective-permute-start.16) | collective-permute-done | bytes 69664 | tf_op jit(solution)/shard_map/ppermute | solution.py:239
  32.4 1.4 %collective-permute-done.17.both_ref = bf16[136,256]{1,0:T(8,128)(2,1)S(1)} collective-permute-done((bf16[136,256]{1,0:T(8,128)(2,1)S(1)}, bf16[136,256]{1,0:T(8,128)(2,1)S(1)}, u32[]{:S(2)}, u32[]{:S(2)}) %collective-permute-start.17) | collective-permute-done | bytes 69664 | tf_op jit(solution)/shard_map/ppermute | solution.py:238
  33.8 1.0 %finish.1 = f32[2,2,64,256]{3,2,1,0:T(8,128)} custom-call(s32[1]{0:T(128)} %bitcast.place, s32[1]{0:T(128)} %bitcast.1.nearer, f32[136,256]{1,0:T(8,128)S(1)} %get-tuple-element.25.keep_ref, f32[136,256]{1,0:T(8,128)S(1)} %collective-permute-done.15.x_ref, bf16[136,256]{1,0:T(8,128)(2,1)S(1)} %collective-permute-done.16.half_ref, ...), custom_call_target="tpu_custom_call" | custom-call | tf_op jit(solution)/shard_map/finish/pallas_call | solution.py:242
  (8 shorter events, 0.0 us)
Async XLA Ops:
  1.3 9.9 %collective-permute-start = (bf16[1,200,256]{2,1,0:T(8,128)(2,1)S(1)}, bf16[1,200,256]{2,1,0:T(8,128)(2,1)S(1)}, u32[]{:S(2)}, u32[]{:S(2)}) collective-permute-start(bf16[1,200,256]{2,1,0:T(8,128)(2,1)S(1)} %get-tuple-element.18), channel_id=1, source_target_pairs={{0,19},{1,18},{2,17},{3,16},{4,23},{5,22},{6,21},{7,20},{16,3},{17... | collective-permute-start | bytes 307208 | tf_op jit(solution)/shard_map/ppermute | solution.py:182
  6.3 8.6 %collective-permute-start.1 = (bf16[1,200,256]{2,1,0:T(8,128)(2,1)S(1)}, bf16[1,200,256]{2,1,0:T(8,128)(2,1)S(1)}, u32[]{:S(2)}, u32[]{:S(2)}) collective-permute-start(bf16[1,200,256]{2,1,0:T(8,128)(2,1)S(1)} %get-tuple-element.19), channel_id=1, source_target_pairs={{0,17},{1,16},{2,19},{3,18},{4,7},{5,6},{6,5},{7,4},{16,1},{17,0},... | collective-permute-start | bytes 307208 | tf_op jit(solution)/shard_map/ppermute | solution.py:182
  6.8 9.5 %collective-permute-start.2 = (bf16[1,200,256]{2,1,0:T(8,128)(2,1)S(1)}, bf16[1,200,256]{2,1,0:T(8,128)(2,1)S(1)}, u32[]{:S(2)}, u32[]{:S(2)}) collective-permute-start(bf16[1,200,256]{2,1,0:T(8,128)(2,1)S(1)} %get-tuple-element.20), channel_id=1, source_target_pairs={{0,18},{1,19},{2,16},{3,17},{4,20},{5,21},{6,22},{7,23},{16,2},{17... | collective-permute-start | bytes 307208 | tf_op jit(solution)/shard_map/ppermute | solution.py:182
  8.2 8.1 %collective-permute-start.3 = (bf16[1,200,256]{2,1,0:T(8,128)(2,1)S(1)}, bf16[1,200,256]{2,1,0:T(8,128)(2,1)S(1)}, u32[]{:S(2)}, u32[]{:S(2)}) collective-permute-start(bf16[1,200,256]{2,1,0:T(8,128)(2,1)S(1)} %get-tuple-element.21), channel_id=1, source_target_pairs={{0,3},{1,2},{2,1},{3,0},{4,21},{5,20},{6,23},{7,22},{16,19},{17,18... | collective-permute-start | bytes 307208 | tf_op jit(solution)/shard_map/ppermute | solution.py:182
  10.7 6.1 %collective-permute-start.4 = (bf16[1,200,256]{2,1,0:T(8,128)(2,1)S(1)}, bf16[1,200,256]{2,1,0:T(8,128)(2,1)S(1)}, u32[]{:S(2)}, u32[]{:S(2)}) collective-permute-start(bf16[1,200,256]{2,1,0:T(8,128)(2,1)S(1)} %get-tuple-element.22), channel_id=1, source_target_pairs={{0,16},{1,17},{2,18},{3,19},{4,6},{5,7},{6,4},{7,5},{16,0},{17,1},... | collective-permute-start | bytes 307208 | tf_op jit(solution)/shard_map/ppermute | solution.py:182
  11.3 5.8 %collective-permute-start.5 = (bf16[1,200,256]{2,1,0:T(8,128)(2,1)S(1)}, bf16[1,200,256]{2,1,0:T(8,128)(2,1)S(1)}, u32[]{:S(2)}, u32[]{:S(2)}) collective-permute-start(bf16[1,200,256]{2,1,0:T(8,128)(2,1)S(1)} %get-tuple-element.23), channel_id=1, source_target_pairs={{0,1},{1,0},{2,3},{3,2},{4,22},{5,23},{6,20},{7,21},{16,17},{17,16... | collective-permute-start | bytes 307208 | tf_op jit(solution)/shard_map/ppermute | solution.py:182
  14.9 4.7 %collective-permute-start.6 = (bf16[1,200,256]{2,1,0:T(8,128)(2,1)S(1)}, bf16[1,200,256]{2,1,0:T(8,128)(2,1)S(1)}, u32[]{:S(2)}, u32[]{:S(2)}) collective-permute-start(bf16[1,200,256]{2,1,0:T(8,128)(2,1)S(1)} %get-tuple-element.24), channel_id=1, source_target_pairs={{0,2},{1,3},{2,0},{3,1},{4,5},{5,4},{6,7},{7,6},{16,18},{17,19},{1... | collective-permute-start | bytes 307208 | tf_op jit(solution)/shard_map/ppermute | solution.py:182
  16.3 3.2 %collective-permute-start.7 = (bf16[1,200,256]{2,1,0:T(8,128)(2,1)S(1)}, bf16[1,200,256]{2,1,0:T(8,128)(2,1)S(1)}, u32[]{:S(2)}, u32[]{:S(2)}) collective-permute-start(bf16[1,200,256]{2,1,0:T(8,128)(2,1)S(1)} %get-tuple-element.17.refs_0_), channel_id=1, source_target_pairs={{0,8},{8,0},{1,9},{9,1},{2,10},{10,2},{3,11},{11,3},{4,12},{12,4},... | collective-permute-start | bytes 307208 | tf_op jit(solution)/shard_map/ppermute | solution.py:185
  16.3 3.7 %collective-permute-start.8 = (bf16[1,200,256]{2,1,0:T(8,128)(2,1)S(1)}, bf16[1,200,256]{2,1,0:T(8,128)(2,1)S(1)}, u32[]{:S(2)}, u32[]{:S(2)}) collective-permute-start(bf16[1,200,256]{2,1,0:T(8,128)(2,1)S(1)} %collective-permute-done.refs_1_), channel_id=1, source_target_pairs={{0,8},{8,0},{1,9},{9,1},{2,10},{10,2},{3,11},{11,3},{4,12},{12,4},... | collective-permute-start | bytes 307208 | tf_op jit(solution)/shard_map/ppermute | solution.py:185
  16.9 3.3 %collective-permute-start.9 = (bf16[1,200,256]{2,1,0:T(8,128)(2,1)S(1)}, bf16[1,200,256]{2,1,0:T(8,128)(2,1)S(1)}, u32[]{:S(2)}, u32[]{:S(2)}) collective-permute-start(bf16[1,200,256]{2,1,0:T(8,128)(2,1)S(1)} %collective-permute-done.1.refs_2_), channel_id=1, source_target_pairs={{0,8},{8,0},{1,9},{9,1},{2,10},{10,2},{3,11},{11,3},{4,12},{12,4},... | collective-permute-start | bytes 307208 | tf_op jit(solution)/shard_map/ppermute | solution.py:185
  17.1 3.5 %collective-permute-start.10 = (bf16[1,200,256]{2,1,0:T(8,128)(2,1)S(1)}, bf16[1,200,256]{2,1,0:T(8,128)(2,1)S(1)}, u32[]{:S(2)}, u32[]{:S(2)}) collective-permute-start(bf16[1,200,256]{2,1,0:T(8,128)(2,1)S(1)} %collective-permute-done.2.refs_3_), channel_id=1, source_target_pairs={{0,8},{8,0},{1,9},{9,1},{2,10},{10,2},{3,11},{11,3},{4,12},{12,4},... | collective-permute-start | bytes 307208 | tf_op jit(solution)/shard_map/ppermute | solution.py:185
  19.6 1.3 %collective-permute-start.11 = (bf16[1,200,256]{2,1,0:T(8,128)(2,1)S(1)}, bf16[1,200,256]{2,1,0:T(8,128)(2,1)S(1)}, u32[]{:S(2)}, u32[]{:S(2)}) collective-permute-start(bf16[1,200,256]{2,1,0:T(8,128)(2,1)S(1)} %collective-permute-done.3.refs_4_), channel_id=1, source_target_pairs={{0,8},{8,0},{1,9},{9,1},{2,10},{10,2},{3,11},{11,3},{4,12},{12,4},... | collective-permute-start | bytes 307208 | tf_op jit(solution)/shard_map/ppermute | solution.py:185
  19.6 1.5 %collective-permute-start.12 = (bf16[1,200,256]{2,1,0:T(8,128)(2,1)S(1)}, bf16[1,200,256]{2,1,0:T(8,128)(2,1)S(1)}, u32[]{:S(2)}, u32[]{:S(2)}) collective-permute-start(bf16[1,200,256]{2,1,0:T(8,128)(2,1)S(1)} %collective-permute-done.4.refs_5_), channel_id=1, source_target_pairs={{0,8},{8,0},{1,9},{9,1},{2,10},{10,2},{3,11},{11,3},{4,12},{12,4},... | collective-permute-start | bytes 307208 | tf_op jit(solution)/shard_map/ppermute | solution.py:185
  20.1 1.3 %collective-permute-start.13 = (bf16[1,200,256]{2,1,0:T(8,128)(2,1)S(1)}, bf16[1,200,256]{2,1,0:T(8,128)(2,1)S(1)}, u32[]{:S(2)}, u32[]{:S(2)}) collective-permute-start(bf16[1,200,256]{2,1,0:T(8,128)(2,1)S(1)} %collective-permute-done.5.refs_6_), channel_id=1, source_target_pairs={{0,8},{8,0},{1,9},{9,1},{2,10},{10,2},{3,11},{11,3},{4,12},{12,4},... | collective-permute-start | bytes 307208 | tf_op jit(solution)/shard_map/ppermute | solution.py:185
  20.2 1.4 %collective-permute-start.14 = (bf16[1,200,256]{2,1,0:T(8,128)(2,1)S(1)}, bf16[1,200,256]{2,1,0:T(8,128)(2,1)S(1)}, u32[]{:S(2)}, u32[]{:S(2)}) collective-permute-start(bf16[1,200,256]{2,1,0:T(8,128)(2,1)S(1)} %collective-permute-done.6.refs_7_), channel_id=1, source_target_pairs={{0,8},{8,0},{1,9},{9,1},{2,10},{10,2},{3,11},{11,3},{4,12},{12,4},... | collective-permute-start | bytes 307208 | tf_op jit(solution)/shard_map/ppermute | solution.py:185
  22.1 11.7 %collective-permute-start.15 = (f32[136,256]{1,0:T(8,128)S(1)}, f32[136,256]{1,0:T(8,128)S(1)}, u32[]{:S(2)}, u32[]{:S(2)}) collective-permute-start(f32[136,256]{1,0:T(8,128)S(1)} %get-tuple-element.26), channel_id=1, source_target_pairs={{0,16},{16,0},{1,17},{17,1},{2,18},{18,2},{3,19},{19,3},{4,20},{20... | collective-permute-start | bytes 417800 | tf_op jit(solution)/shard_map/ppermute | solution.py:241
  23.5 8.8 %collective-permute-start.16 = (bf16[136,256]{1,0:T(8,128)(2,1)S(1)}, bf16[136,256]{1,0:T(8,128)(2,1)S(1)}, u32[]{:S(2)}, u32[]{:S(2)}) collective-permute-start(bf16[136,256]{1,0:T(8,128)(2,1)S(1)} %get-tuple-element.27), channel_id=1, source_target_pairs={{0,4},{4,0},{1,5},{5,1},{2,6},{6,2},{3,7},{7,3},{8,12},{12,8},{9,1... | collective-permute-start | bytes 208904 | tf_op jit(solution)/shard_map/ppermute | solution.py:239
  24.1 9.7 %collective-permute-start.17 = (bf16[136,256]{1,0:T(8,128)(2,1)S(1)}, bf16[136,256]{1,0:T(8,128)(2,1)S(1)}, u32[]{:S(2)}, u32[]{:S(2)}) collective-permute-start(bf16[136,256]{1,0:T(8,128)(2,1)S(1)} %get-tuple-element.28), channel_id=1, source_target_pairs={{0,20},{4,16},{16,4},{20,0},{1,21},{5,17},{17,5},{21,1},{2,22},{6,... | collective-permute-start | bytes 208904 | tf_op jit(solution)/shard_map/ppermute | solution.py:238
